TPU v7x, 32 devices: a whole 2x2x4 slice. The times are simulated.
32 devices in a mesh: loop: 8 (over z, x), rep: 4 (over y, core).
Axes of the slice: x: 2, y: 2, z: 4, core: 2. Of those that a mesh axis runs over, the one named last changes fastest.
Arguments:
- features: float32 [4096, 128], P('loop'), may hold values from -6 to 6
- weight: float32 [128, 256], replicated, may hold values from -0.5 to 0.5
- bias: float32 [256], replicated, may hold values from -3 to 3
- tile_values: float32 [512, 128, 128], P(('loop', 'rep')), may hold values from -0.125 to 0.125
- tile_rows: int32 [512], P(('loop', 'rep')), may hold values from 0 to 31, as said below
- tile_cols: int32 [512], P(('loop', 'rep')), may hold values from 0 to 31, as said below
- tile_count: int32 [32], P(('loop', 'rep')), may hold values from 1 to 16, as said below
- cotangent: float32 [4096, 256], P('loop'), may hold values from -0.6 to 0.6
Outputs:
- output: float32 [4096, 256], P('loop')
- grad_features: float32 [4096, 128], P('loop')
- grad_weight: float32 [128, 256], replicated
- grad_bias: float32 [256], replicated
Inputs may be any that keep to these rules, and one draw needn't show every extreme that they name: `tile_rows`: every slot of a device at loop index l names a row block from l * 4 to (l + 1) * 4 - 1. `tile_cols`: for every loop index m, the live slots of one device name at most 2 different column blocks from m * 4 to (m + 1) * 4 - 1; for every loop index some device names exactly 2 of one such range. `tile_count`: for every loop index some device has all 16 slots live.
All inputs are finite; a program needn't handle non-finite values.
Results may differ from a plain program's by a relative error of at most 0.0001.
Values sent between devices are 32-bit elements; how exact they have to be, the bound alone decides.
No kernel may reach another device: no remote copies, remote signals or barrier semaphores. Data moves between devices by JAX's collectives and lax.ppermute only.
A program may use at most 64 MiB of HBM per device.

v0:
```python
import jax
import jax.numpy as jnp
from jax import lax
from jax.sharding import PartitionSpec as P


def per_device(features, weight, bias, tile_values, tile_rows, tile_cols, tile_count, cotangent):
    highest = lax.Precision.HIGHEST
    tile_side = tile_values.shape[1]
    rows_here = features.shape[0]
    nblocks = rows_here // tile_side
    slots = tile_values.shape[0]
    local_rows = tile_rows - lax.axis_index("loop") * nblocks
    live_slot = (jnp.arange(slots, dtype=jnp.int32) < tile_count[0]).astype(jnp.float32)
    row_pick = (local_rows[:, None] == jnp.arange(nblocks, dtype=jnp.int32)[None, :]).astype(
        jnp.float32
    )
    row_pick = row_pick * live_slot[:, None]
    gathered = lax.all_gather(features, "loop", axis=0, tiled=True)
    width = gathered.shape[1]
    blocks = gathered.reshape(-1, tile_side, width)[tile_cols]
    products = jnp.einsum("kij,kjf->kif", tile_values, blocks, precision=highest)
    aggregated = lax.psum(
        jnp.einsum("kb,kif->bif", row_pick, products, precision=highest), "rep"
    ).reshape(rows_here, -1)
    preactive = jnp.dot(aggregated, weight, precision=highest) + bias
    logistic = jax.nn.sigmoid(preactive)
    output = preactive * logistic
    gradient = cotangent * logistic * (1.0 + preactive * (1.0 - logistic))
    spread = jnp.dot(gradient, weight.T, precision=highest)
    source_blocks = spread.reshape(nblocks, tile_side, spread.shape[1])[
        jnp.clip(local_rows, 0, nblocks - 1)
    ]
    outgoing = jnp.einsum("kji,kjf->kif", tile_values, source_blocks, precision=highest)
    outgoing = outgoing * live_slot[:, None, None]
    span = rows_here * lax.axis_size("loop") // tile_side + 2
    column_pick = (tile_cols[:, None] == jnp.arange(span, dtype=jnp.int32)[None, :]).astype(
        jnp.float32
    )
    placed = jnp.einsum("kb,kif->bif", column_pick, outgoing, precision=highest)
    placed = placed.reshape(span * tile_side, outgoing.shape[2])
    term = lax.psum_scatter(
        lax.slice_in_dim(placed, 0, rows_here * lax.axis_size("loop"), axis=0),
        "loop",
        scatter_dimension=0,
        tiled=True,
    )
    own_rows = lax.psum(term, "rep")
    weight_term = jnp.dot(aggregated.T, gradient, precision=highest)
    bias_term = jnp.sum(gradient, axis=0)
    grad_weight, grad_bias = lax.psum((weight_term, bias_term), "loop")
    return (output, own_rows, grad_weight, grad_bias)


def solution(mesh):
    return jax.shard_map(
        per_device,
        mesh=mesh,
        in_specs=(
            P("loop", None),
            P(),
            P(),
            P(("loop", "rep"), None, None),
            P(("loop", "rep")),
            P(("loop", "rep")),
            P(("loop", "rep")),
            P("loop", None),
        ),
        out_specs=(P("loop", None), P("loop", None), P(), P()),
        check_vma=False,
    )
```

profile of v0, /device:TPU:0, one launch (start us, length us, event | category | flops | bytes accessed | tf_op | source)
XLA Modules:
  0.0 293.9 jit_solution(1856292996977088046)
XLA Ops:
  7.2 0.0 copy-start
  7.2 0.0 all-gather.2.cloned.1.call-start
  7.2 0.7 all-gather.2.cloned.1.call-update
  7.9 0.0 all-reduce.4.cloned.1.call-start
  8.6 0.7 compare_select_fusion.1
  9.3 0.7 compare_select_fusion
  10.0 52.0 %all-gather.2.cloned.1.call-done = f32[4096,128]{1,0:T(8,128)} async-done(((f32[512,128]{1,0:T(8,128)}), f32[4096,128]{1,0:T(8,128)}) %all-gather.2.cloned.1.call-update) | async-done | bytes 2097168 | tf_op jit(solution)/shard_map/all_gather | solution.py:19
  62.0 2.2 gather_fusion
  64.2 0.0 copy-done
  64.2 1.8 fusion.16
  66.0 0.0 copy-start.5
  66.0 0.0 copy-start.4
  66.0 0.0 copy-start.7
  66.1 0.5 copy.14
  66.6 0.0 copy-start.6
  66.6 0.6 fusion.2
  67.2 0.7 copy.12
  67.9 0.0 all-reduce.4.cloned.1.call-update
  68.0 0.0 reduce-scatter.2.cloned.1.call-start
  68.0 0.0 copy-done.5
  68.0 0.1 fusion.7
  68.1 30.8 %all-reduce.4.cloned.1.call-done = f32[512,128]{1,0:T(8,128)} async-done(((f32[512,128]{1,0:T(8,128)}), f32[512,128]{1,0:T(8,128)}) %all-reduce.4.cloned.1.call-update) | async-done | bytes 262160 | tf_op jit(solution)/shard_map/psum | solution.py:23
  98.9 0.0 copy-done.4
  98.9 0.0 copy-done.7
  98.9 0.0 copy-done.6
  98.9 2.5 fusion.15
  101.4 0.0 copy-start.1
  101.4 0.6 fusion.17
  102.0 0.2 copy-done.1
  102.2 0.6 gather_fusion.1
  102.8 1.8 fusion.18
  104.7 0.5 copy.15
  105.2 1.0 fusion
  106.2 2.6 copy.13
  108.8 0.0 reduce-scatter.2.cloned.1.call-update
  108.8 0.0 all-reduce.8.cloned.1.call-start
  108.9 1.0 copy-done.2
  109.8 0.1 copy-done.3
  109.9 1.3 fusion.19
  111.2 0.0 all-reduce.8.cloned.1.call-update
  111.2 0.0 all-reduce.6.cloned.1.call-start
  111.3 66.0 %reduce-scatter.2.cloned.1.call-done = f32[512,128]{1,0:T(8,128)} async-done(((f32[4096,128]{1,0:T(8,128)}), f32[512,128]{1,0:T(8,128)}) %reduce-scatter.2.cloned.1.call-update) | async-done | bytes 262160 | tf_op jit(solution)/shard_map/reduce_scatter | solution.py:42
  177.3 0.0 all-reduce.6.cloned.1.call-update
  177.3 19.7 %psum.31 = f32[256]{0:T(256)} all-reduce(f32[256]{0:T(256)S(1)} %get-tuple-element.4), channel_id=1, replica_groups=mesh['loop'=8,'rep'=4] {'loop'}, use_global_device_ids=true, to_apply=%region_5.6 | all-reduce | flops 256 | bytes 2048 | tf_op jit(solution)/shard_map/psum | solution.py:51
  197.0 53.6 %all-reduce.8.cloned.1.call-done = f32[128,256]{1,0:T(8,128)} async-done(((f32[128,256]{1,0:T(8,128)}), f32[128,256]{1,0:T(8,128)}) %all-reduce.8.cloned.1.call-update) | async-done | bytes 131088 | tf_op jit(solution)/shard_map/psum | solution.py:51
  250.6 33.6 %all-reduce.6.cloned.1.call-done = f32[512,128]{1,0:T(8,128)} async-done(((f32[512,128]{1,0:T(8,128)}), f32[512,128]{1,0:T(8,128)}) %all-reduce.6.cloned.1.call-update) | async-done | bytes 262160 | tf_op jit(solution)/shard_map/psum | solution.py:48
  284.2 1.7 copy.20
  285.8 1.6 copy.21
  (5 shorter events, 0.0 us)
Async XLA Ops:
  7.2 57.0 %copy-start = (f32[16,128,128]{2,1,0:T(8,128)S(1)}, f32[16,128,128]{2,1,0:T(8,128)}, u32[]{:S(2)}) copy-start(f32[16,128,128]{2,1,0:T(8,128)} %param.11) | copy-start | bytes 3145732
  7.2 54.8 %all-gather.2.cloned.1.call-start = ((), (), s32[]{:S(2)}) async-start(), calls=%async_computation.1 | async-start | bytes 2359296 | tf_op jit(solution)/shard_map/all_gather | solution.py:19
  7.9 91.0 %all-reduce.4.cloned.1.call-start = ((), (), s32[]{:S(2)}) async-start(), calls=%async_computation.2 | async-start | bytes 524288 | tf_op jit(solution)/shard_map/psum | solution.py:23
  66.0 2.0 copy-start.5
  66.0 32.9 %copy-start.4 = (f32[128,256]{1,0:T(8,128)S(1)}, f32[128,256]{1,0:T(8,128)}, u32[]{:S(2)}) copy-start(f32[128,256]{1,0:T(8,128)} %param.9) | copy-start | bytes 393220
  66.0 32.9 %copy-start.7 = (f32[256]{0:T(256)S(1)}, f32[256]{0:T(256)}, u32[]{:S(2)}) copy-start(f32[256]{0:T(256)} %param.10) | copy-start | bytes 3076
  66.6 32.4 %copy-start.6 = (f32[512,256]{1,0:T(8,128)S(1)}, f32[512,256]{1,0:T(8,128)}, u32[]{:S(2)}) copy-start(f32[512,256]{1,0:T(8,128)} %param.15) | copy-start | bytes 1572868
  68.0 109.3 %reduce-scatter.2.cloned.1.call-start = ((), (), s32[]{:S(2)}) async-start(), calls=%async_computation.3 | async-start | bytes 2359296 | tf_op jit(solution)/shard_map/reduce_scatter | solution.py:42
  101.4 0.8 copy-start.1
  108.8 1.0 copy-start.2
  108.8 1.1 copy-start.3
  108.8 141.7 %all-reduce.8.cloned.1.call-start = ((), (), s32[]{:S(2)}) async-start(), calls=%async_computation.5 | async-start | bytes 262144 | tf_op jit(solution)/shard_map/psum | solution.py:51
  111.2 173.0 %all-reduce.6.cloned.1.call-start = ((), (), s32[]{:S(2)}) async-start(), calls=%async_computation.4 | async-start | bytes 524288 | tf_op jit(solution)/shard_map/psum | solution.py:48
Sparse Core Ops, SparseCore 0:
  10.1 51.7 all-gather.1
  68.1 30.8 all-reduce.3
  108.9 68.2 reduce-scatter.1
  181.0 69.4 all-reduce.7
  252.7 31.3 all-reduce.5
where the time goes:
time: 294 us
  waiting for transfers between devices  237 us (81%)
  blocking collectives  19.7 us (7%)
  between operations  14.6 us (5%)
  local copies, waits for them, and re-layouts  11.6 us (4%)
  matrix products  9.66 us (3%)
    reduce_scatter x1, waiting for transfers between devices, per_device(): lax.psum_scatter(lax.slice_in_dim(placed, 0, rows_here * lax.axis_size('l...  66 us
    psum x1, waiting for transfers between devices, per_device(): grad_weight, grad_bias = lax.psum((weight_term, bias_term), 'loop')  53.6 us
    all_gather x1, waiting for transfers between devices, per_device(): gathered = lax.all_gather(features, 'loop', axis=0, tiled=True)  52 us
    psum x1, waiting for transfers between devices, per_device(): own_rows = lax.psum(term, 'rep')  33.6 us
    psum x1, waiting for transfers between devices, per_device(): lax.psum(jnp.einsum('kb,kif->bif', row_pick, products, precision=highest)...  30.8 us
    psum x1, blocking collectives, per_device(): grad_weight, grad_bias = lax.psum((weight_term, bias_term), 'loop')  19.7 us
  transfers between devices with their start and end apart: 5, of which 5 were waited for; matrix products, arithmetic and copies ran while one was open for 1% of the time, Pallas kernels for 0%

commit v1 on v0

v1 whole, which is shorter than its diff:
```python
import functools

import jax
import jax.numpy as jnp
from jax import lax
from jax.experimental import pallas as pl
from jax.experimental.pallas import tpu as pltpu
from jax.sharding import PartitionSpec as P

LANES = 128
PAD = 8
F32 = jnp.float32
BF16 = jnp.bfloat16
VMEM = pl.BlockSpec(memory_space=pltpu.VMEM)
SMEM = pl.BlockSpec(memory_space=pltpu.SMEM)


def halves(x):
    high = x.astype(BF16).astype(F32)
    return high, x - high


def dot3(a, b, dims=(((1,), (0,)), ((), ()))):
    ah, al = halves(a)
    bh, bl = halves(b)
    ah, al, bh, bl = (v.astype(BF16) for v in (ah, al, bh, bl))
    dot = functools.partial(lax.dot_general, dimension_numbers=dims, preferred_element_type=F32)
    return dot(ah, bh) + dot(ah, bl) + dot(al, bh)


def call(kernel, out_shapes, in_specs, scratch, flops, moved, name, limit=24):
    return pl.pallas_call(
        kernel,
        out_shape=[jax.ShapeDtypeStruct(s, F32) for s in out_shapes],
        in_specs=in_specs,
        out_specs=[VMEM] * len(out_shapes),
        scratch_shapes=scratch,
        compiler_params=pltpu.CompilerParams(vmem_limit_bytes=limit << 20),
        cost_estimate=pl.CostEstimate(flops=flops, bytes_accessed=moved, transcendentals=0),
        name=name,
    )


def pack_kernel(reps, part, here, count, tiles, meta, *refs):
    outs, turned = refs[:reps], refs[reps]
    slots, side = tiles.shape[0], tiles.shape[1]
    for s in range(slots):
        turned[s] = jnp.where(s < count[0], tiles[s].T, jnp.zeros((side, side), F32))
    for d in range(reps):
        start = pl.multiple_of((here[0] ^ d) * part, 8)
        for s in range(slots):
            outs[d][pl.ds(s * part, part), :] = turned[s, pl.ds(start, part), :]
        outs[d][pl.ds(slots * part, PAD), :] = meta[...]


def forward_kernel(reps, loops, blocks, part, slots, here, rows, cols, *refs):
    tiles, feats = refs[:reps], refs[reps : reps + loops]
    send, keep, rhs, acc = refs[reps + loops :]
    side = acc.shape[0] // blocks
    for k in range(loops):
        for b in range(blocks):
            high, low = halves(feats[k][pl.ds(b * part, part), :])
            rhs[k * blocks + b] = jnp.concatenate([high, low, high], axis=0).astype(BF16)
    acc[...] = jnp.zeros_like(acc)
    for d in range(reps):

        def slot(s, carry, d=d):
            high, low = halves(tiles[d][pl.ds(pl.multiple_of(s * part, 8), part), :])
            lhs = jnp.concatenate([high, high, low], axis=0).astype(BF16)
            product = lax.dot_general(
                lhs, rhs[cols[d, s]], (((0,), (0,)), ((), ())), preferred_element_type=F32
            )
            at = pl.ds(pl.multiple_of(rows[d, s] * side, 8), side)
            acc[at, :] = acc[at, :] + product
            return carry

        lax.fori_loop(0, slots, slot, 0, unroll=4)
    half = acc.shape[0] // 2
    core = here[0] & 1
    keep[...] = acc[pl.ds(pl.multiple_of(core * half, 8), half), :]
    send[...] = acc[pl.ds(pl.multiple_of((1 - core) * half, 8), half), :]


def backward_kernel(reps, loops, blocks, part, slots, here, rows, cols, *refs):
    tiles = refs[:reps]
    mine, other, weight, bias, cotangent, output, send, keep = refs[reps : reps + 8]
    agg, turned, grads, right, products, acc = refs[reps + 8 :]
    total, width = agg.shape
    half, side = total // 2, total // blocks
    wide = output.shape[1]
    core = here[0] & 1
    agg[pl.ds(pl.multiple_of(core * half, 8), half), :] = mine[...]
    agg[pl.ds(pl.multiple_of((1 - core) * half, 8), half), :] = other[...]
    w = weight[...]
    for b in range(blocks):
        at = pl.ds(b * side, side)
        a = agg[at, :]
        turned[:, at] = a.T
        pre = dot3(a, w) + bias[...]
        gate = jax.nn.sigmoid(pre)
        output[at, :] = pre * gate
        gradient = cotangent[at, :] * gate * (1.0 + pre * (1.0 - gate))
        grads[at, :] = gradient
        spread = dot3(gradient, w, (((1,), (1,)), ((), ())))
        high, low = halves(spread)
        right[:, pl.ds(b * side, side)] = jnp.concatenate([high, low, high], axis=0).astype(BF16)
    g = grads[...]
    piece = width // reps
    grad_weight = dot3(turned[pl.ds(pl.multiple_of(here[0] * piece, 8), piece), :], g)
    grad_bias = jnp.sum(g, axis=0, keepdims=True)
    groups = wide // LANES
    acc[...] = jnp.zeros_like(acc)
    for d in range(reps):
        high, low = halves(tiles[d][pl.ds(0, slots * part), :])
        left = jnp.concatenate([high, high, low], axis=1).astype(BF16)
        products[...] = jnp.dot(left, right[...], preferred_element_type=F32)

        def slot(s, carry, d=d):
            lane = pl.multiple_of(rows[d, s] * LANES, LANES)
            value = products[pl.ds(pl.multiple_of(s * part, 8), part), pl.ds(lane, LANES)]
            at = pl.ds(pl.multiple_of(cols[d, s] * part, 8), part)
            acc[at, :] = acc[at, :] + value
            return carry

        lax.fori_loop(0, slots, slot, 0, unroll=4)
    size = blocks * part
    for k in range(loops):
        target = send if k & 1 else keep
        target[pl.ds((k // 2) * size, size), :] = acc[pl.ds(k * size, size), :]
    base = (loops // 2) * size
    for target in (send, keep):
        for q in range(groups):
            target[pl.ds(base + q * piece, piece), :] = grad_weight[:, q * LANES : (q + 1) * LANES]
        tail = [grad_bias[:, q * LANES : (q + 1) * LANES] for q in range(groups)]
        tail.append(jnp.zeros((PAD - groups, LANES), F32))
        target[pl.ds(base + groups * piece, PAD), :] = jnp.concatenate(tail, axis=0)


def add_kernel(count, size, extra, mine, theirs, *outs):
    for k in range(count):
        at = pl.ds(k * size, size)
        value = mine[at, :] + theirs[at, :]
        if count == 1:
            outs[0][at, :] = value
        else:
            outs[1 - (k & 1)][pl.ds((k // 2) * size, size), :] = value
    value = mine[pl.ds(count * size, extra), :] + theirs[pl.ds(count * size, extra), :]
    for out in outs:
        out[pl.ds(max(count // 2, 1) * size, extra), :] = value


def final_kernel(reps, blocks, part, piece, here, *refs):
    parts = refs[:reps]
    grad_features, grad_weight, grad_bias = refs[reps:]
    side = grad_features.shape[0] // blocks
    groups = grad_weight.shape[1] // LANES
    base = blocks * part
    for d in range(reps):
        q = here[0] ^ d
        for b in range(blocks):
            at = pl.ds(pl.multiple_of(b * side + q * part, 8), part)
            grad_features[at, :] = parts[d][pl.ds(b * part, part), :]
        at = pl.ds(pl.multiple_of(q * piece, 8), piece)
        for g in range(groups):
            grad_weight[at, pl.ds(g * LANES, LANES)] = parts[d][pl.ds(base + g * piece, piece), :]
    for g in range(groups):
        row = parts[0][pl.ds(base + groups * piece + g, 1), :]
        grad_bias[:, pl.ds(g * LANES, LANES)] = row


def per_device(features, weight, bias, tile_values, tile_rows, tile_cols, tile_count, cotangent):
    loops, reps = lax.axis_size("loop"), lax.axis_size("rep")
    loop_at, rep_at = lax.axis_index("loop"), lax.axis_index("rep")
    slots, side = tile_values.shape[0], tile_values.shape[1]
    total, width = features.shape
    wide = weight.shape[1]
    blocks = total // side
    part, piece, groups = side // reps, width // reps, wide // LANES
    size = blocks * part
    extra = groups * piece + PAD
    here = rep_at.astype(jnp.int32).reshape(1)

    def swap(x, axis, bit):
        n = lax.axis_size(axis)
        return lax.ppermute(x, axis, [(i, i ^ bit) for i in range(n)])

    own = lax.dynamic_index_in_dim(
        features.reshape(blocks, reps, part, width), rep_at, 1, keepdims=False
    ).reshape(size, width)
    feats = {0: own}
    bit = loops // 2
    while bit:
        for k in list(feats):
            feats[k | bit] = swap(feats[k], "loop", bit)
        bit //= 2

    local_rows = jnp.clip(tile_rows - loop_at * blocks, 0, blocks - 1)
    place = ((tile_cols // blocks) ^ loop_at) * blocks + tile_cols % blocks
    meta = jnp.pad(
        jnp.stack([local_rows, place]).astype(F32), ((0, PAD - 2), (0, LANES - slots))
    )
    chunks = call(
        functools.partial(pack_kernel, reps, part),
        [(slots * part + PAD, side)] * reps,
        [SMEM, SMEM, VMEM, VMEM],
        [pltpu.VMEM((slots, side, side), F32)],
        0,
        2 * tile_values.size * 4,
        "pack",
    )(here, tile_count, tile_values, meta)
    tiles = [chunks[0]] + [swap(chunks[d], "rep", d) for d in range(1, reps)]
    index = jnp.stack([t[slots * part : slots * part + 2, :slots] for t in tiles]).astype(jnp.int32)
    rows, cols = index[:, 0], index[:, 1]

    count = reps * slots
    send, keep = call(
        functools.partial(forward_kernel, reps, loops, blocks, part, slots),
        [(total // 2, width)] * 2,
        [SMEM] * 3 + [VMEM] * (reps + loops),
        [
            pltpu.VMEM((loops * blocks, 3 * part, width), BF16),
            pltpu.VMEM((total, width), F32),
        ],
        2 * count * part * side * width * 3,
        4 << 20,
        "forward",
    )(here, rows, cols, *tiles, *[feats[k] for k in range(loops)])
    mine = keep + swap(send, "rep", 1)
    bit = 2
    while bit < reps:
        mine = mine + swap(mine, "rep", bit)
        bit *= 2
    other = swap(mine, "rep", 1)

    shape = ((loops // 2) * size + extra, width)
    output, send, keep = call(
        functools.partial(backward_kernel, reps, loops, blocks, part, slots),
        [(total, wide), shape, shape],
        [SMEM] * 3 + [VMEM] * (reps + 5),
        [
            pltpu.VMEM((total, width), F32),
            pltpu.VMEM((width, total), F32),
            pltpu.VMEM((total, wide), F32),
            pltpu.VMEM((3 * width, total), BF16),
            pltpu.VMEM((slots * part, blocks * width), F32),
            pltpu.VMEM((loops * size, width), F32),
        ],
        2 * count * part * side * width * blocks * 3,
        4 << 20,
        "backward",
        limit=32,
    )(here, rows, cols, *tiles, mine, other, weight, bias.reshape(1, wide), cotangent)

    bit, left = 1, loops // 2
    while left:
        shape = (max(left // 2, 1) * size + extra, width)
        summed = call(
            functools.partial(add_kernel, left, size, extra),
            [shape] * (1 if left == 1 else 2),
            [VMEM] * 2,
            [],
            left * size * width,
            3 * left * size * width * 4,
            "add",
        )(keep, swap(send, "loop", bit))
        if left > 1:
            send, keep = summed
        else:
            keep = summed[0]
        bit, left = bit * 2, left // 2

    parts = {0: keep}
    bit = reps // 2
    while bit:
        for k in list(parts):
            parts[k | bit] = swap(parts[k], "rep", bit)
        bit //= 2
    grad_features, grad_weight, grad_bias = call(
        functools.partial(final_kernel, reps, blocks, part, piece),
        [(total, width), (width, wide), (1, wide)],
        [SMEM] + [VMEM] * reps,
        [],
        0,
        2 * total * width * 4,
        "final",
    )(here, *[parts[d] for d in range(reps)])
    return (output, grad_features, grad_weight, grad_bias.reshape(wide))


def solution(mesh):
    return jax.shard_map(
        per_device,
        mesh=mesh,
        in_specs=(
            P("loop", None),
            P(),
            P(),
            P(("loop", "rep"), None, None),
            P(("loop", "rep")),
            P(("loop", "rep")),
            P(("loop", "rep")),
            P("loop", None),
        ),
        out_specs=(P("loop", None), P("loop", None), P(), P()),
        check_vma=False,
    )
```

time: 294 us -> 70.1 us (0.24)
  waiting for transfers between devices: 237 us -> 38.1 us
  blocking collectives: 19.7 us -> 0 us
  starting transfers between devices: 0.2 us -> 18.5 us
  between operations: 14.6 us -> 1.5 us
  Pallas kernels: 0 us -> 9.81 us
  local copies, waits for them, and re-layouts: 11.6 us -> 1.93 us
  matrix products: 9.66 us -> 0 us
    psum x3 -> x0, waiting for transfers between devices: 118 us -> none  [the longest x1 53.6 us: per_device(): grad_weight, grad_bias = lax.psum((weight_term, bias_term), 'loop')]
    reduce_scatter x1 -> x0, waiting for transfers between devices: 66 us -> none  [per_device(): lax.psum_scatter(lax.slice_in_dim(placed, 0, rows_here * lax.axis_size('l...]
    all_gather x1 -> x0, waiting for transfers between devices: 52 us -> none  [per_device(): gathered = lax.all_gather(features, 'loop', axis=0, tiled=True)]
    ppermute x0 -> x19, waiting for transfers between devices: none -> 38.1 us  [swap(): return lax.ppermute(x, axis, [(i, i ^ bit) for i in range(n)])]
    psum x1 -> x0, blocking collectives: 19.7 us -> none  [per_device(): grad_weight, grad_bias = lax.psum((weight_term, bias_term), 'loop')]
    ppermute x0 -> x19, starting transfers between devices: none -> 18.5 us  [swap(): return lax.ppermute(x, axis, [(i, i ^ bit) for i in range(n)])]
    pallas_call x0 -> x7, Pallas kernels: none -> 9.81 us  [the longest x1 4.28 us: per_device(): call(functools.partial(backward_kernel, reps, loops, blocks, part, slots)...]
    dot_general x7 -> x0, matrix products: 9.66 us -> none  [the longest x1 2.46 us: per_device(): preactive = jnp.dot(aggregated, weight, precision=highest) + bias]
  transfers between devices with their start and end apart: 5 -> 19, of which waited for: 5 -> 12; matrix products, arithmetic and copies ran while one was open for 1% -> 0% of each run, Pallas kernels for 0% -> 0%
where the time goes in v1:
time: 70.1 us; the launch traced here: 69.9 us
  waiting for transfers between devices  38.1 us (54%)
  starting transfers between devices  18.5 us (26%)
  Pallas kernels  9.81 us (14%)
  local copies, waits for them, and re-layouts  1.93 us (3%)
  between operations  1.5 us (2%)
    ppermute x19, waiting for transfers between devices, swap(): return lax.ppermute(x, axis, [(i, i ^ bit) for i in range(n)])  38.1 us
    ppermute x19, starting transfers between devices, swap(): return lax.ppermute(x, axis, [(i, i ^ bit) for i in range(n)])  18.5 us
    pallas_call x1, Pallas kernels, per_device(): call(functools.partial(backward_kernel, reps, loops, blocks, part, slots)...  4.28 us
    pallas_call x1, Pallas kernels, per_device(): call(functools.partial(forward_kernel, reps, loops, blocks, part, slots),...  4.28 us
    unnamed x14, local copies, waits for them, and re-layouts  1.9 us
  transfers between devices with their start and end apart: 19, of which 12 were waited for; matrix products, arithmetic and copies ran while one was open for 0% of the time, Pallas kernels for 0%

profile of v1, /device:TPU:0, one launch (start us, length us, event | category | flops | bytes accessed | tf_op | source)
XLA Modules:
  0.0 69.9 jit_solution(16801093006409544964)
XLA Ops:
  0.6 0.0 copy-start
  1.4 0.6 copy-done.5
  2.0 0.0 copy-done.6
  2.1 0.0 copy-start.1
  2.1 1.2 %copy-done.1 = f32[16,128,128]{2,1,0:T(8,128)S(1)} copy-done((f32[16,128,128]{2,1,0:T(8,128)S(1)}, f32[16,128,128]{2,1,0:T(8,128)}, u32[]{:S(2)}) %copy-start.1) | copy-done | bytes 1048600
  3.3 0.4 pack.1
  3.7 0.6 collective-permute-start
  4.3 3.7 %collective-permute-start.6 = (f32[128,128]{1,0:T(8,128)S(1)}, f32[128,128]{1,0:T(8,128)S(1)}, u32[]{:S(2)}, u32[]{:S(2)}) collective-permute-start(f32[128,128]{1,0:T(8,128)S(1)} %bitcast.22), channel_id=1, source_target_pairs={{0,16},{4,20},{8,24},{12,28},{16,0},{20,4},{24,8},{28,12},{1,17},{... | collective-permute-start | bytes 196616 | tf_op jit(solution)/shard_map/ppermute | solution.py:185
  7.9 1.6 %collective-permute-start.4 = (f32[128,128]{1,0:T(8,128)S(1)}, f32[128,128]{1,0:T(8,128)S(1)}, u32[]{:S(2)}, u32[]{:S(2)}) collective-permute-start(f32[128,128]{1,0:T(8,128)S(1)} %bitcast.23), channel_id=1, source_target_pairs={{0,8},{4,12},{8,0},{12,4},{16,24},{20,28},{24,16},{28,20},{1,9},{5... | collective-permute-start | bytes 196616 | tf_op jit(solution)/shard_map/ppermute | solution.py:185
  9.5 1.5 %collective-permute-start.3 = (f32[128,128]{1,0:T(8,128)S(1)}, f32[128,128]{1,0:T(8,128)S(1)}, u32[]{:S(2)}, u32[]{:S(2)}) collective-permute-start(f32[128,128]{1,0:T(8,128)S(1)} %bitcast.24), channel_id=1, source_target_pairs={{0,4},{4,0},{8,12},{12,8},{16,20},{20,16},{24,28},{28,24},{1,5},{5... | collective-permute-start | bytes 196616 | tf_op jit(solution)/shard_map/ppermute | solution.py:185
  11.0 1.5 %collective-permute-start.1 = (f32[520,128]{1,0:T(8,128)S(1)}, f32[520,128]{1,0:T(8,128)S(1)}, u32[]{:S(2)}, u32[]{:S(2)}) collective-permute-start(f32[520,128]{1,0:T(8,128)S(1)} %get-tuple-element.22), channel_id=1, source_target_pairs={{0,2},{1,3},{2,0},{3,1},{4,6},{5,7},{6,4},{7,5},{8,10},{9,11},{10,... | collective-permute-start | bytes 798728 | tf_op jit(solution)/shard_map/ppermute | solution.py:185
  12.5 0.0 collective-permute-done.6.refs_8_
  12.5 0.0 collective-permute-start.2
  12.5 0.0 collective-permute-done.refs_1_
  12.5 1.5 %collective-permute-start.8 = (f32[128,128]{1,0:T(8,128)S(1)}, f32[128,128]{1,0:T(8,128)S(1)}, u32[]{:S(2)}, u32[]{:S(2)}) collective-permute-start(f32[128,128]{1,0:T(8,128)S(1)} %collective-permute-done.6.refs_8_), channel_id=1, source_target_pairs={{0,8},{4,12},{8,0},{12,4},{16,24},{20,28},{24,16},{28,20},{1,9},{5... | collective-permute-start | bytes 196616 | tf_op jit(solution)/shard_map/ppermute | solution.py:185
  14.0 0.0 collective-permute-done.4.refs_6_
  14.0 1.5 %collective-permute-start.7 = (f32[128,128]{1,0:T(8,128)S(1)}, f32[128,128]{1,0:T(8,128)S(1)}, u32[]{:S(2)}, u32[]{:S(2)}) collective-permute-start(f32[128,128]{1,0:T(8,128)S(1)} %collective-permute-done.6.refs_8_), channel_id=1, source_target_pairs={{0,4},{4,0},{8,12},{12,8},{16,20},{20,16},{24,28},{28,24},{1,5},{5... | collective-permute-start | bytes 196616 | tf_op jit(solution)/shard_map/ppermute | solution.py:185
  15.5 2.0 %collective-permute-done.8.refs_10_ = f32[128,128]{1,0:T(8,128)S(1)} collective-permute-done((f32[128,128]{1,0:T(8,128)S(1)}, f32[128,128]{1,0:T(8,128)S(1)}, u32[]{:S(2)}, u32[]{:S(2)}) %collective-permute-start.8) | collective-permute-done | bytes 65568 | tf_op jit(solution)/shard_map/ppermute | solution.py:185
  17.5 0.3 collective-permute-start.5
  17.8 2.4 %collective-permute-done.1.refs_2_ = f32[520,128]{1,0:T(8,128)S(1)} collective-permute-done((f32[520,128]{1,0:T(8,128)S(1)}, f32[520,128]{1,0:T(8,128)S(1)}, u32[]{:S(2)}, u32[]{:S(2)}) %collective-permute-start.1) | collective-permute-done | bytes 266272 | tf_op jit(solution)/shard_map/ppermute | solution.py:185
  20.3 0.5 collective-permute-start.9
  20.8 2.9 %collective-permute-done.2.refs_3_ = f32[520,128]{1,0:T(8,128)S(1)} collective-permute-done((f32[520,128]{1,0:T(8,128)S(1)}, f32[520,128]{1,0:T(8,128)S(1)}, u32[]{:S(2)}, u32[]{:S(2)}) %collective-permute-start.2) | collective-permute-done | bytes 266272 | tf_op jit(solution)/shard_map/ppermute | solution.py:185
  23.7 0.0 collective-permute-done.7.refs_9_
  23.7 0.0 collective-permute-done.5.refs_7_
  23.7 0.8 %collective-permute-done.9.refs_11_ = f32[128,128]{1,0:T(8,128)S(1)} collective-permute-done((f32[128,128]{1,0:T(8,128)S(1)}, f32[128,128]{1,0:T(8,128)S(1)}, u32[]{:S(2)}, u32[]{:S(2)}) %collective-permute-start.9) | collective-permute-done | bytes 65568 | tf_op jit(solution)/shard_map/ppermute | solution.py:185
  24.5 4.3 %forward.1 = (f32[256,128]{1,0:T(8,128)S(1)}, f32[256,128]{1,0:T(8,128)S(1)}) custom-call(s32[1]{0:T(128)} %bitcast.here, s32[4,16]{1,0:T(4,128)S(1)} %bitcast.28, s32[4,16]{1,0:T(4,128)S(1)} %bitcast.26, f32[520,128]{1,0:T(8,128)S(1)} %get-tuple-element.20.refs_0_, f32[520,128]{1,0:T(8,128)S(1)} %collective-permute-done.refs_1_, ...), custom_call_target="tpu_custom_call" | custom-call | flops 201326592 | bytes 4194304 | tf_op jit(solution)/shard_map/forward/pallas_call | solution.py:216
  28.8 0.0 copy-start.2
  28.8 0.3 collective-permute-start.10
  29.1 1.2 %collective-permute-done.10 = f32[256,128]{1,0:T(8,128)S(1)} collective-permute-done((f32[256,128]{1,0:T(8,128)S(1)}, f32[256,128]{1,0:T(8,128)S(1)}, u32[]{:S(2)}, u32[]{:S(2)}) %collective-permute-start.10) | collective-permute-done | bytes 131104 | tf_op jit(solution)/shard_map/ppermute | solution.py:185
  30.3 0.0 copy-start.3
  30.3 1.6 %collective-permute-start.11 = (f32[256,128]{1,0:T(8,128)S(1)}, f32[256,128]{1,0:T(8,128)S(1)}, u32[]{:S(2)}, u32[]{:S(2)}) collective-permute-start(f32[256,128]{1,0:T(8,128)S(1)} %add.28), channel_id=1, source_target_pairs={{0,2},{1,3},{2,0},{3,1},{4,6},{5,7},{6,4},{7,5},{8,10},{9,11},{10,... | collective-permute-start | bytes 393224 | tf_op jit(solution)/shard_map/ppermute | solution.py:185
  31.9 4.1 %collective-permute-done.11 = f32[256,128]{1,0:T(8,128)S(1)} collective-permute-done((f32[256,128]{1,0:T(8,128)S(1)}, f32[256,128]{1,0:T(8,128)S(1)}, u32[]{:S(2)}, u32[]{:S(2)}) %collective-permute-start.11) | collective-permute-done | bytes 131104 | tf_op jit(solution)/shard_map/ppermute | solution.py:185
  36.0 0.0 copy-start.4
  36.0 0.1 collective-permute-start.12
  36.1 1.3 %collective-permute-done.12.refs_5_ = f32[256,128]{1,0:T(8,128)S(1)} collective-permute-done((f32[256,128]{1,0:T(8,128)S(1)}, f32[256,128]{1,0:T(8,128)S(1)}, u32[]{:S(2)}, u32[]{:S(2)}) %collective-permute-start.12) | collective-permute-done | bytes 131104 | tf_op jit(solution)/shard_map/ppermute | solution.py:185
  37.4 4.3 %backward.1 = (f32[512,256]{1,0:T(8,128)}, f32[584,128]{1,0:T(8,128)S(1)}, f32[584,128]{1,0:T(8,128)S(1)}) custom-call(s32[1]{0:T(128)} %bitcast.here, s32[4,16]{1,0:T(4,128)S(1)} %bitcast.29, s32[4,16]{1,0:T(4,128)S(1)} %bitcast.27, f32[520,128]{1,0:T(8,128)S(1)} %get-tuple-element.20.refs_0_, f32[520,128]{1,0:T(8,128)S(1)} %collective-permute-done.refs_1_, ...), custom_call_target="tpu_custom_call" | custom-call | flops 805306368 | bytes 4194304 | tf_op jit(solution)/shard_map/backward/pallas_call | solution.py:236
  41.7 0.5 collective-permute-start.13
  42.2 8.6 %collective-permute-done.13.theirs = f32[584,128]{1,0:T(8,128)S(1)} collective-permute-done((f32[584,128]{1,0:T(8,128)S(1)}, f32[584,128]{1,0:T(8,128)S(1)}, u32[]{:S(2)}, u32[]{:S(2)}) %collective-permute-start.13) | collective-permute-done | bytes 299040 | tf_op jit(solution)/shard_map/ppermute | solution.py:185
  50.9 0.5 collective-permute-start.14
  51.4 5.0 %collective-permute-done.14.theirs = f32[328,128]{1,0:T(8,128)S(1)} collective-permute-done((f32[328,128]{1,0:T(8,128)S(1)}, f32[328,128]{1,0:T(8,128)S(1)}, u32[]{:S(2)}, u32[]{:S(2)}) %collective-permute-start.14) | collective-permute-done | bytes 167968 | tf_op jit(solution)/shard_map/ppermute | solution.py:185
  56.4 1.3 %collective-permute-start.15 = (f32[200,128]{1,0:T(8,128)S(1)}, f32[200,128]{1,0:T(8,128)S(1)}, u32[]{:S(2)}, u32[]{:S(2)}) collective-permute-start(f32[200,128]{1,0:T(8,128)S(1)} %get-tuple-element.32), channel_id=1, source_target_pairs={{0,16},{4,20},{8,24},{12,28},{16,0},{20,4},{24,8},{28,12},{1,17},{... | collective-permute-start | bytes 307208 | tf_op jit(solution)/shard_map/ppermute | solution.py:185
  57.8 5.3 %collective-permute-done.15.theirs = f32[200,128]{1,0:T(8,128)S(1)} collective-permute-done((f32[200,128]{1,0:T(8,128)S(1)}, f32[200,128]{1,0:T(8,128)S(1)}, u32[]{:S(2)}, u32[]{:S(2)}) %collective-permute-start.15) | collective-permute-done | bytes 102432 | tf_op jit(solution)/shard_map/ppermute | solution.py:185
  63.1 1.6 %collective-permute-start.17 = (f32[200,128]{1,0:T(8,128)S(1)}, f32[200,128]{1,0:T(8,128)S(1)}, u32[]{:S(2)}, u32[]{:S(2)}) collective-permute-start(f32[200,128]{1,0:T(8,128)S(1)} %add.42.refs_0_), channel_id=1, source_target_pairs={{0,2},{1,3},{2,0},{3,1},{4,6},{5,7},{6,4},{7,5},{8,10},{9,11},{10,... | collective-permute-start | bytes 307208 | tf_op jit(solution)/shard_map/ppermute | solution.py:185
  64.7 0.0 collective-permute-start.16
  64.7 3.1 %collective-permute-done.17.refs_2_ = f32[200,128]{1,0:T(8,128)S(1)} collective-permute-done((f32[200,128]{1,0:T(8,128)S(1)}, f32[200,128]{1,0:T(8,128)S(1)}, u32[]{:S(2)}, u32[]{:S(2)}) %collective-permute-start.17) | collective-permute-done | bytes 102432 | tf_op jit(solution)/shard_map/ppermute | solution.py:185
  67.8 0.0 collective-permute-done.16.refs_1_
  67.8 1.3 %collective-permute-done.18.refs_3_ = f32[200,128]{1,0:T(8,128)S(1)} collective-permute-done((f32[200,128]{1,0:T(8,128)S(1)}, f32[200,128]{1,0:T(8,128)S(1)}, u32[]{:S(2)}, u32[]{:S(2)}) %collective-permute-start.18) | collective-permute-done | bytes 102432 | tf_op jit(solution)/shard_map/ppermute | solution.py:185
  69.1 0.8 %final.1 = (f32[512,128]{1,0:T(8,128)}, f32[128,256]{1,0:T(8,128)}, f32[1,256]{1,0:T(1,128)}) custom-call(s32[1]{0:T(128)} %bitcast.here, f32[200,128]{1,0:T(8,128)S(1)} %add.42.refs_0_, f32[200,128]{1,0:T(8,128)S(1)} %collective-permute-done.16.refs_1_, f32[200,128]{1,0:T(8,128)S(1)} %collective-permute-done.17.refs_2_, ...), custom_call_target="tpu_custom_call" | custom-call | bytes 524288 | tf_op jit(solution)/shard_map/final/pallas_call | solution.py:278
  (23 shorter events, 0.2 us)
Async XLA Ops:
  0.6 3.6 %copy-start = (f32[512,128]{1,0:T(8,128)S(1)}, f32[512,128]{1,0:T(8,128)}, u32[]{:S(2)}) copy-start(f32[512,128]{1,0:T(8,128)} %param.8) | copy-start | bytes 786436
  1.3 0.7 copy-start.5
  1.3 0.7 copy-start.6
  2.1 1.2 %copy-start.1 = (f32[16,128,128]{2,1,0:T(8,128)S(1)}, f32[16,128,128]{2,1,0:T(8,128)}, u32[]{:S(2)}) copy-start(f32[16,128,128]{2,1,0:T(8,128)} %tiles.1) | copy-start | bytes 3145732
  3.7 8.8 %collective-permute-start = (f32[520,128]{1,0:T(8,128)S(1)}, f32[520,128]{1,0:T(8,128)S(1)}, u32[]{:S(2)}, u32[]{:S(2)}) collective-permute-start(f32[520,128]{1,0:T(8,128)S(1)} %get-tuple-element.21), channel_id=1, source_target_pairs={{0,1},{1,0},{2,3},{3,2},{4,5},{5,4},{6,7},{7,6},{8,9},{9,8},{10,11... | collective-permute-start | bytes 798728 | tf_op jit(solution)/shard_map/ppermute | solution.py:185
  4.3 8.3 %collective-permute-start.6 = (f32[128,128]{1,0:T(8,128)S(1)}, f32[128,128]{1,0:T(8,128)S(1)}, u32[]{:S(2)}, u32[]{:S(2)}) collective-permute-start(f32[128,128]{1,0:T(8,128)S(1)} %bitcast.22), channel_id=1, source_target_pairs={{0,16},{4,20},{8,24},{12,28},{16,0},{20,4},{24,8},{28,12},{1,17},{... | collective-permute-start | bytes 196616 | tf_op jit(solution)/shard_map/ppermute | solution.py:185
  7.9 6.1 %collective-permute-start.4 = (f32[128,128]{1,0:T(8,128)S(1)}, f32[128,128]{1,0:T(8,128)S(1)}, u32[]{:S(2)}, u32[]{:S(2)}) collective-permute-start(f32[128,128]{1,0:T(8,128)S(1)} %bitcast.23), channel_id=1, source_target_pairs={{0,8},{4,12},{8,0},{12,4},{16,24},{20,28},{24,16},{28,20},{1,9},{5... | collective-permute-start | bytes 196616 | tf_op jit(solution)/shard_map/ppermute | solution.py:185
  9.5 14.2 %collective-permute-start.3 = (f32[128,128]{1,0:T(8,128)S(1)}, f32[128,128]{1,0:T(8,128)S(1)}, u32[]{:S(2)}, u32[]{:S(2)}) collective-permute-start(f32[128,128]{1,0:T(8,128)S(1)} %bitcast.24), channel_id=1, source_target_pairs={{0,4},{4,0},{8,12},{12,8},{16,20},{20,16},{24,28},{28,24},{1,5},{5... | collective-permute-start | bytes 196616 | tf_op jit(solution)/shard_map/ppermute | solution.py:185
  11.0 9.3 %collective-permute-start.1 = (f32[520,128]{1,0:T(8,128)S(1)}, f32[520,128]{1,0:T(8,128)S(1)}, u32[]{:S(2)}, u32[]{:S(2)}) collective-permute-start(f32[520,128]{1,0:T(8,128)S(1)} %get-tuple-element.22), channel_id=1, source_target_pairs={{0,2},{1,3},{2,0},{3,1},{4,6},{5,7},{6,4},{7,5},{8,10},{9,11},{10,... | collective-permute-start | bytes 798728 | tf_op jit(solution)/shard_map/ppermute | solution.py:185
  12.5 11.2 %collective-permute-start.2 = (f32[520,128]{1,0:T(8,128)S(1)}, f32[520,128]{1,0:T(8,128)S(1)}, u32[]{:S(2)}, u32[]{:S(2)}) collective-permute-start(f32[520,128]{1,0:T(8,128)S(1)} %get-tuple-element.23), channel_id=1, source_target_pairs={{0,3},{1,2},{2,1},{3,0},{4,7},{5,6},{6,5},{7,4},{8,11},{9,10},{10,... | collective-permute-start | bytes 798728 | tf_op jit(solution)/shard_map/ppermute | solution.py:185
  12.5 5.0 %collective-permute-start.8 = (f32[128,128]{1,0:T(8,128)S(1)}, f32[128,128]{1,0:T(8,128)S(1)}, u32[]{:S(2)}, u32[]{:S(2)}) collective-permute-start(f32[128,128]{1,0:T(8,128)S(1)} %collective-permute-done.6.refs_8_), channel_id=1, source_target_pairs={{0,8},{4,12},{8,0},{12,4},{16,24},{20,28},{24,16},{28,20},{1,9},{5... | collective-permute-start | bytes 196616 | tf_op jit(solution)/shard_map/ppermute | solution.py:185
  14.0 9.7 %collective-permute-start.7 = (f32[128,128]{1,0:T(8,128)S(1)}, f32[128,128]{1,0:T(8,128)S(1)}, u32[]{:S(2)}, u32[]{:S(2)}) collective-permute-start(f32[128,128]{1,0:T(8,128)S(1)} %collective-permute-done.6.refs_8_), channel_id=1, source_target_pairs={{0,4},{4,0},{8,12},{12,8},{16,20},{20,16},{24,28},{28,24},{1,5},{5... | collective-permute-start | bytes 196616 | tf_op jit(solution)/shard_map/ppermute | solution.py:185
  17.5 6.2 %collective-permute-start.5 = (f32[128,128]{1,0:T(8,128)S(1)}, f32[128,128]{1,0:T(8,128)S(1)}, u32[]{:S(2)}, u32[]{:S(2)}) collective-permute-start(f32[128,128]{1,0:T(8,128)S(1)} %collective-permute-done.4.refs_6_), channel_id=1, source_target_pairs={{0,4},{4,0},{8,12},{12,8},{16,20},{20,16},{24,28},{28,24},{1,5},{5... | collective-permute-start | bytes 196616 | tf_op jit(solution)/shard_map/ppermute | solution.py:185
  20.3 4.3 %collective-permute-start.9 = (f32[128,128]{1,0:T(8,128)S(1)}, f32[128,128]{1,0:T(8,128)S(1)}, u32[]{:S(2)}, u32[]{:S(2)}) collective-permute-start(f32[128,128]{1,0:T(8,128)S(1)} %collective-permute-done.8.refs_10_), channel_id=1, source_target_pairs={{0,4},{4,0},{8,12},{12,8},{16,20},{20,16},{24,28},{28,24},{1,5},{5... | collective-permute-start | bytes 196616 | tf_op jit(solution)/shard_map/ppermute | solution.py:185
  28.8 8.6 %copy-start.2 = (f32[512,256]{1,0:T(8,128)S(1)}, f32[512,256]{1,0:T(8,128)}, u32[]{:S(2)}) copy-start(f32[512,256]{1,0:T(8,128)} %refs_8_.1) | copy-start | bytes 1572868
  28.8 1.4 %collective-permute-start.10 = (f32[256,128]{1,0:T(8,128)S(1)}, f32[256,128]{1,0:T(8,128)S(1)}, u32[]{:S(2)}, u32[]{:S(2)}) collective-permute-start(f32[256,128]{1,0:T(8,128)S(1)} %get-tuple-element.25), channel_id=1, source_target_pairs={{0,1},{1,0},{2,3},{3,2},{4,5},{5,4},{6,7},{7,6},{8,9},{9,8},{10,11... | collective-permute-start | bytes 393224 | tf_op jit(solution)/shard_map/ppermute | solution.py:185
  30.3 7.1 %copy-start.3 = (f32[128,256]{1,0:T(8,128)S(1)}, f32[128,256]{1,0:T(8,128)}, u32[]{:S(2)}) copy-start(f32[128,256]{1,0:T(8,128)} %refs_6_.1) | copy-start | bytes 393220
  30.3 5.7 %collective-permute-start.11 = (f32[256,128]{1,0:T(8,128)S(1)}, f32[256,128]{1,0:T(8,128)S(1)}, u32[]{:S(2)}, u32[]{:S(2)}) collective-permute-start(f32[256,128]{1,0:T(8,128)S(1)} %add.28), channel_id=1, source_target_pairs={{0,2},{1,3},{2,0},{3,1},{4,6},{5,7},{6,4},{7,5},{8,10},{9,11},{10,... | collective-permute-start | bytes 393224 | tf_op jit(solution)/shard_map/ppermute | solution.py:185
  36.0 1.4 %copy-start.4 = (f32[256]{0:T(256)S(1)}, f32[256]{0:T(256)}, u32[]{:S(2)}) copy-start(f32[256]{0:T(256)} %param.10) | copy-start | bytes 3076
  36.0 1.4 %collective-permute-start.12 = (f32[256,128]{1,0:T(8,128)S(1)}, f32[256,128]{1,0:T(8,128)S(1)}, u32[]{:S(2)}, u32[]{:S(2)}) collective-permute-start(f32[256,128]{1,0:T(8,128)S(1)} %add.29.refs_4_), channel_id=1, source_target_pairs={{0,1},{1,0},{2,3},{3,2},{4,5},{5,4},{6,7},{7,6},{8,9},{9,8},{10,11... | collective-permute-start | bytes 393224 | tf_op jit(solution)/shard_map/ppermute | solution.py:185
  41.7 9.1 %collective-permute-start.13 = (f32[584,128]{1,0:T(8,128)S(1)}, f32[584,128]{1,0:T(8,128)S(1)}, u32[]{:S(2)}, u32[]{:S(2)}) collective-permute-start(f32[584,128]{1,0:T(8,128)S(1)} %get-tuple-element.28), channel_id=1, source_target_pairs={{0,4},{4,0},{8,12},{12,8},{16,20},{20,16},{24,28},{28,24},{1,5},{5... | collective-permute-start | bytes 897032 | tf_op jit(solution)/shard_map/ppermute | solution.py:185
  50.9 5.5 %collective-permute-start.14 = (f32[328,128]{1,0:T(8,128)S(1)}, f32[328,128]{1,0:T(8,128)S(1)}, u32[]{:S(2)}, u32[]{:S(2)}) collective-permute-start(f32[328,128]{1,0:T(8,128)S(1)} %get-tuple-element.30), channel_id=1, source_target_pairs={{0,8},{4,12},{8,0},{12,4},{16,24},{20,28},{24,16},{28,20},{1,9},{5... | collective-permute-start | bytes 503816 | tf_op jit(solution)/shard_map/ppermute | solution.py:185
  56.4 6.6 %collective-permute-start.15 = (f32[200,128]{1,0:T(8,128)S(1)}, f32[200,128]{1,0:T(8,128)S(1)}, u32[]{:S(2)}, u32[]{:S(2)}) collective-permute-start(f32[200,128]{1,0:T(8,128)S(1)} %get-tuple-element.32), channel_id=1, source_target_pairs={{0,16},{4,20},{8,24},{12,28},{16,0},{20,4},{24,8},{28,12},{1,17},{... | collective-permute-start | bytes 307208 | tf_op jit(solution)/shard_map/ppermute | solution.py:185
  63.1 4.7 %collective-permute-start.17 = (f32[200,128]{1,0:T(8,128)S(1)}, f32[200,128]{1,0:T(8,128)S(1)}, u32[]{:S(2)}, u32[]{:S(2)}) collective-permute-start(f32[200,128]{1,0:T(8,128)S(1)} %add.42.refs_0_), channel_id=1, source_target_pairs={{0,2},{1,3},{2,0},{3,1},{4,6},{5,7},{6,4},{7,5},{8,10},{9,11},{10,... | collective-permute-start | bytes 307208 | tf_op jit(solution)/shard_map/ppermute | solution.py:185
  64.7 3.2 %collective-permute-start.16 = (f32[200,128]{1,0:T(8,128)S(1)}, f32[200,128]{1,0:T(8,128)S(1)}, u32[]{:S(2)}, u32[]{:S(2)}) collective-permute-start(f32[200,128]{1,0:T(8,128)S(1)} %add.42.refs_0_), channel_id=1, source_target_pairs={{0,1},{1,0},{2,3},{3,2},{4,5},{5,4},{6,7},{7,6},{8,9},{9,8},{10,11... | collective-permute-start | bytes 307208 | tf_op jit(solution)/shard_map/ppermute | solution.py:185
  67.8 1.3 %collective-permute-start.18 = (f32[200,128]{1,0:T(8,128)S(1)}, f32[200,128]{1,0:T(8,128)S(1)}, u32[]{:S(2)}, u32[]{:S(2)}) collective-permute-start(f32[200,128]{1,0:T(8,128)S(1)} %collective-permute-done.17.refs_2_), channel_id=1, source_target_pairs={{0,1},{1,0},{2,3},{3,2},{4,5},{5,4},{6,7},{7,6},{8,9},{9,8},{10,11... | collective-permute-start | bytes 307208 | tf_op jit(solution)/shard_map/ppermute | solution.py:185

commit v2 on v0

v2 whole, which is shorter than its diff:
```python
import functools

import jax
import jax.numpy as jnp
from jax import lax
from jax.experimental import pallas as pl
from jax.experimental.pallas import tpu as pltpu
from jax.sharding import PartitionSpec as P

LANES = 128
PAD = 8
F32 = jnp.float32
BF16 = jnp.bfloat16
VMEM = pl.BlockSpec(memory_space=pltpu.VMEM)
SMEM = pl.BlockSpec(memory_space=pltpu.SMEM)
HBM = pl.BlockSpec(memory_space=pltpu.HBM)


def halves(x):
    high = x.astype(BF16).astype(F32)
    return high, x - high


def dot3(a, b, dims=(((1,), (0,)), ((), ()))):
    ah, al = halves(a)
    bh, bl = halves(b)
    ah, al, bh, bl = (v.astype(BF16) for v in (ah, al, bh, bl))
    dot = functools.partial(lax.dot_general, dimension_numbers=dims, preferred_element_type=F32)
    return dot(ah, bh) + dot(ah, bl) + dot(al, bh)


def call(kernel, out_shapes, in_specs, scratch, flops, moved, name, limit=24):
    return pl.pallas_call(
        kernel,
        out_shape=[
            jax.ShapeDtypeStruct(*(s if isinstance(s[0], tuple) else (s, F32))) for s in out_shapes
        ],
        in_specs=in_specs,
        out_specs=[VMEM] * len(out_shapes),
        scratch_shapes=scratch,
        compiler_params=pltpu.CompilerParams(vmem_limit_bytes=limit << 20),
        cost_estimate=pl.CostEstimate(flops=flops, bytes_accessed=moved, transcendentals=0),
        name=name,
    )


def pack_kernel(reps, blocks, part, rep_at, at_loop, count, features, tiles, rows, cols, *refs):
    own, outs = refs[0], refs[1 : 1 + reps]
    held, turned, row_ids, col_ids, sem = refs[1 + reps :]
    here, loop_at = rep_at[0], at_loop[0]
    slots, side = tiles.shape[0], tiles.shape[1]
    chunks = sem.shape[0] - 2 - blocks
    step = slots // chunks
    small = [
        pltpu.make_async_copy(source, target, sem.at[n])
        for n, (source, target) in enumerate([(rows, row_ids), (cols, col_ids)])
    ]
    large = [
        pltpu.make_async_copy(
            tiles.at[pl.ds(n * step, step)], held.at[pl.ds(n * step, step)], sem.at[2 + n]
        )
        for n in range(chunks)
    ]
    pieces = [
        pltpu.make_async_copy(
            features.at[pl.ds(pl.multiple_of(b * side + here * part, 8), part), :],
            own.at[pl.ds(b * part, part), :],
            sem.at[2 + chunks + b],
        )
        for b in range(blocks)
    ]
    for copy in small + large + pieces:
        copy.start()
    for copy in small:
        copy.wait()
    local_rows = row_ids[...] - loop_at * blocks
    shift = blocks.bit_length() - 1
    column = (((col_ids[...] >> shift) ^ loop_at) << shift) | (col_ids[...] & (blocks - 1))
    meta = jnp.concatenate([local_rows, column], axis=0).astype(F32)
    for d in range(reps):
        outs[d][pl.ds(slots * part, 2), pl.ds(0, slots)] = meta
    alive = count[0]
    for n in range(chunks):
        large[n].wait()
        for s in range(n * step, (n + 1) * step):
            turned[s] = jnp.where(s < alive, held[s].T, jnp.zeros((side, side), F32))
            for d in range(reps):
                start = pl.multiple_of((here ^ d) * part, 8)
                outs[d][pl.ds(s * part, part), :] = turned[s, pl.ds(start, part), :]
    for copy in pieces:
        copy.wait()


def build_kernel(reps, blocks, part, slots, *refs):
    tiles = refs[:reps]
    high_out, low_out, dense, place_vector, place, sem = refs[-6:]
    side = dense.shape[1] // blocks
    for d in range(reps):
        place_vector[d] = tiles[d][pl.ds(slots * part, PAD), :].astype(jnp.int32)
    copy = pltpu.make_async_copy(place_vector, place, sem)
    copy.start()
    dense[...] = jnp.zeros_like(dense)
    copy.wait()
    for d in range(reps):
        for s in range(slots):
            lane = pl.ds(pl.multiple_of(place[d, 0, s] * side, LANES), side)
            at = pl.ds(pl.multiple_of(place[d, 1, s] * part, 8), part)
            dense[at, lane] = dense[at, lane] + tiles[d][pl.ds(s * part, part), :]
    for k in range(dense.shape[0] // side):
        at = pl.ds(k * side, side)
        high, low = halves(dense[at, :])
        high_out[at, :] = high.astype(BF16)
        low_out[at, :] = low.astype(BF16)


def forward_kernel(loops, here, high, low, *refs):
    feats = refs[:loops]
    send, keep, left, acc = refs[loops:]
    rows, width = feats[0].shape
    for k in range(loops):
        at = pl.ds(k * rows, rows)
        upper, lower = halves(feats[k][...].T)
        left[:width, at] = upper.astype(BF16)
        left[width:, at] = lower.astype(BF16)
    both = jnp.dot(left[...], high[...], preferred_element_type=F32)
    rest = jnp.dot(left[:width, :], low[...], preferred_element_type=F32)
    acc[...] = both[:width, :] + both[width:, :] + rest
    half = acc.shape[0] // 2
    core = here[0] & 1
    keep[...] = acc[pl.ds(pl.multiple_of(core * half, 8), half), :]
    send[...] = acc[pl.ds(pl.multiple_of((1 - core) * half, 8), half), :]


def times(high, low, right, width):
    both = jnp.dot(high, right, preferred_element_type=F32)
    rest = jnp.dot(low, right[:, :width], preferred_element_type=F32)
    return both[:, :width] + both[:, width:] + rest


def backward_kernel(
    reps, blocks, groups, here, high, low, mine, other, weight, bias, cotangent, *refs
):
    outs = refs[: len(groups)]
    output, grads, piece_t, agg, right = refs[len(groups) :]
    width, total = agg.shape
    half, side = width // 2, total // blocks
    core = here[0] & 1
    agg[pl.ds(pl.multiple_of(core * half, 8), half), :] = mine[...]
    agg[pl.ds(pl.multiple_of((1 - core) * half, 8), half), :] = other[...]
    piece = width // reps
    piece_t[...] = agg[pl.ds(pl.multiple_of(here[0] * piece, 8), piece), :]
    w = weight[...]
    for b in range(blocks):
        at = pl.ds(b * side, side)
        pre = dot3(agg[:, at].T, w) + bias[...]
        gate = jax.nn.sigmoid(pre)
        output[at, :] = pre * gate
        gradient = cotangent[at, :] * gate * (1.0 + pre * (1.0 - gate))
        grads[at, :] = gradient
        spread = dot3(gradient, w, (((1,), (1,)), ((), ())))
        upper, lower = halves(spread)
        right[at, :width] = upper.astype(BF16)
        right[at, width:] = lower.astype(BF16)
    for group, out in zip(groups, outs):
        size = out.shape[0] // len(group)
        for n, k in enumerate(group):
            at = pl.ds(k * size, size)
            out[pl.ds(n * size, size), :] = times(high[at, :], low[at, :], right[...], width)


def weight_kernel(piece_t, grads, out):
    piece, groups = piece_t.shape[0], grads.shape[1] // LANES
    g = grads[...]
    grad_weight = dot3(piece_t[...], g)
    grad_bias = jnp.sum(g, axis=0, keepdims=True)
    for q in range(groups):
        out[pl.ds(q * piece, piece), :] = grad_weight[:, q * LANES : (q + 1) * LANES]
    tail = [grad_bias[:, q * LANES : (q + 1) * LANES] for q in range(groups)]
    tail.append(jnp.zeros((PAD - groups, LANES), F32))
    out[pl.ds(groups * piece, PAD), :] = jnp.concatenate(tail, axis=0)


def add_kernel(cuts, count, *refs):
    mine, theirs, outs = refs[:count], refs[count : 2 * count], refs[2 * count :]
    for cut, out in zip(cuts, outs):
        to = 0
        for pair, first, rows in cut:
            at = pl.ds(first, rows)
            out[pl.ds(to, rows), :] = mine[pair][at, :] + theirs[pair][at, :]
            to += rows


def add(mine, theirs, cuts=None):
    cuts = cuts or [[(n, 0, x.shape[0])] for n, x in enumerate(mine)]
    total = sum(x.size for x in mine)
    return call(
        functools.partial(add_kernel, cuts, len(mine)),
        [(sum(rows for _, _, rows in cut), mine[0].shape[1]) for cut in cuts],
        [VMEM] * (2 * len(mine)),
        [],
        total,
        12 * total,
        "add",
    )(*mine, *theirs)


def final_kernel(reps, blocks, part, piece, here, *refs):
    parts = refs[:reps]
    grad_features, grad_weight, grad_bias = refs[reps:]
    side = grad_features.shape[0] // blocks
    groups = grad_weight.shape[1] // LANES
    base = blocks * part
    for d in range(reps):
        q = here[0] ^ d
        for b in range(blocks):
            at = pl.ds(pl.multiple_of(b * side + q * part, 8), part)
            grad_features[at, :] = parts[d][pl.ds(b * part, part), :]
        at = pl.ds(pl.multiple_of(q * piece, 8), piece)
        for g in range(groups):
            grad_weight[at, pl.ds(g * LANES, LANES)] = parts[d][pl.ds(base + g * piece, piece), :]
    for g in range(groups):
        row = parts[0][pl.ds(base + groups * piece + g, 1), :]
        grad_bias[:, pl.ds(g * LANES, LANES)] = row


def per_device(features, weight, bias, tile_values, tile_rows, tile_cols, tile_count, cotangent):
    loops, reps = lax.axis_size("loop"), lax.axis_size("rep")
    slots, side = tile_values.shape[0], tile_values.shape[1]
    total, width = features.shape
    wide = weight.shape[1]
    blocks = total // side
    part, piece = side // reps, width // reps
    size, depth = blocks * part, loops * blocks * part
    extra = wide // LANES * piece + PAD
    here = lax.axis_index("rep").astype(jnp.int32).reshape(1)
    loop_at = lax.axis_index("loop").astype(jnp.int32).reshape(1)
    bias = bias.reshape(1, wide)

    def swap(x, axis, bit):
        n = lax.axis_size(axis)
        return lax.ppermute(x, axis, [(i, i ^ bit) for i in range(n)])

    chunks = 4 if slots % 4 == 0 else 1
    sources = (features, tile_values, tile_rows[None], tile_cols[None])
    own, *parcels = call(
        functools.partial(pack_kernel, reps, blocks, part),
        [(size, width)] + [(slots * part + PAD, side)] * reps,
        [SMEM] * 3 + [HBM] * 4,
        [
            pltpu.VMEM((slots, side, side), F32),
            pltpu.VMEM((slots, side, side), F32),
            pltpu.VMEM((1, slots), jnp.int32),
            pltpu.VMEM((1, slots), jnp.int32),
            pltpu.SemaphoreType.DMA((2 + chunks + blocks,)),
        ],
        0,
        2 * tile_values.size * 4,
        "pack",
    )(here, loop_at, tile_count, *[pltpu.with_memory_space_constraint(x, pltpu.HBM) for x in sources])
    tiles = [parcels[0]] + [swap(parcels[d], "rep", d) for d in range(1, reps)]

    feats = {0: own}
    bit = loops // 2
    while bit:
        for k in list(feats):
            feats[k | bit] = swap(feats[k], "loop", bit)
        bit //= 2

    high, low = call(
        functools.partial(build_kernel, reps, blocks, part, slots),
        [((depth, total), BF16)] * 2,
        [VMEM] * (reps + 3),
        [
            pltpu.VMEM((depth, total), F32),
            pltpu.VMEM((reps, PAD, LANES), jnp.int32),
            pltpu.SMEM((reps, PAD, LANES), jnp.int32),
            pltpu.SemaphoreType.DMA,
        ],
        0,
        8 << 20,
        "build",
    )(*tiles, weight, bias, cotangent)

    send, keep = call(
        functools.partial(forward_kernel, loops),
        [(width // 2, total)] * 2,
        [SMEM] + [VMEM] * (2 + loops),
        [pltpu.VMEM((2 * width, depth), BF16), pltpu.VMEM((width, total), F32)],
        2 * depth * total * width * 3,
        4 << 20,
        "forward",
    )(here, high, low, *[feats[k] for k in range(loops)])
    (mine,) = add([keep], [swap(send, "rep", 1)])
    bit = 2
    while bit < reps:
        (mine,) = add([mine], [swap(mine, "rep", bit)])
        bit *= 2
    other = swap(mine, "rep", 1)

    even = range(0, loops, 2)
    on, stay = [k for k in even if k & 2], [k for k in even if not k & 2]
    groups = [[k | 1 for k in on], [k | 1 for k in stay], on, stay]
    *moved, output, grads, piece_t = call(
        functools.partial(backward_kernel, reps, blocks, groups),
        [(len(g) * size, width) for g in groups] + [(total, wide)] * 2 + [(piece, total)],
        [SMEM] + [VMEM] * 7,
        [pltpu.VMEM((width, total), F32), pltpu.VMEM((total, 2 * width), BF16)],
        2 * depth * total * width * 3,
        4 << 20,
        "backward",
    )(here, high, low, mine, other, weight, bias, cotangent)
    on_term, stay_term = swap(moved[0], "loop", 1), swap(moved[1], "loop", 1)
    (grad,) = call(
        weight_kernel,
        [(extra, LANES)],
        [VMEM] * 2,
        [],
        2 * piece * total * wide * 3,
        1 << 20,
        "weight",
    )(piece_t, grads)

    last = loops // 2
    grad_term = swap(grad, "loop", last)
    going, grad = add([moved[2], grad], [on_term, grad_term])
    term = swap(going, "loop", 2)
    grad_term = swap(grad, "loop", 1)
    (held,) = add([moved[3]], [stay_term])
    bit, rest = 2, stay
    while bit < last:
        ahead = [(0, n * size, size) for n, k in enumerate(rest) if k & (2 * bit)]
        behind = [(0, n * size, size) for n, k in enumerate(rest) if not k & (2 * bit)]
        rest = [k for k in rest if not k & (2 * bit)]
        going, held, grad = add([held, grad], [term, grad_term], [ahead, behind, [(1, 0, extra)]])
        term = swap(going, "loop", 2 * bit)
        grad_term = swap(grad, "loop", bit)
        bit *= 2
    (both,) = add([held, grad], [term, grad_term], [[(0, 0, size), (1, 0, extra)]])

    parts = {0: both}
    bit = reps // 2
    while bit:
        for k in list(parts):
            parts[k | bit] = swap(parts[k], "rep", bit)
        bit //= 2
    grad_features, grad_weight, grad_bias = call(
        functools.partial(final_kernel, reps, blocks, part, piece),
        [(total, width), (width, wide), (1, wide)],
        [SMEM] + [VMEM] * reps,
        [],
        0,
        2 * total * width * 4,
        "final",
    )(here, *[parts[d] for d in range(reps)])
    return (output, grad_features, grad_weight, grad_bias.reshape(wide))


def solution(mesh):
    return jax.shard_map(
        per_device,
        mesh=mesh,
        in_specs=(
            P("loop", None),
            P(),
            P(),
            P(("loop", "rep"), None, None),
            P(("loop", "rep")),
            P(("loop", "rep")),
            P(("loop", "rep")),
            P("loop", None),
        ),
        out_specs=(P("loop", None), P("loop", None), P(), P()),
        check_vma=False,
    )
```

time: 294 us -> 60.3 us (0.21)
  waiting for transfers between devices: 237 us -> 23.4 us
  starting transfers between devices: 0.2 us -> 27.7 us
  blocking collectives: 19.7 us -> 0 us
  between operations: 14.6 us -> 1.41 us
  local copies, waits for them, and re-layouts: 11.6 us -> 0.68 us
  matrix products: 9.66 us -> 0 us
  Pallas kernels: 0 us -> 6.91 us
    psum x3 -> x0, waiting for transfers between devices: 118 us -> none  [the longest x1 53.6 us: per_device(): grad_weight, grad_bias = lax.psum((weight_term, bias_term), 'loop')]
    reduce_scatter x1 -> x0, waiting for transfers between devices: 66 us -> none  [per_device(): lax.psum_scatter(lax.slice_in_dim(placed, 0, rows_here * lax.axis_size('l...]
    all_gather x1 -> x0, waiting for transfers between devices: 52 us -> none  [per_device(): gathered = lax.all_gather(features, 'loop', axis=0, tiled=True)]
    ppermute x0 -> x23, starting transfers between devices: none -> 27.7 us  [swap(): return lax.ppermute(x, axis, [(i, i ^ bit) for i in range(n)])]
    ppermute x0 -> x23, waiting for transfers between devices: none -> 23.4 us  [swap(): return lax.ppermute(x, axis, [(i, i ^ bit) for i in range(n)])]
    psum x1 -> x0, blocking collectives: 19.7 us -> none  [per_device(): grad_weight, grad_bias = lax.psum((weight_term, bias_term), 'loop')]
    dot_general x7 -> x0, matrix products: 9.66 us -> none  [the longest x1 2.46 us: per_device(): preactive = jnp.dot(aggregated, weight, precision=highest) + bias]
    pallas_call x0 -> x12, Pallas kernels: none -> 6.91 us  [the longest x1 1.78 us: per_device(): call(functools.partial(build_kernel, reps, blocks, part, slots), [((depth...]
  transfers between devices with their start and end apart: 5 -> 23, of which waited for: 5 -> 12; matrix products, arithmetic and copies ran while one was open for 1% -> 0% of each run, Pallas kernels for 0% -> 3%
where the time goes in v2:
time: 60.3 us; the launch traced here: 60.1 us
  starting transfers between devices  27.7 us (46%)
  waiting for transfers between devices  23.4 us (39%)
  Pallas kernels  6.91 us (11%)
  between operations  1.41 us (2%)
  local copies, waits for them, and re-layouts  0.68 us (1%)
    ppermute x23, starting transfers between devices, swap(): return lax.ppermute(x, axis, [(i, i ^ bit) for i in range(n)])  27.7 us
    ppermute x23, waiting for transfers between devices, swap(): return lax.ppermute(x, axis, [(i, i ^ bit) for i in range(n)])  23.4 us
    pallas_call x1, Pallas kernels, per_device(): call(functools.partial(build_kernel, reps, blocks, part, slots), [((depth...  1.78 us
    pallas_call x1, Pallas kernels, per_device(): call(functools.partial(pack_kernel, reps, blocks, part), [(size, width)]...  1.75 us
    pallas_call x1, Pallas kernels, per_device(): call(functools.partial(backward_kernel, reps, blocks, groups), [(len(g) *...  1.57 us
  transfers between devices with their start and end apart: 23, of which 12 were waited for; matrix products, arithmetic and copies ran while one was open for 0% of the time, Pallas kernels for 3%

profile of v2, /device:TPU:0, one launch (start us, length us, event | category | flops | bytes accessed | tf_op | source)
XLA Modules:
  0.0 60.1 jit_solution(2650436227948462851)
XLA Ops:
  1.3 1.7 %pack.1 = (f32[128,128]{1,0:T(8,128)S(1)}, f32[520,128]{1,0:T(8,128)S(1)}, f32[520,128]{1,0:T(8,128)S(1)}, f32[520,128]{1,0:T(8,128)S(1)}, f32[520,128]{1,0:T(8,128)S(1)}) custom-call(s32[1]{0:T(128)} %bitcast.rep_at.here, s32[1]{0:T(128)} %bitcast.1.at_loop, s32[1]{0:T(128)S(6)} %copy.12.count, f32[512,128]{1,0:T(8,128)} %features.1, ...), custom_call_target="tpu_custom_call" | custom-call | bytes 2097152 | tf_op jit(solution)/shard_map/pack/pallas_call | solution.py:245
  3.1 0.6 collective-permute-start
  3.6 2.6 %collective-permute-start.1 = (f32[520,128]{1,0:T(8,128)S(1)}, f32[520,128]{1,0:T(8,128)S(1)}, u32[]{:S(2)}, u32[]{:S(2)}) collective-permute-start(f32[520,128]{1,0:T(8,128)S(1)} %get-tuple-element.30), channel_id=1, source_target_pairs={{0,2},{1,3},{2,0},{3,1},{4,6},{5,7},{6,4},{7,5},{8,10},{9,11},{10,... | collective-permute-start | bytes 798728 | tf_op jit(solution)/shard_map/ppermute | solution.py:241
  6.2 0.0 collective-permute-start.2
  6.3 2.8 %collective-permute-start.6 = (f32[128,128]{1,0:T(8,128)S(1)}, f32[128,128]{1,0:T(8,128)S(1)}, u32[]{:S(2)}, u32[]{:S(2)}) collective-permute-start(f32[128,128]{1,0:T(8,128)S(1)} %get-tuple-element.34.refs_0_), channel_id=1, source_target_pairs={{0,16},{4,20},{8,24},{12,28},{16,0},{20,4},{24,8},{28,12},{1,17},{... | collective-permute-start | bytes 196616 | tf_op jit(solution)/shard_map/ppermute | solution.py:241
  9.1 1.6 %collective-permute-start.4 = (f32[128,128]{1,0:T(8,128)S(1)}, f32[128,128]{1,0:T(8,128)S(1)}, u32[]{:S(2)}, u32[]{:S(2)}) collective-permute-start(f32[128,128]{1,0:T(8,128)S(1)} %get-tuple-element.34.refs_0_), channel_id=1, source_target_pairs={{0,8},{4,12},{8,0},{12,4},{16,24},{20,28},{24,16},{28,20},{1,9},{5... | collective-permute-start | bytes 196616 | tf_op jit(solution)/shard_map/ppermute | solution.py:241
  10.6 2.2 %collective-permute-done.6.refs_4_ = f32[128,128]{1,0:T(8,128)S(1)} collective-permute-done((f32[128,128]{1,0:T(8,128)S(1)}, f32[128,128]{1,0:T(8,128)S(1)}, u32[]{:S(2)}, u32[]{:S(2)}) %collective-permute-start.6) | collective-permute-done | bytes 65568 | tf_op jit(solution)/shard_map/ppermute | solution.py:241
  12.8 1.1 %collective-permute-start.8 = (f32[128,128]{1,0:T(8,128)S(1)}, f32[128,128]{1,0:T(8,128)S(1)}, u32[]{:S(2)}, u32[]{:S(2)}) collective-permute-start(f32[128,128]{1,0:T(8,128)S(1)} %collective-permute-done.6.refs_4_), channel_id=1, source_target_pairs={{0,8},{4,12},{8,0},{12,4},{16,24},{20,28},{24,16},{28,20},{1,9},{5... | collective-permute-start | bytes 196616 | tf_op jit(solution)/shard_map/ppermute | solution.py:241
  13.9 0.0 collective-permute-done.4.refs_2_
  13.9 1.5 %collective-permute-start.3 = (f32[128,128]{1,0:T(8,128)S(1)}, f32[128,128]{1,0:T(8,128)S(1)}, u32[]{:S(2)}, u32[]{:S(2)}) collective-permute-start(f32[128,128]{1,0:T(8,128)S(1)} %get-tuple-element.34.refs_0_), channel_id=1, source_target_pairs={{0,4},{4,0},{8,12},{12,8},{16,20},{20,16},{24,28},{28,24},{1,5},{5... | collective-permute-start | bytes 196616 | tf_op jit(solution)/shard_map/ppermute | solution.py:241
  15.4 1.7 %collective-permute-done.8.refs_6_ = f32[128,128]{1,0:T(8,128)S(1)} collective-permute-done((f32[128,128]{1,0:T(8,128)S(1)}, f32[128,128]{1,0:T(8,128)S(1)}, u32[]{:S(2)}, u32[]{:S(2)}) %collective-permute-start.8) | collective-permute-done | bytes 65568 | tf_op jit(solution)/shard_map/ppermute | solution.py:241
  17.1 1.6 %collective-permute-start.7 = (f32[128,128]{1,0:T(8,128)S(1)}, f32[128,128]{1,0:T(8,128)S(1)}, u32[]{:S(2)}, u32[]{:S(2)}) collective-permute-start(f32[128,128]{1,0:T(8,128)S(1)} %collective-permute-done.6.refs_4_), channel_id=1, source_target_pairs={{0,4},{4,0},{8,12},{12,8},{16,20},{20,16},{24,28},{28,24},{1,5},{5... | collective-permute-start | bytes 196616 | tf_op jit(solution)/shard_map/ppermute | solution.py:241
  18.7 0.0 collective-permute-done.refs_1_
  18.7 0.4 collective-permute-start.5
  19.1 0.0 collective-permute-done.1.refs_2_
  19.1 1.6 %collective-permute-start.9 = (f32[128,128]{1,0:T(8,128)S(1)}, f32[128,128]{1,0:T(8,128)S(1)}, u32[]{:S(2)}, u32[]{:S(2)}) collective-permute-start(f32[128,128]{1,0:T(8,128)S(1)} %collective-permute-done.8.refs_6_), channel_id=1, source_target_pairs={{0,4},{4,0},{8,12},{12,8},{16,20},{20,16},{24,28},{28,24},{1,5},{5... | collective-permute-start | bytes 196616 | tf_op jit(solution)/shard_map/ppermute | solution.py:241
  20.7 0.7 %copy-done.2 = f32[256]{0:T(256)S(1)} copy-done((f32[256]{0:T(256)S(1)}, f32[256]{0:T(256)}, u32[]{:S(2)}) %copy-start.2) | copy-done | bytes 1048
  21.4 1.8 %build.1 = (bf16[1024,512]{1,0:T(8,128)(2,1)S(1)}, bf16[1024,512]{1,0:T(8,128)(2,1)S(1)}) custom-call(f32[520,128]{1,0:T(8,128)S(1)} %get-tuple-element.28.refs_0_, f32[520,128]{1,0:T(8,128)S(1)} %collective-permute-done.refs_1_, f32[520,128]{1,0:T(8,128)S(1)} %collective-permute-done.1.refs_2_, f32[520,128]{1,0:T(8,128)S(1)} %collective-permute-done.2.refs_3_, ...), custom_call_target="tpu_custom_call" | custom-call | bytes 8388608 | tf_op jit(solution)/shard_map/build/pallas_call | solution.py:269
  23.2 0.0 collective-permute-done.7.refs_5_
  23.2 0.0 collective-permute-done.5.refs_3_
  23.2 0.4 collective-permute-done.9.refs_7_
  23.6 0.7 %forward.1 = (f32[64,512]{1,0:T(8,128)S(1)}, f32[64,512]{1,0:T(8,128)S(1)}) custom-call(s32[1]{0:T(128)} %bitcast.rep_at.here, bf16[1024,512]{1,0:T(8,128)(2,1)S(1)} %get-tuple-element.32.high, bf16[1024,512]{1,0:T(8,128)(2,1)S(1)} %get-tuple-element.33.low, f32[128,128]{1,0:T(8,128)S(1)} %get-tuple-element.34.refs_0_, ...), custom_call_target="tpu_custom_call" | custom-call | flops 402653184 | bytes 4194304 | tf_op jit(solution)/shard_map/forward/pallas_call | solution.py:284
  24.3 0.1 collective-permute-start.10
  24.4 1.3 %collective-permute-done.10.refs_1_ = f32[64,512]{1,0:T(8,128)S(1)} collective-permute-done((f32[64,512]{1,0:T(8,128)S(1)}, f32[64,512]{1,0:T(8,128)S(1)}, u32[]{:S(2)}, u32[]{:S(2)}) %collective-permute-start.10) | collective-permute-done | bytes 131104 | tf_op jit(solution)/shard_map/ppermute | solution.py:241
  25.8 1.6 %collective-permute-start.11 = (f32[64,512]{1,0:T(8,128)S(1)}, f32[64,512]{1,0:T(8,128)S(1)}, u32[]{:S(2)}, u32[]{:S(2)}) collective-permute-start(f32[64,512]{1,0:T(8,128)S(1)} %add.6.refs_0_), channel_id=1, source_target_pairs={{0,2},{1,3},{2,0},{3,1},{4,6},{5,7},{6,4},{7,5},{8,10},{9,11},{10,... | collective-permute-start | bytes 393224 | tf_op jit(solution)/shard_map/ppermute | solution.py:241
  27.4 4.0 %collective-permute-done.11.refs_1_ = f32[64,512]{1,0:T(8,128)S(1)} collective-permute-done((f32[64,512]{1,0:T(8,128)S(1)}, f32[64,512]{1,0:T(8,128)S(1)}, u32[]{:S(2)}, u32[]{:S(2)}) %collective-permute-start.11) | collective-permute-done | bytes 131104 | tf_op jit(solution)/shard_map/ppermute | solution.py:241
  31.4 0.1 collective-permute-start.12
  31.5 1.3 %collective-permute-done.12.other = f32[64,512]{1,0:T(8,128)S(1)} collective-permute-done((f32[64,512]{1,0:T(8,128)S(1)}, f32[64,512]{1,0:T(8,128)S(1)}, u32[]{:S(2)}, u32[]{:S(2)}) %collective-permute-start.12) | collective-permute-done | bytes 131104 | tf_op jit(solution)/shard_map/ppermute | solution.py:241
  32.8 1.6 %backward.1 = (f32[256,128]{1,0:T(8,128)S(1)}, f32[256,128]{1,0:T(8,128)S(1)}, f32[256,128]{1,0:T(8,128)S(1)}, f32[256,128]{1,0:T(8,128)S(1)}, f32[512,256]{1,0:...) custom-call(s32[1]{0:T(128)} %bitcast.rep_at.here, bf16[1024,512]{1,0:T(8,128)(2,1)S(1)} %get-tuple-element.32.high, ...), custom_call_target="tpu_custom_call" | custom-call | flops 402653184 | bytes 4194304 | tf_op jit(solution)/shard_map/backward/pallas_call | solution.py:303
  34.4 1.4 %collective-permute-start.14 = (f32[256,128]{1,0:T(8,128)S(1)}, f32[256,128]{1,0:T(8,128)S(1)}, u32[]{:S(2)}, u32[]{:S(2)}) collective-permute-start(f32[256,128]{1,0:T(8,128)S(1)} %get-tuple-element.43), channel_id=1, source_target_pairs={{0,4},{4,0},{8,12},{12,8},{16,20},{20,16},{24,28},{28,24},{1,5},{5... | collective-permute-start | bytes 393224 | tf_op jit(solution)/shard_map/ppermute | solution.py:241
  35.8 0.2 weight.3.refs_1_
  36.0 2.4 %collective-permute-start.15 = (f32[72,128]{1,0:T(8,128)S(1)}, f32[72,128]{1,0:T(8,128)S(1)}, u32[]{:S(2)}, u32[]{:S(2)}) collective-permute-start(f32[72,128]{1,0:T(8,128)S(1)} %weight.3.refs_1_), channel_id=1, source_target_pairs={{0,16},{4,20},{8,24},{12,28},{16,0},{20,4},{24,8},{28,12},{1,17},{... | collective-permute-start | bytes 110600 | tf_op jit(solution)/shard_map/ppermute | solution.py:241
  38.5 1.0 %collective-permute-start.13 = (f32[256,128]{1,0:T(8,128)S(1)}, f32[256,128]{1,0:T(8,128)S(1)}, u32[]{:S(2)}, u32[]{:S(2)}) collective-permute-start(f32[256,128]{1,0:T(8,128)S(1)} %get-tuple-element.39), channel_id=1, source_target_pairs={{0,4},{4,0},{8,12},{12,8},{16,20},{20,16},{24,28},{28,24},{1,5},{5... | collective-permute-start | bytes 393224 | tf_op jit(solution)/shard_map/ppermute | solution.py:241
  39.4 1.9 %collective-permute-done.15.refs_3_ = f32[72,128]{1,0:T(8,128)S(1)} collective-permute-done((f32[72,128]{1,0:T(8,128)S(1)}, f32[72,128]{1,0:T(8,128)S(1)}, u32[]{:S(2)}, u32[]{:S(2)}) %collective-permute-start.15) | collective-permute-done | bytes 36896 | tf_op jit(solution)/shard_map/ppermute | solution.py:241
  41.3 0.0 collective-permute-done.14.refs_2_
  41.3 1.1 %collective-permute-start.16 = (f32[256,128]{1,0:T(8,128)S(1)}, f32[256,128]{1,0:T(8,128)S(1)}, u32[]{:S(2)}, u32[]{:S(2)}) collective-permute-start(f32[256,128]{1,0:T(8,128)S(1)} %get-tuple-element.45), channel_id=1, source_target_pairs={{0,8},{4,12},{8,0},{12,4},{16,24},{20,28},{24,16},{28,20},{1,9},{5... | collective-permute-start | bytes 393224 | tf_op jit(solution)/shard_map/ppermute | solution.py:241
  42.4 0.8 %collective-permute-start.17 = (f32[72,128]{1,0:T(8,128)S(1)}, f32[72,128]{1,0:T(8,128)S(1)}, u32[]{:S(2)}, u32[]{:S(2)}) collective-permute-start(f32[72,128]{1,0:T(8,128)S(1)} %get-tuple-element.44.refs_1_), channel_id=1, source_target_pairs={{0,4},{4,0},{8,12},{12,8},{16,20},{20,16},{24,28},{28,24},{1,5},{5... | collective-permute-start | bytes 110600 | tf_op jit(solution)/shard_map/ppermute | solution.py:241
  43.1 0.3 collective-permute-done.13.refs_1_
  43.5 2.9 %collective-permute-done.17.refs_3_ = f32[72,128]{1,0:T(8,128)S(1)} collective-permute-done((f32[72,128]{1,0:T(8,128)S(1)}, f32[72,128]{1,0:T(8,128)S(1)}, u32[]{:S(2)}, u32[]{:S(2)}) %collective-permute-start.17) | collective-permute-done | bytes 36896 | tf_op jit(solution)/shard_map/ppermute | solution.py:241
  46.3 0.0 collective-permute-done.16.refs_2_
  46.4 3.0 %collective-permute-start.18 = (f32[128,128]{1,0:T(8,128)S(1)}, f32[128,128]{1,0:T(8,128)S(1)}, u32[]{:S(2)}, u32[]{:S(2)}) collective-permute-start(f32[128,128]{1,0:T(8,128)S(1)} %get-tuple-element.48), channel_id=1, source_target_pairs={{0,16},{4,20},{8,24},{12,28},{16,0},{20,4},{24,8},{28,12},{1,17},{... | collective-permute-start | bytes 196616 | tf_op jit(solution)/shard_map/ppermute | solution.py:241
  49.4 1.0 %collective-permute-start.19 = (f32[72,128]{1,0:T(8,128)S(1)}, f32[72,128]{1,0:T(8,128)S(1)}, u32[]{:S(2)}, u32[]{:S(2)}) collective-permute-start(f32[72,128]{1,0:T(8,128)S(1)} %get-tuple-element.47.refs_1_), channel_id=1, source_target_pairs={{0,8},{4,12},{8,0},{12,4},{16,24},{20,28},{24,16},{28,20},{1,9},{5... | collective-permute-start | bytes 110600 | tf_op jit(solution)/shard_map/ppermute | solution.py:241
  50.4 3.0 %collective-permute-done.19.refs_3_ = f32[72,128]{1,0:T(8,128)S(1)} collective-permute-done((f32[72,128]{1,0:T(8,128)S(1)}, f32[72,128]{1,0:T(8,128)S(1)}, u32[]{:S(2)}, u32[]{:S(2)}) %collective-permute-start.19) | collective-permute-done | bytes 36896 | tf_op jit(solution)/shard_map/ppermute | solution.py:241
  53.3 1.6 %collective-permute-start.21 = (f32[200,128]{1,0:T(8,128)S(1)}, f32[200,128]{1,0:T(8,128)S(1)}, u32[]{:S(2)}, u32[]{:S(2)}) collective-permute-start(f32[200,128]{1,0:T(8,128)S(1)} %add.11.refs_0_), channel_id=1, source_target_pairs={{0,2},{1,3},{2,0},{3,1},{4,6},{5,7},{6,4},{7,5},{8,10},{9,11},{10,... | collective-permute-start | bytes 307208 | tf_op jit(solution)/shard_map/ppermute | solution.py:241
  54.9 3.1 %collective-permute-done.21.refs_2_ = f32[200,128]{1,0:T(8,128)S(1)} collective-permute-done((f32[200,128]{1,0:T(8,128)S(1)}, f32[200,128]{1,0:T(8,128)S(1)}, u32[]{:S(2)}, u32[]{:S(2)}) %collective-permute-start.21) | collective-permute-done | bytes 102432 | tf_op jit(solution)/shard_map/ppermute | solution.py:241
  58.1 0.0 collective-permute-start.22
  58.1 1.3 %collective-permute-done.22.refs_3_ = f32[200,128]{1,0:T(8,128)S(1)} collective-permute-done((f32[200,128]{1,0:T(8,128)S(1)}, f32[200,128]{1,0:T(8,128)S(1)}, u32[]{:S(2)}, u32[]{:S(2)}) %collective-permute-start.22) | collective-permute-done | bytes 102432 | tf_op jit(solution)/shard_map/ppermute | solution.py:241
  59.4 0.8 %final.1 = (f32[512,128]{1,0:T(8,128)}, f32[128,256]{1,0:T(8,128)}, f32[1,256]{1,0:T(1,128)}) custom-call(s32[1]{0:T(128)} %bitcast.rep_at.here, f32[200,128]{1,0:T(8,128)S(1)} %add.11.refs_0_, f32[200,128]{1,0:T(8,128)S(1)} %collective-permute-done.20.refs_1_, f32[200,128]{1,0:T(8,128)S(1)} %collective-permute-done.21.refs_2_, ...), custom_call_target="tpu_custom_call" | custom-call | bytes 524288 | tf_op jit(solution)/shard_map/final/pallas_call | solution.py:346
  (16 shorter events, 0.1 us)
Async XLA Ops:
  1.3 19.4 %copy-start = (f32[512,256]{1,0:T(8,128)S(1)}, f32[512,256]{1,0:T(8,128)}, u32[]{:S(2)}) copy-start(f32[512,256]{1,0:T(8,128)} %cotangent.1) | copy-start | bytes 1572868
  1.3 19.4 %copy-start.1 = (f32[128,256]{1,0:T(8,128)S(1)}, f32[128,256]{1,0:T(8,128)}, u32[]{:S(2)}) copy-start(f32[128,256]{1,0:T(8,128)} %weight.2) | copy-start | bytes 393220
  3.1 15.6 %collective-permute-start = (f32[520,128]{1,0:T(8,128)S(1)}, f32[520,128]{1,0:T(8,128)S(1)}, u32[]{:S(2)}, u32[]{:S(2)}) collective-permute-start(f32[520,128]{1,0:T(8,128)S(1)} %get-tuple-element.29), channel_id=1, source_target_pairs={{0,1},{1,0},{2,3},{3,2},{4,5},{5,4},{6,7},{7,6},{8,9},{9,8},{10,11... | collective-permute-start | bytes 798728 | tf_op jit(solution)/shard_map/ppermute | solution.py:241
  3.6 15.5 %collective-permute-start.1 = (f32[520,128]{1,0:T(8,128)S(1)}, f32[520,128]{1,0:T(8,128)S(1)}, u32[]{:S(2)}, u32[]{:S(2)}) collective-permute-start(f32[520,128]{1,0:T(8,128)S(1)} %get-tuple-element.30), channel_id=1, source_target_pairs={{0,2},{1,3},{2,0},{3,1},{4,6},{5,7},{6,4},{7,5},{8,10},{9,11},{10,... | collective-permute-start | bytes 798728 | tf_op jit(solution)/shard_map/ppermute | solution.py:241
  6.2 14.5 %collective-permute-start.2 = (f32[520,128]{1,0:T(8,128)S(1)}, f32[520,128]{1,0:T(8,128)S(1)}, u32[]{:S(2)}, u32[]{:S(2)}) collective-permute-start(f32[520,128]{1,0:T(8,128)S(1)} %get-tuple-element.31), channel_id=1, source_target_pairs={{0,3},{1,2},{2,1},{3,0},{4,7},{5,6},{6,5},{7,4},{8,11},{9,10},{10,... | collective-permute-start | bytes 798728 | tf_op jit(solution)/shard_map/ppermute | solution.py:241
  6.3 6.5 %collective-permute-start.6 = (f32[128,128]{1,0:T(8,128)S(1)}, f32[128,128]{1,0:T(8,128)S(1)}, u32[]{:S(2)}, u32[]{:S(2)}) collective-permute-start(f32[128,128]{1,0:T(8,128)S(1)} %get-tuple-element.34.refs_0_), channel_id=1, source_target_pairs={{0,16},{4,20},{8,24},{12,28},{16,0},{20,4},{24,8},{28,12},{1,17},{... | collective-permute-start | bytes 196616 | tf_op jit(solution)/shard_map/ppermute | solution.py:241
  9.1 4.9 %collective-permute-start.4 = (f32[128,128]{1,0:T(8,128)S(1)}, f32[128,128]{1,0:T(8,128)S(1)}, u32[]{:S(2)}, u32[]{:S(2)}) collective-permute-start(f32[128,128]{1,0:T(8,128)S(1)} %get-tuple-element.34.refs_0_), channel_id=1, source_target_pairs={{0,8},{4,12},{8,0},{12,4},{16,24},{20,28},{24,16},{28,20},{1,9},{5... | collective-permute-start | bytes 196616 | tf_op jit(solution)/shard_map/ppermute | solution.py:241
  12.8 4.3 %collective-permute-start.8 = (f32[128,128]{1,0:T(8,128)S(1)}, f32[128,128]{1,0:T(8,128)S(1)}, u32[]{:S(2)}, u32[]{:S(2)}) collective-permute-start(f32[128,128]{1,0:T(8,128)S(1)} %collective-permute-done.6.refs_4_), channel_id=1, source_target_pairs={{0,8},{4,12},{8,0},{12,4},{16,24},{20,28},{24,16},{28,20},{1,9},{5... | collective-permute-start | bytes 196616 | tf_op jit(solution)/shard_map/ppermute | solution.py:241
  13.9 9.3 %collective-permute-start.3 = (f32[128,128]{1,0:T(8,128)S(1)}, f32[128,128]{1,0:T(8,128)S(1)}, u32[]{:S(2)}, u32[]{:S(2)}) collective-permute-start(f32[128,128]{1,0:T(8,128)S(1)} %get-tuple-element.34.refs_0_), channel_id=1, source_target_pairs={{0,4},{4,0},{8,12},{12,8},{16,20},{20,16},{24,28},{28,24},{1,5},{5... | collective-permute-start | bytes 196616 | tf_op jit(solution)/shard_map/ppermute | solution.py:241
  17.1 6.1 %collective-permute-start.7 = (f32[128,128]{1,0:T(8,128)S(1)}, f32[128,128]{1,0:T(8,128)S(1)}, u32[]{:S(2)}, u32[]{:S(2)}) collective-permute-start(f32[128,128]{1,0:T(8,128)S(1)} %collective-permute-done.6.refs_4_), channel_id=1, source_target_pairs={{0,4},{4,0},{8,12},{12,8},{16,20},{20,16},{24,28},{28,24},{1,5},{5... | collective-permute-start | bytes 196616 | tf_op jit(solution)/shard_map/ppermute | solution.py:241
  18.7 4.5 %collective-permute-start.5 = (f32[128,128]{1,0:T(8,128)S(1)}, f32[128,128]{1,0:T(8,128)S(1)}, u32[]{:S(2)}, u32[]{:S(2)}) collective-permute-start(f32[128,128]{1,0:T(8,128)S(1)} %collective-permute-done.4.refs_2_), channel_id=1, source_target_pairs={{0,4},{4,0},{8,12},{12,8},{16,20},{20,16},{24,28},{28,24},{1,5},{5... | collective-permute-start | bytes 196616 | tf_op jit(solution)/shard_map/ppermute | solution.py:241
  19.1 4.5 %collective-permute-start.9 = (f32[128,128]{1,0:T(8,128)S(1)}, f32[128,128]{1,0:T(8,128)S(1)}, u32[]{:S(2)}, u32[]{:S(2)}) collective-permute-start(f32[128,128]{1,0:T(8,128)S(1)} %collective-permute-done.8.refs_6_), channel_id=1, source_target_pairs={{0,4},{4,0},{8,12},{12,8},{16,20},{20,16},{24,28},{28,24},{1,5},{5... | collective-permute-start | bytes 196616 | tf_op jit(solution)/shard_map/ppermute | solution.py:241
  20.7 0.7 %copy-start.2 = (f32[256]{0:T(256)S(1)}, f32[256]{0:T(256)}, u32[]{:S(2)}) copy-start(f32[256]{0:T(256)} %param.10) | copy-start | bytes 3076
  24.3 1.4 %collective-permute-start.10 = (f32[64,512]{1,0:T(8,128)S(1)}, f32[64,512]{1,0:T(8,128)S(1)}, u32[]{:S(2)}, u32[]{:S(2)}) collective-permute-start(f32[64,512]{1,0:T(8,128)S(1)} %get-tuple-element.36), channel_id=1, source_target_pairs={{0,1},{1,0},{2,3},{3,2},{4,5},{5,4},{6,7},{7,6},{8,9},{9,8},{10,11... | collective-permute-start | bytes 393224 | tf_op jit(solution)/shard_map/ppermute | solution.py:241
  25.8 5.6 %collective-permute-start.11 = (f32[64,512]{1,0:T(8,128)S(1)}, f32[64,512]{1,0:T(8,128)S(1)}, u32[]{:S(2)}, u32[]{:S(2)}) collective-permute-start(f32[64,512]{1,0:T(8,128)S(1)} %add.6.refs_0_), channel_id=1, source_target_pairs={{0,2},{1,3},{2,0},{3,1},{4,6},{5,7},{6,4},{7,5},{8,10},{9,11},{10,... | collective-permute-start | bytes 393224 | tf_op jit(solution)/shard_map/ppermute | solution.py:241
  31.4 1.4 %collective-permute-start.12 = (f32[64,512]{1,0:T(8,128)S(1)}, f32[64,512]{1,0:T(8,128)S(1)}, u32[]{:S(2)}, u32[]{:S(2)}) collective-permute-start(f32[64,512]{1,0:T(8,128)S(1)} %add.7.mine), channel_id=1, source_target_pairs={{0,1},{1,0},{2,3},{3,2},{4,5},{5,4},{6,7},{7,6},{8,9},{9,8},{10,11... | collective-permute-start | bytes 393224 | tf_op jit(solution)/shard_map/ppermute | solution.py:241
  34.4 6.9 %collective-permute-start.14 = (f32[256,128]{1,0:T(8,128)S(1)}, f32[256,128]{1,0:T(8,128)S(1)}, u32[]{:S(2)}, u32[]{:S(2)}) collective-permute-start(f32[256,128]{1,0:T(8,128)S(1)} %get-tuple-element.43), channel_id=1, source_target_pairs={{0,4},{4,0},{8,12},{12,8},{16,20},{20,16},{24,28},{28,24},{1,5},{5... | collective-permute-start | bytes 393224 | tf_op jit(solution)/shard_map/ppermute | solution.py:241
  36.0 5.3 %collective-permute-start.15 = (f32[72,128]{1,0:T(8,128)S(1)}, f32[72,128]{1,0:T(8,128)S(1)}, u32[]{:S(2)}, u32[]{:S(2)}) collective-permute-start(f32[72,128]{1,0:T(8,128)S(1)} %weight.3.refs_1_), channel_id=1, source_target_pairs={{0,16},{4,20},{8,24},{12,28},{16,0},{20,4},{24,8},{28,12},{1,17},{... | collective-permute-start | bytes 110600 | tf_op jit(solution)/shard_map/ppermute | solution.py:241
  38.5 5.0 %collective-permute-start.13 = (f32[256,128]{1,0:T(8,128)S(1)}, f32[256,128]{1,0:T(8,128)S(1)}, u32[]{:S(2)}, u32[]{:S(2)}) collective-permute-start(f32[256,128]{1,0:T(8,128)S(1)} %get-tuple-element.39), channel_id=1, source_target_pairs={{0,4},{4,0},{8,12},{12,8},{16,20},{20,16},{24,28},{28,24},{1,5},{5... | collective-permute-start | bytes 393224 | tf_op jit(solution)/shard_map/ppermute | solution.py:241
  41.3 5.0 %collective-permute-start.16 = (f32[256,128]{1,0:T(8,128)S(1)}, f32[256,128]{1,0:T(8,128)S(1)}, u32[]{:S(2)}, u32[]{:S(2)}) collective-permute-start(f32[256,128]{1,0:T(8,128)S(1)} %get-tuple-element.45), channel_id=1, source_target_pairs={{0,8},{4,12},{8,0},{12,4},{16,24},{20,28},{24,16},{28,20},{1,9},{5... | collective-permute-start | bytes 393224 | tf_op jit(solution)/shard_map/ppermute | solution.py:241
  42.4 4.0 %collective-permute-start.17 = (f32[72,128]{1,0:T(8,128)S(1)}, f32[72,128]{1,0:T(8,128)S(1)}, u32[]{:S(2)}, u32[]{:S(2)}) collective-permute-start(f32[72,128]{1,0:T(8,128)S(1)} %get-tuple-element.44.refs_1_), channel_id=1, source_target_pairs={{0,4},{4,0},{8,12},{12,8},{16,20},{20,16},{24,28},{28,24},{1,5},{5... | collective-permute-start | bytes 110600 | tf_op jit(solution)/shard_map/ppermute | solution.py:241
  46.4 6.9 %collective-permute-start.18 = (f32[128,128]{1,0:T(8,128)S(1)}, f32[128,128]{1,0:T(8,128)S(1)}, u32[]{:S(2)}, u32[]{:S(2)}) collective-permute-start(f32[128,128]{1,0:T(8,128)S(1)} %get-tuple-element.48), channel_id=1, source_target_pairs={{0,16},{4,20},{8,24},{12,28},{16,0},{20,4},{24,8},{28,12},{1,17},{... | collective-permute-start | bytes 196616 | tf_op jit(solution)/shard_map/ppermute | solution.py:241
  49.4 4.0 %collective-permute-start.19 = (f32[72,128]{1,0:T(8,128)S(1)}, f32[72,128]{1,0:T(8,128)S(1)}, u32[]{:S(2)}, u32[]{:S(2)}) collective-permute-start(f32[72,128]{1,0:T(8,128)S(1)} %get-tuple-element.47.refs_1_), channel_id=1, source_target_pairs={{0,8},{4,12},{8,0},{12,4},{16,24},{20,28},{24,16},{28,20},{1,9},{5... | collective-permute-start | bytes 110600 | tf_op jit(solution)/shard_map/ppermute | solution.py:241
  53.3 4.7 %collective-permute-start.21 = (f32[200,128]{1,0:T(8,128)S(1)}, f32[200,128]{1,0:T(8,128)S(1)}, u32[]{:S(2)}, u32[]{:S(2)}) collective-permute-start(f32[200,128]{1,0:T(8,128)S(1)} %add.11.refs_0_), channel_id=1, source_target_pairs={{0,2},{1,3},{2,0},{3,1},{4,6},{5,7},{6,4},{7,5},{8,10},{9,11},{10,... | collective-permute-start | bytes 307208 | tf_op jit(solution)/shard_map/ppermute | solution.py:241
  54.9 3.1 %collective-permute-start.20 = (f32[200,128]{1,0:T(8,128)S(1)}, f32[200,128]{1,0:T(8,128)S(1)}, u32[]{:S(2)}, u32[]{:S(2)}) collective-permute-start(f32[200,128]{1,0:T(8,128)S(1)} %add.11.refs_0_), channel_id=1, source_target_pairs={{0,1},{1,0},{2,3},{3,2},{4,5},{5,4},{6,7},{7,6},{8,9},{9,8},{10,11... | collective-permute-start | bytes 307208 | tf_op jit(solution)/shard_map/ppermute | solution.py:241
  58.1 1.3 %collective-permute-start.22 = (f32[200,128]{1,0:T(8,128)S(1)}, f32[200,128]{1,0:T(8,128)S(1)}, u32[]{:S(2)}, u32[]{:S(2)}) collective-permute-start(f32[200,128]{1,0:T(8,128)S(1)} %collective-permute-done.21.refs_2_), channel_id=1, source_target_pairs={{0,1},{1,0},{2,3},{3,2},{4,5},{5,4},{6,7},{7,6},{8,9},{9,8},{10,11... | collective-permute-start | bytes 307208 | tf_op jit(solution)/shard_map/ppermute | solution.py:241

commit v3 on v2

v3 whole, which is shorter than its diff:
```python
import functools

import jax
import jax.numpy as jnp
from jax import lax
from jax.experimental import pallas as pl
from jax.experimental.pallas import tpu as pltpu
from jax.sharding import PartitionSpec as P


LANES = 128
PAD = 8
F32 = jnp.float32
BF16 = jnp.bfloat16
VMEM = pl.BlockSpec(memory_space=pltpu.VMEM)
SMEM = pl.BlockSpec(memory_space=pltpu.SMEM)
HBM = pl.BlockSpec(memory_space=pltpu.HBM)


def halves(x):
    high = x.astype(BF16).astype(F32)
    return high, x - high


def dot3(a, b, dims=(((1,), (0,)), ((), ()))):
    ah, al = halves(a)
    bh, bl = halves(b)
    ah, al, bh, bl = (v.astype(BF16) for v in (ah, al, bh, bl))
    dot = functools.partial(lax.dot_general, dimension_numbers=dims, preferred_element_type=F32)
    return dot(ah, bh) + dot(ah, bl) + dot(al, bh)


def call(kernel, out_shapes, in_specs, scratch, flops, moved, limit=24, aliases=None):
    return pl.pallas_call(
        kernel,
        input_output_aliases=aliases or {},
        out_shape=[
            jax.ShapeDtypeStruct(*(s if isinstance(s[0], tuple) else (s, F32))) for s in out_shapes
        ],
        in_specs=in_specs,
        out_specs=[VMEM] * len(out_shapes),
        scratch_shapes=scratch,
        compiler_params=pltpu.CompilerParams(vmem_limit_bytes=limit << 20),
        cost_estimate=pl.CostEstimate(flops=flops, bytes_accessed=moved, transcendentals=0),
    )


def join_kernel(*refs):
    at = 0
    for ref in refs[:-1]:
        refs[-1][pl.ds(at, ref.shape[0]), :] = ref[...]
        at += ref.shape[0]


def pack_kernel(reps, loops, blocks, part, rep_at, at_loop, count, features, tiles, rows, cols, *refs):
    own, outs = refs[0], refs[1 : 1 + reps]
    held, turned, row_ids, col_ids, sem = refs[1 + reps :]
    here, loop_at = rep_at[0], at_loop[0]
    slots, side = tiles.shape[0], tiles.shape[1]
    chunks = sem.shape[0] - 2 - blocks
    step = slots // chunks
    small = [
        pltpu.make_async_copy(source, target, sem.at[n])
        for n, (source, target) in enumerate([(rows, row_ids), (cols, col_ids)])
    ]
    large = [
        pltpu.make_async_copy(
            tiles.at[pl.ds(n * step, step)], held.at[pl.ds(n * step, step)], sem.at[2 + n]
        )
        for n in range(chunks)
    ]
    pieces = [
        pltpu.make_async_copy(
            features.at[pl.ds(pl.multiple_of(b * side + here * part, 8), part), :],
            own.at[pl.ds(b * part, part), :],
            sem.at[2 + chunks + b],
        )
        for b in range(blocks)
    ]
    for copy in small + large + pieces:
        copy.start()
    for copy in small:
        copy.wait()
    local_rows = row_ids[...] - loop_at * blocks
    shift = blocks.bit_length() - 1
    away = (col_ids[...] >> shift) ^ loop_at
    low = min(loops, 4) - 1
    other_way = (away & ~low) | ((away & low) >> 1) | jnp.where(away & 1 == 1, (low + 1) // 2, 0)
    for d in range(reps):
        second = ((here ^ d) & 1) * jnp.ones_like(away)
        order = jnp.where(second == 1, away, other_way)
        column = (order << shift) | (col_ids[...] & (blocks - 1))
        meta = jnp.concatenate([local_rows, column], axis=0).astype(F32)
        outs[d][pl.ds(slots * part, 2), pl.ds(0, slots)] = meta
    alive = count[0]
    for n in range(chunks):
        large[n].wait()
        for s in range(n * step, (n + 1) * step):
            turned[s] = jnp.where(s < alive, held[s].T, jnp.zeros((side, side), F32))
            for d in range(reps):
                start = pl.multiple_of((here ^ d) * part, 8)
                outs[d][pl.ds(s * part, part), :] = turned[s, pl.ds(start, part), :]
    for copy in pieces:
        copy.wait()


def place_parts(blocks, part, slots, tiles, dense, place_vector, place, sem, clear):
    side = dense.shape[1] // blocks
    for d, tile in enumerate(tiles):
        place_vector[d] = tile[pl.ds(slots * part, PAD), :].astype(jnp.int32)
    copy = pltpu.make_async_copy(place_vector, place, sem)
    copy.start()
    if clear:
        dense[...] = jnp.zeros_like(dense)
    copy.wait()
    for d, tile in enumerate(tiles):
        for s in range(slots):
            lane = pl.ds(pl.multiple_of(place[d, 0, s] * side, LANES), side)
            at = pl.ds(pl.multiple_of(place[d, 1, s] * part, 8), part)
            dense[at, lane] = dense[at, lane] + tile[pl.ds(s * part, part), :]


def near_kernel(blocks, part, slots, *refs):
    place_parts(blocks, part, slots, refs[:-4], refs[-4], *refs[-3:], True)


def far_kernel(blocks, part, slots, count, *refs):
    tiles = refs[1 : 1 + count]
    dense, high_out, low_out = refs[-6:-3]
    place_parts(blocks, part, slots, tiles, dense, *refs[-3:], False)
    side = dense.shape[1] // blocks
    for k in range(dense.shape[0] // side):
        at = pl.ds(k * side, side)
        high, low = halves(dense[at, :])
        high_out[at, :] = high.astype(BF16)
        low_out[at, :] = low.astype(BF16)


def forward_kernel(orders, here, high, low, *refs):
    feats = refs[: len(orders)]
    send, keep, left, acc = refs[len(orders) :]
    width = left.shape[0] // 2
    for order, feat in zip(orders, feats):
        rows = feat.shape[0] // len(order)
        for n, k in enumerate(order):
            at = pl.ds(k * rows, rows)
            upper, lower = halves(feat[pl.ds(n * rows, rows), :].T)
            left[:width, at] = upper.astype(BF16)
            left[width:, at] = lower.astype(BF16)
    both = jnp.dot(left[...], high[...], preferred_element_type=F32)
    rest = jnp.dot(left[:width, :], low[...], preferred_element_type=F32)
    acc[...] = both[:width, :] + both[width:, :] + rest
    half = acc.shape[0] // 2
    core = here[0] & 1
    keep[...] = acc[pl.ds(pl.multiple_of(core * half, 8), half), :]
    send[...] = acc[pl.ds(pl.multiple_of((1 - core) * half, 8), half), :]


def times(high, low, right, width):
    both = jnp.dot(high, right, preferred_element_type=F32)
    rest = jnp.dot(low, right[:, :width], preferred_element_type=F32)
    return both[:, :width] + both[:, width:] + rest


def products(group, size, high, low, right, out):
    for n, k in enumerate(group):
        at = pl.ds(k * size, size)
        value = times(high[at, :], low[at, :], right[...], right.shape[1] // 2)
        out[pl.ds(n * size, size), :] = value


def dense_kernel(
    blocks, group, size, here, high, low, mine, other, weight, bias, cotangent, *refs
):
    out, output, grads, piece_t, right, agg = refs
    width, total = agg.shape
    half, side = width // 2, total // blocks
    core = here[0] & 1
    agg[pl.ds(pl.multiple_of(core * half, 8), half), :] = mine[...]
    agg[pl.ds(pl.multiple_of((1 - core) * half, 8), half), :] = other[...]
    w = weight[...]
    for b in range(blocks):
        at = pl.ds(b * side, side)
        pre = dot3(agg[:, at].T, w) + bias[...]
        gate = jax.nn.sigmoid(pre)
        output[at, :] = pre * gate
        gradient = cotangent[at, :] * gate * (1.0 + pre * (1.0 - gate))
        grads[at, :] = gradient
        spread = dot3(gradient, w, (((1,), (1,)), ((), ())))
        upper, lower = halves(spread)
        right[at, :width] = upper.astype(BF16)
        right[at, width:] = lower.astype(BF16)
    products(group, size, high, low, right, out)
    piece = piece_t.shape[0]
    piece_t[...] = agg[pl.ds(pl.multiple_of(here[0] * piece, 8), piece), :]


def rest_kernel(groups, size, high, low, right, *outs):
    for group, out in zip(groups, outs):
        products(group, size, high, low, right, out)


def weight_kernel(piece_t, grads, out):
    piece, parts = piece_t.shape[0], grads.shape[1] // LANES
    g = grads[...]
    grad_weight = dot3(piece_t[...], g)
    grad_bias = jnp.sum(g, axis=0, keepdims=True)
    for q in range(parts):
        out[pl.ds(q * piece, piece), :] = grad_weight[:, q * LANES : (q + 1) * LANES]
    tail = [grad_bias[:, q * LANES : (q + 1) * LANES] for q in range(parts)]
    tail.append(jnp.zeros((PAD - parts, LANES), F32))
    out[pl.ds(parts * piece, PAD), :] = jnp.concatenate(tail, axis=0)


def add_kernel(cuts, count, *refs):
    mine, theirs, outs = refs[:count], refs[count : 2 * count], refs[2 * count :]
    for cut, out in zip(cuts, outs):
        to = 0
        for pair, first, second, rows in cut:
            left, right = pl.ds(first, rows), pl.ds(second, rows)
            out[pl.ds(to, rows), :] = mine[pair][left, :] + theirs[pair][right, :]
            to += rows


def add(mine, theirs, cuts=None):
    cuts = cuts or [[(n, 0, 0, x.shape[0])] for n, x in enumerate(mine)]
    total = sum(x.size for x in mine)
    return call(
        functools.partial(add_kernel, cuts, len(mine)),
        [(sum(cut[-1] for cut in cuts_of), mine[0].shape[1]) for cuts_of in cuts],
        [VMEM] * (2 * len(mine)),
        [],
        total,
        12 * total,
    )(*mine, *theirs)


def final_kernel(reps, blocks, part, piece, here, *refs):
    parts = refs[:reps]
    grad_features, grad_weight, grad_bias = refs[reps:]
    side = grad_features.shape[0] // blocks
    groups = grad_weight.shape[1] // LANES
    base = blocks * part
    for d in range(reps):
        q = here[0] ^ d
        for b in range(blocks):
            at = pl.ds(pl.multiple_of(b * side + q * part, 8), part)
            grad_features[at, :] = parts[d][pl.ds(b * part, part), :]
        at = pl.ds(pl.multiple_of(q * piece, 8), piece)
        for g in range(groups):
            grad_weight[at, pl.ds(g * LANES, LANES)] = parts[d][pl.ds(base + g * piece, piece), :]
    for g in range(groups):
        row = parts[0][pl.ds(base + groups * piece + g, 1), :]
        grad_bias[:, pl.ds(g * LANES, LANES)] = row


def per_device(features, weight, bias, tile_values, tile_rows, tile_cols, tile_count, cotangent):
    loops, reps = lax.axis_size("loop"), lax.axis_size("rep")
    slots, side = tile_values.shape[0], tile_values.shape[1]
    total, width = features.shape
    wide = weight.shape[1]
    blocks = total // side
    part, piece = side // reps, width // reps
    size, depth = blocks * part, loops * blocks * part
    extra = wide // LANES * piece + PAD
    here = lax.axis_index("rep").astype(jnp.int32).reshape(1)
    loop_at = lax.axis_index("loop").astype(jnp.int32).reshape(1)
    bias = bias.reshape(1, wide)

    def swap(x, axis, bit):
        pairs, low = [], min(loops, 4)
        for a in range(loops):
            for b in range(reps):
                turn = axis == "loop" and bit < low and not b & 1
                over = (2 * bit if 2 * bit < low else 1) if turn else bit
                to = (a ^ over, b) if axis == "loop" else (a, b ^ bit)
                pairs.append((a * reps + b, to[0] * reps + to[1]))
        return lax.ppermute(x, ("loop", "rep"), pairs)

    def join(*arrays):
        shape = (sum(x.shape[0] for x in arrays), arrays[0].shape[1])
        return call(
            join_kernel, [shape], [VMEM] * len(arrays), [], 0, 8 * shape[0] * shape[1]
        )(*arrays)[0]

    chunks = 4 if slots % 4 == 0 else 1
    sources = (features, tile_values, tile_rows[None], tile_cols[None])
    own, *parcels = call(
        functools.partial(pack_kernel, reps, loops, blocks, part),
        [(size, width)] + [(slots * part + PAD, side)] * reps,
        [SMEM] * 3 + [HBM] * 4,
        [
            pltpu.VMEM((slots, side, side), F32),
            pltpu.VMEM((slots, side, side), F32),
            pltpu.VMEM((1, slots), jnp.int32),
            pltpu.VMEM((1, slots), jnp.int32),
            pltpu.SemaphoreType.DMA((2 + chunks + blocks,)),
        ],
        0,
        2 * tile_values.size * 4,
    )(here, loop_at, tile_count, *[pltpu.with_memory_space_constraint(x, pltpu.HBM) for x in sources])
    tiles = [parcels[0]] + [swap(parcels[d], "rep", d) for d in range(1, reps)]

    bit = loops // 2
    feats, orders = [own, swap(own, "loop", bit)], [[0], [bit]]
    bit //= 2
    while bit > 1:
        feats, order = [join(*feats)], sum(orders, [])
        feats.append(swap(feats[0], "loop", bit))
        orders = [order, [k | bit for k in order]]
        bit //= 2
    feats += [swap(x, "loop", 1) for x in feats]
    orders += [[k | 1 for k in order] for order in orders]

    def scratch(count):
        return [
            pltpu.VMEM((count, PAD, LANES), jnp.int32),
            pltpu.SMEM((count, PAD, LANES), jnp.int32),
            pltpu.SemaphoreType.DMA,
        ]

    (dense,) = call(
        functools.partial(near_kernel, blocks, part, slots),
        [(depth, total)],
        [VMEM] * 2,
        scratch(2),
        0,
        4 << 20,
    )(*tiles[:2])
    _, high, low = call(
        functools.partial(far_kernel, blocks, part, slots, reps - 2),
        [(depth, total)] + [((depth, total), BF16)] * 2,
        [VMEM] * (reps + 2),
        scratch(reps - 2),
        0,
        8 << 20,
        aliases={0: 0},
    )(dense, *tiles[2:], weight, bias, cotangent)

    send, keep = call(
        functools.partial(forward_kernel, orders),
        [(width // 2, total)] * 2,
        [SMEM] + [VMEM] * (2 + len(feats)),
        [pltpu.VMEM((2 * width, depth), BF16), pltpu.VMEM((width, total), F32)],
        2 * depth * total * width * 3,
        4 << 20,
    )(here, high, low, *feats)
    (mine,) = add([keep], [swap(send, "rep", 1)])
    bit = 2
    while bit < reps:
        (mine,) = add([mine], [swap(mine, "rep", bit)])
        bit *= 2
    other = swap(mine, "rep", 1)

    even = range(0, loops, 2)
    on, stay = [k for k in even if k & 2], [k for k in even if not k & 2]
    groups = [[k | 1 for k in on], [k | 1 for k in stay], on, stay]
    first, output, grads, piece_t, right = call(
        functools.partial(dense_kernel, blocks, groups[0], size),
        [(len(on) * size, width)]
        + [(total, wide)] * 2
        + [(piece, total), ((total, 2 * width), BF16)],
        [SMEM] + [VMEM] * 7,
        [pltpu.VMEM((width, total), F32)],
        2 * depth * total * width,
        4 << 20,
    )(here, high, low, mine, other, weight, bias, cotangent)
    on_term = swap(first, "loop", 1)
    sent, on_own, stay_own = call(
        functools.partial(rest_kernel, groups[1:], size),
        [(len(g) * size, width) for g in groups[1:]],
        [VMEM] * 3,
        [],
        2 * depth * total * width * 2,
        3 << 20,
    )(high, low, right)
    stay_term = swap(sent, "loop", 1)
    (grad,) = call(
        weight_kernel, [(extra, LANES)], [VMEM] * 2, [], 2 * piece * total * wide * 3, 1 << 20
    )(piece_t, grads)

    grad_term = swap(grad, "loop", loops // 2)
    (going,) = add([on_own], [on_term])
    term = swap(going, "loop", 2)
    (grad,) = add([grad], [grad_term])
    grad_term = swap(grad, "loop", 1)
    (held,) = add([stay_own], [stay_term])
    bit, rest = 2, stay
    while bit < loops // 2:
        ahead = [(0, n * size, n * size, size) for n, k in enumerate(rest) if k & (2 * bit)]
        behind = [(0, n * size, n * size, size) for n, k in enumerate(rest) if not k & (2 * bit)]
        rest = [k for k in rest if not k & (2 * bit)]
        going, held = add([held], [term], [ahead, behind])
        term = swap(going, "loop", 2 * bit)
        (grad,) = add([grad], [grad_term])
        grad_term = swap(grad, "loop", bit)
        bit *= 2
    (both,) = add([held, grad], [term, grad_term], [[(0, 0, 0, size), (1, 0, 0, extra)]])

    parts = {0: both}
    bit = reps // 2
    while bit:
        for k in list(parts):
            parts[k | bit] = swap(parts[k], "rep", bit)
        bit //= 2
    output = join(output)
    grad_features, grad_weight, grad_bias = call(
        functools.partial(final_kernel, reps, blocks, part, piece),
        [(total, width), (width, wide), (1, wide)],
        [SMEM] + [VMEM] * reps,
        [],
        0,
        2 * total * width * 4,
    )(here, *[parts[d] for d in range(reps)])
    return (output, grad_features, grad_weight, grad_bias.reshape(wide))


def solution(mesh):
    return jax.shard_map(
        per_device,
        mesh=mesh,
        in_specs=(
            P("loop", None),
            P(),
            P(),
            P(("loop", "rep"), None, None),
            P(("loop", "rep")),
            P(("loop", "rep")),
            P(("loop", "rep")),
            P("loop", None),
        ),
        out_specs=(P("loop", None), P("loop", None), P(), P()),
        check_vma=False,
    )
```

time: 60.3 us -> 60.7 us (level)
  starting transfers between devices: 27.7 us -> 19.3 us
  waiting for transfers between devices: 23.4 us -> 31.4 us
  Pallas kernels: 6.91 us -> 8.46 us
  local copies, waits for them, and re-layouts: 0.68 us -> 0.01 us
    ppermute x23 -> x20, starting transfers between devices: 27.7 us -> 19.3 us  [swap(): return lax.ppermute(x, ('loop', 'rep'), pairs)]
    ppermute x23 -> x20, waiting for transfers between devices: 23.4 us -> 31.4 us  [swap(): return lax.ppermute(x, ('loop', 'rep'), pairs)]
    pallas_call x10 -> x16, Pallas kernels: 5.9 us -> 7.45 us  [the longest x1 1.75 us: per_device(): call(functools.partial(pack_kernel, reps, loops, blocks, part), [(size, w...]
    unnamed x6, local copies, waits for them, and re-layouts: 0.68 us -> 0.01 us
  transfers between devices with their start and end apart: 23 -> 20, of which waited for: 12 -> 12; matrix products, arithmetic and copies ran while one was open for 0% -> 0% of each run, Pallas kernels for 3% -> 7%
where the time goes in v3:
time: 60.7 us; the launch traced here: 60.5 us
  waiting for transfers between devices  31.4 us (52%)
  starting transfers between devices  19.3 us (32%)
  Pallas kernels  8.46 us (14%)
  between operations  1.45 us (2%)
    ppermute x20, waiting for transfers between devices, swap(): return lax.ppermute(x, ('loop', 'rep'), pairs)  31.4 us
    ppermute x20, starting transfers between devices, swap(): return lax.ppermute(x, ('loop', 'rep'), pairs)  19.3 us
    pallas_call x1, Pallas kernels, per_device(): call(functools.partial(pack_kernel, reps, loops, blocks, part), [(size, w...  1.75 us
    pallas_call x1, Pallas kernels, per_device(): call(functools.partial(far_kernel, blocks, part, slots, reps - 2), [(dept...  1.33 us
  transfers between devices with their start and end apart: 20, of which 12 were waited for; matrix products, arithmetic and copies ran while one was open for 0% of the time, Pallas kernels for 7%

profile of v3, /device:TPU:0, one launch (start us, length us, event | category | flops | bytes accessed | tf_op | source)
XLA Modules:
  0.0 60.5 jit_solution(4786093043194290633)
XLA Ops:
  1.3 1.7 %shard_map.111 = (f32[128,128]{1,0:T(8,128)S(1)}, f32[520,128]{1,0:T(8,128)S(1)}, f32[520,128]{1,0:T(8,128)S(1)}, f32[520,128]{1,0:T(8,128)S(1)}, f32[520,128]{1,0:T(8,128)S(1)}) custom-call(s32[1]{0:T(128)} %bitcast.rep_at.here, s32[1]{0:T(128)} %bitcast.1.at_loop, s32[1]{0:T(128)S(6)} %copy.14.count, f32[512,128]{1,0:T(8,128)} %features.1, ...), custom_call_target="tpu_custom_call" | custom-call | bytes 2097152 | tf_op jit(solution)/shard_map/pallas_call | solution.py:288
  3.1 4.1 %collective-permute-start.3 = (f32[128,128]{1,0:T(8,128)S(1)}, f32[128,128]{1,0:T(8,128)S(1)}, u32[]{:S(2)}, u32[]{:S(2)}) collective-permute-start(f32[128,128]{1,0:T(8,128)S(1)} %get-tuple-element.32.refs_0_), channel_id=1, source_target_pairs={{0,16},{1,17},{2,18},{3,19},{4,20},{5,21},{6,22},{7,23},{8,24},{9,... | collective-permute-start | bytes 196616 | tf_op jit(solution)/shard_map/ppermute | solution.py:278
  7.2 0.0 collective-permute-start
  7.2 1.5 %collective-permute-start.1 = (f32[520,128]{1,0:T(8,128)S(1)}, f32[520,128]{1,0:T(8,128)S(1)}, u32[]{:S(2)}, u32[]{:S(2)}) collective-permute-start(f32[520,128]{1,0:T(8,128)S(1)} %get-tuple-element.28), channel_id=1, source_target_pairs={{0,2},{1,3},{2,0},{3,1},{4,6},{5,7},{6,4},{7,5},{8,10},{9,11},{10,... | collective-permute-start | bytes 798728 | tf_op jit(solution)/shard_map/ppermute | solution.py:278
  8.7 0.3 collective-permute-start.2
  9.1 1.8 %collective-permute-done.3.refs_1_ = f32[128,128]{1,0:T(8,128)S(1)} collective-permute-done((f32[128,128]{1,0:T(8,128)S(1)}, f32[128,128]{1,0:T(8,128)S(1)}, u32[]{:S(2)}, u32[]{:S(2)}) %collective-permute-start.3) | collective-permute-done | bytes 65568 | tf_op jit(solution)/shard_map/ppermute | solution.py:278
  10.9 1.8 %collective-permute-start.4 = (f32[256,128]{1,0:T(8,128)S(1)}, f32[256,128]{1,0:T(8,128)S(1)}, u32[]{:S(2)}, u32[]{:S(2)}) collective-permute-start(f32[256,128]{1,0:T(8,128)S(1)} %shard_map.114.refs_0_), channel_id=1, source_target_pairs={{0,4},{1,9},{2,6},{3,11},{4,0},{5,13},{6,2},{7,15},{8,12},{9,1},{1... | collective-permute-start | bytes 393224 | tf_op jit(solution)/shard_map/ppermute | solution.py:278
  12.6 0.4 collective-permute-start.5
  13.0 3.2 %collective-permute-done.4.refs_1_ = f32[256,128]{1,0:T(8,128)S(1)} collective-permute-done((f32[256,128]{1,0:T(8,128)S(1)}, f32[256,128]{1,0:T(8,128)S(1)}, u32[]{:S(2)}, u32[]{:S(2)}) %collective-permute-start.4) | collective-permute-done | bytes 131104 | tf_op jit(solution)/shard_map/ppermute | solution.py:278
  16.2 0.4 collective-permute-start.6
  16.6 0.0 collective-permute-done.refs_1_
  16.6 1.0 %shard_map.112.refs_0_ = f32[1024,512]{1,0:T(8,128)S(1)} custom-call(f32[520,128]{1,0:T(8,128)S(1)} %get-tuple-element.26.refs_0_, f32[520,128]{1,0:T(8,128)S(1)} %collective-permute-done.refs_1_), custom_call_target="tpu_custom_call" | custom-call | bytes 4194304 | tf_op jit(solution)/shard_map/pallas_call | solution.py:322
  17.6 0.0 collective-permute-done.1.refs_1_
  17.6 3.6 %collective-permute-done.2.refs_2_ = f32[520,128]{1,0:T(8,128)S(1)} collective-permute-done((f32[520,128]{1,0:T(8,128)S(1)}, f32[520,128]{1,0:T(8,128)S(1)}, u32[]{:S(2)}, u32[]{:S(2)}) %collective-permute-start.2) | collective-permute-done | bytes 266272 | tf_op jit(solution)/shard_map/ppermute | solution.py:278
  21.3 1.3 %shard_map.113 = (f32[1024,512]{1,0:T(8,128)S(1)}, bf16[1024,512]{1,0:T(8,128)(2,1)S(1)}, bf16[1024,512]{1,0:T(8,128)(2,1)S(1)}) custom-call(f32[1024,512]{1,0:T(8,128)S(1)} %shard_map.112.refs_0_, f32[520,128]{1,0:T(8,128)S(1)} %collective-permute-done.1.refs_1_, f32[520,128]{1,0:T(8,128)S(1)} %collective-permute-done.2.refs_2_, ...), custom_call_target="tpu_custom_call", output_to_operand_aliasing={{0}: (0, {})} | custom-call | bytes 8388608 | tf_op jit(solution)/shard_map/pallas_call | solution.py:330
  22.6 0.0 collective-permute-done.6.refs_3_
  22.6 0.7 %shard_map.115 = (f32[64,512]{1,0:T(8,128)S(1)}, f32[64,512]{1,0:T(8,128)S(1)}) custom-call(s32[1]{0:T(128)} %bitcast.rep_at.here, bf16[1024,512]{1,0:T(8,128)(2,1)S(1)} %get-tuple-element.30.high, bf16[1024,512]{1,0:T(8,128)(2,1)S(1)} %get-tuple-element.31.low, f32[256,128]{1,0:T(8,128)S(1)} %shard_map.114.refs_0_, ...), custom_call_target="tpu_custom_call" | custom-call | flops 402653184 | bytes 4194304 | tf_op jit(solution)/shard_map/pallas_call | solution.py:340
  23.3 0.4 collective-permute-start.7
  23.7 1.1 %collective-permute-done.7.refs_1_ = f32[64,512]{1,0:T(8,128)S(1)} collective-permute-done((f32[64,512]{1,0:T(8,128)S(1)}, f32[64,512]{1,0:T(8,128)S(1)}, u32[]{:S(2)}, u32[]{:S(2)}) %collective-permute-start.7) | collective-permute-done | bytes 131104 | tf_op jit(solution)/shard_map/ppermute | solution.py:278
  24.8 1.6 %collective-permute-start.8 = (f32[64,512]{1,0:T(8,128)S(1)}, f32[64,512]{1,0:T(8,128)S(1)}, u32[]{:S(2)}, u32[]{:S(2)}) collective-permute-start(f32[64,512]{1,0:T(8,128)S(1)} %shard_map.116.refs_0_), channel_id=1, source_target_pairs={{0,2},{1,3},{2,0},{3,1},{4,6},{5,7},{6,4},{7,5},{8,10},{9,11},{10,... | collective-permute-start | bytes 393224 | tf_op jit(solution)/shard_map/ppermute | solution.py:278
  26.4 4.2 %collective-permute-done.8.refs_1_ = f32[64,512]{1,0:T(8,128)S(1)} collective-permute-done((f32[64,512]{1,0:T(8,128)S(1)}, f32[64,512]{1,0:T(8,128)S(1)}, u32[]{:S(2)}, u32[]{:S(2)}) %collective-permute-start.8) | collective-permute-done | bytes 131104 | tf_op jit(solution)/shard_map/ppermute | solution.py:278
  30.5 0.1 collective-permute-start.9
  30.6 1.3 %collective-permute-done.9.other = f32[64,512]{1,0:T(8,128)S(1)} collective-permute-done((f32[64,512]{1,0:T(8,128)S(1)}, f32[64,512]{1,0:T(8,128)S(1)}, u32[]{:S(2)}, u32[]{:S(2)}) %collective-permute-start.9) | collective-permute-done | bytes 131104 | tf_op jit(solution)/shard_map/ppermute | solution.py:278
  31.9 1.1 %shard_map.118 = (f32[256,128]{1,0:T(8,128)S(1)}, f32[512,256]{1,0:T(8,128)S(1)}, f32[512,256]{1,0:T(8,128)S(1)}, f32[32,512]{1,0:T(8,128)S(1)}, bf16[512,256]{1,0:T(8,128)(2,1)S(1)}) custom-call(s32[1]{0:T(128)} %bitcast.rep_at.here, bf16[1024,512]{1,0:T(8,128)(2,1)S(1)} %get-tuple-element.30.high, bf16[1024,512]{1,0:T(8,128)(2,1)S(1)} %get-tuple-element.31.low, ...), custom_call_target="tpu_custom_call" | custom-call | flops 134217728 | bytes 4194304 | tf_op jit(solution)/shard_map/pallas_call | solution.py:358
  33.1 1.6 %collective-permute-start.11 = (f32[256,128]{1,0:T(8,128)S(1)}, f32[256,128]{1,0:T(8,128)S(1)}, u32[]{:S(2)}, u32[]{:S(2)}) collective-permute-start(f32[256,128]{1,0:T(8,128)S(1)} %get-tuple-element.40), channel_id=1, source_target_pairs={{0,8},{1,5},{2,10},{3,7},{4,12},{5,1},{6,14},{7,3},{8,0},{9,13},{1... | collective-permute-start | bytes 393224 | tf_op jit(solution)/shard_map/ppermute | solution.py:278
  34.7 0.6 shard_map.120
  35.3 0.5 collective-permute-start.10
  35.8 2.3 %collective-permute-done.11.refs_1_ = f32[256,128]{1,0:T(8,128)S(1)} collective-permute-done((f32[256,128]{1,0:T(8,128)S(1)}, f32[256,128]{1,0:T(8,128)S(1)}, u32[]{:S(2)}, u32[]{:S(2)}) %collective-permute-start.11) | collective-permute-done | bytes 131104 | tf_op jit(solution)/shard_map/ppermute | solution.py:278
  38.2 1.6 %collective-permute-start.12 = (f32[256,128]{1,0:T(8,128)S(1)}, f32[256,128]{1,0:T(8,128)S(1)}, u32[]{:S(2)}, u32[]{:S(2)}) collective-permute-start(f32[256,128]{1,0:T(8,128)S(1)} %shard_map.122), channel_id=1, source_target_pairs={{0,4},{1,9},{2,6},{3,11},{4,0},{5,13},{6,2},{7,15},{8,12},{9,1},{1... | collective-permute-start | bytes 393224 | tf_op jit(solution)/shard_map/ppermute | solution.py:278
  39.7 0.2 shard_map.124.refs_0_
  39.9 0.7 %collective-permute-start.13 = (f32[72,128]{1,0:T(8,128)S(1)}, f32[72,128]{1,0:T(8,128)S(1)}, u32[]{:S(2)}, u32[]{:S(2)}) collective-permute-start(f32[72,128]{1,0:T(8,128)S(1)} %shard_map.124.refs_0_), channel_id=1, source_target_pairs={{0,16},{1,17},{2,18},{3,19},{4,20},{5,21},{6,22},{7,23},{8,24},{9,... | collective-permute-start | bytes 110600 | tf_op jit(solution)/shard_map/ppermute | solution.py:278
  40.6 4.2 %collective-permute-done.13.refs_1_ = f32[72,128]{1,0:T(8,128)S(1)} collective-permute-done((f32[72,128]{1,0:T(8,128)S(1)}, f32[72,128]{1,0:T(8,128)S(1)}, u32[]{:S(2)}, u32[]{:S(2)}) %collective-permute-start.13) | collective-permute-done | bytes 36896 | tf_op jit(solution)/shard_map/ppermute | solution.py:278
  44.9 1.6 %collective-permute-start.14 = (f32[72,128]{1,0:T(8,128)S(1)}, f32[72,128]{1,0:T(8,128)S(1)}, u32[]{:S(2)}, u32[]{:S(2)}) collective-permute-start(f32[72,128]{1,0:T(8,128)S(1)} %shard_map.125.refs_0_), channel_id=1, source_target_pairs={{0,8},{1,5},{2,10},{3,7},{4,12},{5,1},{6,14},{7,3},{8,0},{9,13},{1... | collective-permute-start | bytes 110600 | tf_op jit(solution)/shard_map/ppermute | solution.py:278
  46.5 0.0 collective-permute-done.10.refs_1_
  46.5 0.0 collective-permute-done.12.refs_1_
  46.5 1.0 %collective-permute-start.15 = (f32[128,128]{1,0:T(8,128)S(1)}, f32[128,128]{1,0:T(8,128)S(1)}, u32[]{:S(2)}, u32[]{:S(2)}) collective-permute-start(f32[128,128]{1,0:T(8,128)S(1)} %get-tuple-element.44), channel_id=1, source_target_pairs={{0,16},{1,17},{2,18},{3,19},{4,20},{5,21},{6,22},{7,23},{8,24},{9,... | collective-permute-start | bytes 196616 | tf_op jit(solution)/shard_map/ppermute | solution.py:278
  47.5 2.3 %collective-permute-done.14.refs_1_ = f32[72,128]{1,0:T(8,128)S(1)} collective-permute-done((f32[72,128]{1,0:T(8,128)S(1)}, f32[72,128]{1,0:T(8,128)S(1)}, u32[]{:S(2)}, u32[]{:S(2)}) %collective-permute-start.14) | collective-permute-done | bytes 36896 | tf_op jit(solution)/shard_map/ppermute | solution.py:278
  49.8 0.2 collective-permute-start.16
  49.9 3.8 %collective-permute-done.16.refs_3_ = f32[72,128]{1,0:T(8,128)S(1)} collective-permute-done((f32[72,128]{1,0:T(8,128)S(1)}, f32[72,128]{1,0:T(8,128)S(1)}, u32[]{:S(2)}, u32[]{:S(2)}) %collective-permute-start.16) | collective-permute-done | bytes 36896 | tf_op jit(solution)/shard_map/ppermute | solution.py:278
  53.7 0.0 collective-permute-done.15.refs_2_
  53.7 1.6 %collective-permute-start.18 = (f32[200,128]{1,0:T(8,128)S(1)}, f32[200,128]{1,0:T(8,128)S(1)}, u32[]{:S(2)}, u32[]{:S(2)}) collective-permute-start(f32[200,128]{1,0:T(8,128)S(1)} %shard_map.127.refs_0_), channel_id=1, source_target_pairs={{0,2},{1,3},{2,0},{3,1},{4,6},{5,7},{6,4},{7,5},{8,10},{9,11},{10,... | collective-permute-start | bytes 307208 | tf_op jit(solution)/shard_map/ppermute | solution.py:278
  55.3 0.0 collective-permute-start.17
  55.3 3.1 %collective-permute-done.18.refs_2_ = f32[200,128]{1,0:T(8,128)S(1)} collective-permute-done((f32[200,128]{1,0:T(8,128)S(1)}, f32[200,128]{1,0:T(8,128)S(1)}, u32[]{:S(2)}, u32[]{:S(2)}) %collective-permute-start.18) | collective-permute-done | bytes 102432 | tf_op jit(solution)/shard_map/ppermute | solution.py:278
  58.5 0.0 collective-permute-start.19
  58.5 0.8 %shard_map.119 = f32[512,256]{1,0:T(8,128)} custom-call(f32[512,256]{1,0:T(8,128)S(1)} %get-tuple-element.35.refs_0_), custom_call_target="tpu_custom_call" | custom-call | bytes 1048576 | tf_op jit(solution)/shard_map/pallas_call | solution.py:282
  59.3 0.0 collective-permute-done.17.refs_1_
  59.3 0.5 collective-permute-done.19.refs_3_
  59.8 0.8 %shard_map.128 = (f32[512,128]{1,0:T(8,128)}, f32[128,256]{1,0:T(8,128)}, f32[1,256]{1,0:T(1,128)}) custom-call(s32[1]{0:T(128)} %bitcast.rep_at.here, f32[200,128]{1,0:T(8,128)S(1)} %shard_map.127.refs_0_, f32[200,128]{1,0:T(8,128)S(1)} %collective-permute-done.17.refs_1_, f32[200,128]{1,0:T(8,128)S(1)} %collective-permute-done.18.refs_2_, ...), custom_call_target="tpu_custom_call" | custom-call | bytes 524288 | tf_op jit(solution)/shard_map/pallas_call | solution.py:407
  (16 shorter events, 0.1 us)
Async XLA Ops:
  1.3 20.0 %copy-start = (f32[512,256]{1,0:T(8,128)S(1)}, f32[512,256]{1,0:T(8,128)}, u32[]{:S(2)}) copy-start(f32[512,256]{1,0:T(8,128)} %cotangent.1) | copy-start | bytes 1572868
  1.3 20.0 %copy-start.1 = (f32[128,256]{1,0:T(8,128)S(1)}, f32[128,256]{1,0:T(8,128)}, u32[]{:S(2)}) copy-start(f32[128,256]{1,0:T(8,128)} %weight.1) | copy-start | bytes 393220
  1.3 20.0 %copy-start.2 = (f32[256]{0:T(256)S(1)}, f32[256]{0:T(256)}, u32[]{:S(2)}) copy-start(f32[256]{0:T(256)} %param.10) | copy-start | bytes 3076
  3.1 7.8 %collective-permute-start.3 = (f32[128,128]{1,0:T(8,128)S(1)}, f32[128,128]{1,0:T(8,128)S(1)}, u32[]{:S(2)}, u32[]{:S(2)}) collective-permute-start(f32[128,128]{1,0:T(8,128)S(1)} %get-tuple-element.32.refs_0_), channel_id=1, source_target_pairs={{0,16},{1,17},{2,18},{3,19},{4,20},{5,21},{6,22},{7,23},{8,24},{9,... | collective-permute-start | bytes 196616 | tf_op jit(solution)/shard_map/ppermute | solution.py:278
  7.2 9.4 %collective-permute-start = (f32[520,128]{1,0:T(8,128)S(1)}, f32[520,128]{1,0:T(8,128)S(1)}, u32[]{:S(2)}, u32[]{:S(2)}) collective-permute-start(f32[520,128]{1,0:T(8,128)S(1)} %get-tuple-element.27), channel_id=1, source_target_pairs={{0,1},{1,0},{2,3},{3,2},{4,5},{5,4},{6,7},{7,6},{8,9},{9,8},{10,11... | collective-permute-start | bytes 798728 | tf_op jit(solution)/shard_map/ppermute | solution.py:278
  7.2 10.4 %collective-permute-start.1 = (f32[520,128]{1,0:T(8,128)S(1)}, f32[520,128]{1,0:T(8,128)S(1)}, u32[]{:S(2)}, u32[]{:S(2)}) collective-permute-start(f32[520,128]{1,0:T(8,128)S(1)} %get-tuple-element.28), channel_id=1, source_target_pairs={{0,2},{1,3},{2,0},{3,1},{4,6},{5,7},{6,4},{7,5},{8,10},{9,11},{10,... | collective-permute-start | bytes 798728 | tf_op jit(solution)/shard_map/ppermute | solution.py:278
  8.7 12.5 %collective-permute-start.2 = (f32[520,128]{1,0:T(8,128)S(1)}, f32[520,128]{1,0:T(8,128)S(1)}, u32[]{:S(2)}, u32[]{:S(2)}) collective-permute-start(f32[520,128]{1,0:T(8,128)S(1)} %get-tuple-element.29), channel_id=1, source_target_pairs={{0,3},{1,2},{2,1},{3,0},{4,7},{5,6},{6,5},{7,4},{8,11},{9,10},{10,... | collective-permute-start | bytes 798728 | tf_op jit(solution)/shard_map/ppermute | solution.py:278
  10.9 5.3 %collective-permute-start.4 = (f32[256,128]{1,0:T(8,128)S(1)}, f32[256,128]{1,0:T(8,128)S(1)}, u32[]{:S(2)}, u32[]{:S(2)}) collective-permute-start(f32[256,128]{1,0:T(8,128)S(1)} %shard_map.114.refs_0_), channel_id=1, source_target_pairs={{0,4},{1,9},{2,6},{3,11},{4,0},{5,13},{6,2},{7,15},{8,12},{9,1},{1... | collective-permute-start | bytes 393224 | tf_op jit(solution)/shard_map/ppermute | solution.py:278
  12.6 10.0 %collective-permute-start.5 = (f32[256,128]{1,0:T(8,128)S(1)}, f32[256,128]{1,0:T(8,128)S(1)}, u32[]{:S(2)}, u32[]{:S(2)}) collective-permute-start(f32[256,128]{1,0:T(8,128)S(1)} %shard_map.114.refs_0_), channel_id=1, source_target_pairs={{0,8},{1,5},{2,10},{3,7},{4,12},{5,1},{6,14},{7,3},{8,0},{9,13},{1... | collective-permute-start | bytes 393224 | tf_op jit(solution)/shard_map/ppermute | solution.py:278
  16.2 6.4 %collective-permute-start.6 = (f32[256,128]{1,0:T(8,128)S(1)}, f32[256,128]{1,0:T(8,128)S(1)}, u32[]{:S(2)}, u32[]{:S(2)}) collective-permute-start(f32[256,128]{1,0:T(8,128)S(1)} %collective-permute-done.4.refs_1_), channel_id=1, source_target_pairs={{0,8},{1,5},{2,10},{3,7},{4,12},{5,1},{6,14},{7,3},{8,0},{9,13},{1... | collective-permute-start | bytes 393224 | tf_op jit(solution)/shard_map/ppermute | solution.py:278
  23.3 1.4 %collective-permute-start.7 = (f32[64,512]{1,0:T(8,128)S(1)}, f32[64,512]{1,0:T(8,128)S(1)}, u32[]{:S(2)}, u32[]{:S(2)}) collective-permute-start(f32[64,512]{1,0:T(8,128)S(1)} %get-tuple-element.34), channel_id=1, source_target_pairs={{0,1},{1,0},{2,3},{3,2},{4,5},{5,4},{6,7},{7,6},{8,9},{9,8},{10,11... | collective-permute-start | bytes 393224 | tf_op jit(solution)/shard_map/ppermute | solution.py:278
  24.8 5.8 %collective-permute-start.8 = (f32[64,512]{1,0:T(8,128)S(1)}, f32[64,512]{1,0:T(8,128)S(1)}, u32[]{:S(2)}, u32[]{:S(2)}) collective-permute-start(f32[64,512]{1,0:T(8,128)S(1)} %shard_map.116.refs_0_), channel_id=1, source_target_pairs={{0,2},{1,3},{2,0},{3,1},{4,6},{5,7},{6,4},{7,5},{8,10},{9,11},{10,... | collective-permute-start | bytes 393224 | tf_op jit(solution)/shard_map/ppermute | solution.py:278
  30.5 1.4 %collective-permute-start.9 = (f32[64,512]{1,0:T(8,128)S(1)}, f32[64,512]{1,0:T(8,128)S(1)}, u32[]{:S(2)}, u32[]{:S(2)}) collective-permute-start(f32[64,512]{1,0:T(8,128)S(1)} %shard_map.117.mine), channel_id=1, source_target_pairs={{0,1},{1,0},{2,3},{3,2},{4,5},{5,4},{6,7},{7,6},{8,9},{9,8},{10,11... | collective-permute-start | bytes 393224 | tf_op jit(solution)/shard_map/ppermute | solution.py:278
  33.1 5.0 %collective-permute-start.11 = (f32[256,128]{1,0:T(8,128)S(1)}, f32[256,128]{1,0:T(8,128)S(1)}, u32[]{:S(2)}, u32[]{:S(2)}) collective-permute-start(f32[256,128]{1,0:T(8,128)S(1)} %get-tuple-element.40), channel_id=1, source_target_pairs={{0,8},{1,5},{2,10},{3,7},{4,12},{5,1},{6,14},{7,3},{8,0},{9,13},{1... | collective-permute-start | bytes 393224 | tf_op jit(solution)/shard_map/ppermute | solution.py:278
  35.3 11.1 %collective-permute-start.10 = (f32[256,128]{1,0:T(8,128)S(1)}, f32[256,128]{1,0:T(8,128)S(1)}, u32[]{:S(2)}, u32[]{:S(2)}) collective-permute-start(f32[256,128]{1,0:T(8,128)S(1)} %get-tuple-element.38), channel_id=1, source_target_pairs={{0,8},{1,5},{2,10},{3,7},{4,12},{5,1},{6,14},{7,3},{8,0},{9,13},{1... | collective-permute-start | bytes 393224 | tf_op jit(solution)/shard_map/ppermute | solution.py:278
  38.2 8.3 %collective-permute-start.12 = (f32[256,128]{1,0:T(8,128)S(1)}, f32[256,128]{1,0:T(8,128)S(1)}, u32[]{:S(2)}, u32[]{:S(2)}) collective-permute-start(f32[256,128]{1,0:T(8,128)S(1)} %shard_map.122), channel_id=1, source_target_pairs={{0,4},{1,9},{2,6},{3,11},{4,0},{5,13},{6,2},{7,15},{8,12},{9,1},{1... | collective-permute-start | bytes 393224 | tf_op jit(solution)/shard_map/ppermute | solution.py:278
  39.9 4.9 %collective-permute-start.13 = (f32[72,128]{1,0:T(8,128)S(1)}, f32[72,128]{1,0:T(8,128)S(1)}, u32[]{:S(2)}, u32[]{:S(2)}) collective-permute-start(f32[72,128]{1,0:T(8,128)S(1)} %shard_map.124.refs_0_), channel_id=1, source_target_pairs={{0,16},{1,17},{2,18},{3,19},{4,20},{5,21},{6,22},{7,23},{8,24},{9,... | collective-permute-start | bytes 110600 | tf_op jit(solution)/shard_map/ppermute | solution.py:278
  44.9 4.9 %collective-permute-start.14 = (f32[72,128]{1,0:T(8,128)S(1)}, f32[72,128]{1,0:T(8,128)S(1)}, u32[]{:S(2)}, u32[]{:S(2)}) collective-permute-start(f32[72,128]{1,0:T(8,128)S(1)} %shard_map.125.refs_0_), channel_id=1, source_target_pairs={{0,8},{1,5},{2,10},{3,7},{4,12},{5,1},{6,14},{7,3},{8,0},{9,13},{1... | collective-permute-start | bytes 110600 | tf_op jit(solution)/shard_map/ppermute | solution.py:278
  46.5 7.2 %collective-permute-start.15 = (f32[128,128]{1,0:T(8,128)S(1)}, f32[128,128]{1,0:T(8,128)S(1)}, u32[]{:S(2)}, u32[]{:S(2)}) collective-permute-start(f32[128,128]{1,0:T(8,128)S(1)} %get-tuple-element.44), channel_id=1, source_target_pairs={{0,16},{1,17},{2,18},{3,19},{4,20},{5,21},{6,22},{7,23},{8,24},{9,... | collective-permute-start | bytes 196616 | tf_op jit(solution)/shard_map/ppermute | solution.py:278
  49.8 4.0 %collective-permute-start.16 = (f32[72,128]{1,0:T(8,128)S(1)}, f32[72,128]{1,0:T(8,128)S(1)}, u32[]{:S(2)}, u32[]{:S(2)}) collective-permute-start(f32[72,128]{1,0:T(8,128)S(1)} %shard_map.126.refs_1_), channel_id=1, source_target_pairs={{0,4},{1,9},{2,6},{3,11},{4,0},{5,13},{6,2},{7,15},{8,12},{9,1},{1... | collective-permute-start | bytes 110600 | tf_op jit(solution)/shard_map/ppermute | solution.py:278
  53.7 4.7 %collective-permute-start.18 = (f32[200,128]{1,0:T(8,128)S(1)}, f32[200,128]{1,0:T(8,128)S(1)}, u32[]{:S(2)}, u32[]{:S(2)}) collective-permute-start(f32[200,128]{1,0:T(8,128)S(1)} %shard_map.127.refs_0_), channel_id=1, source_target_pairs={{0,2},{1,3},{2,0},{3,1},{4,6},{5,7},{6,4},{7,5},{8,10},{9,11},{10,... | collective-permute-start | bytes 307208 | tf_op jit(solution)/shard_map/ppermute | solution.py:278
  55.3 3.9 %collective-permute-start.17 = (f32[200,128]{1,0:T(8,128)S(1)}, f32[200,128]{1,0:T(8,128)S(1)}, u32[]{:S(2)}, u32[]{:S(2)}) collective-permute-start(f32[200,128]{1,0:T(8,128)S(1)} %shard_map.127.refs_0_), channel_id=1, source_target_pairs={{0,1},{1,0},{2,3},{3,2},{4,5},{5,4},{6,7},{7,6},{8,9},{9,8},{10,11... | collective-permute-start | bytes 307208 | tf_op jit(solution)/shard_map/ppermute | solution.py:278
  58.5 1.3 %collective-permute-start.19 = (f32[200,128]{1,0:T(8,128)S(1)}, f32[200,128]{1,0:T(8,128)S(1)}, u32[]{:S(2)}, u32[]{:S(2)}) collective-permute-start(f32[200,128]{1,0:T(8,128)S(1)} %collective-permute-done.18.refs_2_), channel_id=1, source_target_pairs={{0,1},{1,0},{2,3},{3,2},{4,5},{5,4},{6,7},{7,6},{8,9},{9,8},{10,11... | collective-permute-start | bytes 307208 | tf_op jit(solution)/shard_map/ppermute | solution.py:278

commit v4 on v3

--- a/solution.py
+++ b/solution.py
@@ -104,7 +104,7 @@
         copy.wait()
 
 
-def place_parts(blocks, part, slots, tiles, dense, place_vector, place, sem, clear):
+def place_parts(blocks, part, slots, tiles, dense, place_vector, place, sem, clear, both=()):
     side = dense.shape[1] // blocks
     for d, tile in enumerate(tiles):
         place_vector[d] = tile[pl.ds(slots * part, PAD), :].astype(jnp.int32)
@@ -116,24 +116,35 @@
     for d, tile in enumerate(tiles):
         for s in range(slots):
             lane = pl.ds(pl.multiple_of(place[d, 0, s] * side, LANES), side)
-            at = pl.ds(pl.multiple_of(place[d, 1, s] * part, 8), part)
-            dense[at, lane] = dense[at, lane] + tile[pl.ds(s * part, part), :]
-
-
-def near_kernel(blocks, part, slots, *refs):
-    place_parts(blocks, part, slots, refs[:-4], refs[-4], *refs[-3:], True)
-
-
-def far_kernel(blocks, part, slots, count, *refs):
-    tiles = refs[1 : 1 + count]
-    dense, high_out, low_out = refs[-6:-3]
-    place_parts(blocks, part, slots, tiles, dense, *refs[-3:], False)
-    side = dense.shape[1] // blocks
+            at = pl.ds(pl.multiple_of(place[d, 1, s] * part, part), part)
+            value = dense[at, lane] + tile[pl.ds(s * part, part), :]
+            dense[at, lane] = value
+            for ref, term in zip(both, halves(value)):
+                ref[at, lane] = term.astype(BF16)
+
+
+def split(dense, high_out, low_out):
+    side = 8 * 16
     for k in range(dense.shape[0] // side):
         at = pl.ds(k * side, side)
         high, low = halves(dense[at, :])
         high_out[at, :] = high.astype(BF16)
         low_out[at, :] = low.astype(BF16)
+
+
+def near_kernel(blocks, part, slots, *refs):
+    dense, high_out, low_out = refs[-6:-3]
+    place_parts(blocks, part, slots, refs[:-6], dense, *refs[-3:], True)
+    split(dense, high_out, low_out)
+
+
+def far_kernel(blocks, part, slots, count, *refs):
+    tiles = refs[3 : 3 + count]
+    dense, high_out, low_out = refs[-6:-3]
+    both = (high_out, low_out) if part % 16 == 0 else ()
+    place_parts(blocks, part, slots, tiles, dense, *refs[-3:], False, both)
+    if not both:
+        split(dense, high_out, low_out)
 
 
 def forward_kernel(orders, here, high, low, *refs):
@@ -236,11 +247,10 @@
 
 
 def final_kernel(reps, blocks, part, piece, here, *refs):
-    parts = refs[:reps]
-    grad_features, grad_weight, grad_bias = refs[reps:]
+    parts, weights = refs[:reps], refs[reps : 2 * reps]
+    grad_features, grad_weight, grad_bias = refs[2 * reps :]
     side = grad_features.shape[0] // blocks
     groups = grad_weight.shape[1] // LANES
-    base = blocks * part
     for d in range(reps):
         q = here[0] ^ d
         for b in range(blocks):
@@ -248,9 +258,9 @@
             grad_features[at, :] = parts[d][pl.ds(b * part, part), :]
         at = pl.ds(pl.multiple_of(q * piece, 8), piece)
         for g in range(groups):
-            grad_weight[at, pl.ds(g * LANES, LANES)] = parts[d][pl.ds(base + g * piece, piece), :]
+            grad_weight[at, pl.ds(g * LANES, LANES)] = weights[d][pl.ds(g * piece, piece), :]
     for g in range(groups):
-        row = parts[0][pl.ds(base + groups * piece + g, 1), :]
+        row = weights[0][pl.ds(groups * piece + g, 1), :]
         grad_bias[:, pl.ds(g * LANES, LANES)] = row
 
 
@@ -319,23 +329,24 @@
             pltpu.SemaphoreType.DMA,
         ]
 
-    (dense,) = call(
+    shapes = [(depth, total)] + [((depth, total), BF16)] * 2
+    matrix = call(
         functools.partial(near_kernel, blocks, part, slots),
-        [(depth, total)],
+        shapes,
         [VMEM] * 2,
         scratch(2),
         0,
-        4 << 20,
+        8 << 20,
     )(*tiles[:2])
     _, high, low = call(
         functools.partial(far_kernel, blocks, part, slots, reps - 2),
-        [(depth, total)] + [((depth, total), BF16)] * 2,
-        [VMEM] * (reps + 2),
+        shapes,
+        [VMEM] * (reps + 4),
         scratch(reps - 2),
         0,
         8 << 20,
-        aliases={0: 0},
-    )(dense, *tiles[2:], weight, bias, cotangent)
+        aliases={0: 0, 1: 1, 2: 2},
+    )(*matrix, *tiles[2:], weight, bias, cotangent)
 
     send, keep = call(
         functools.partial(forward_kernel, orders),
@@ -383,7 +394,7 @@
     (going,) = add([on_own], [on_term])
     term = swap(going, "loop", 2)
     (grad,) = add([grad], [grad_term])
-    grad_term = swap(grad, "loop", 1)
+    grad_term = swap(grad, "loop", 2)
     (held,) = add([stay_own], [stay_term])
     bit, rest = 2, stay
     while bit < loops // 2:
@@ -393,25 +404,30 @@
         going, held = add([held], [term], [ahead, behind])
         term = swap(going, "loop", 2 * bit)
         (grad,) = add([grad], [grad_term])
-        grad_term = swap(grad, "loop", bit)
+        grad_term = swap(grad, "loop", bit if bit > 2 else 1)
         bit *= 2
-    (both,) = add([held, grad], [term, grad_term], [[(0, 0, 0, size), (1, 0, 0, extra)]])
-
-    parts = {0: both}
-    bit = reps // 2
-    while bit:
-        for k in list(parts):
-            parts[k | bit] = swap(parts[k], "rep", bit)
-        bit //= 2
+    (mine,) = add([held], [term])
+    (grad,) = add([grad], [grad_term])
+
+    def spread(own):
+        found = {0: own}
+        bit = reps // 2
+        while bit:
+            for k in list(found):
+                found[k | bit] = swap(found[k], "rep", bit)
+            bit //= 2
+        return [found[d] for d in range(reps)]
+
+    parts, weights = spread(mine), spread(grad)
     output = join(output)
     grad_features, grad_weight, grad_bias = call(
         functools.partial(final_kernel, reps, blocks, part, piece),
         [(total, width), (width, wide), (1, wide)],
-        [SMEM] + [VMEM] * reps,
+        [SMEM] + [VMEM] * (2 * reps),
         [],
         0,
         2 * total * width * 4,
-    )(here, *[parts[d] for d in range(reps)])
+    )(here, *parts, *weights)
     return (output, grad_features, grad_weight, grad_bias.reshape(wide))
 
 

time: 60.7 us -> 63.5 us (1.046)
  starting transfers between devices: 19.3 us -> 23.7 us
  waiting for transfers between devices: 31.4 us -> 29.8 us
    ppermute x20 -> x23, starting transfers between devices: 19.3 us -> 23.7 us  [swap(): return lax.ppermute(x, ('loop', 'rep'), pairs)]
    ppermute x20 -> x23, waiting for transfers between devices: 31.4 us -> 29.8 us  [swap(): return lax.ppermute(x, ('loop', 'rep'), pairs)]
  transfers between devices with their start and end apart: 20 -> 23, of which waited for: 12 -> 14; matrix products, arithmetic and copies ran while one was open for 0% -> 0% of each run, Pallas kernels for 7% -> 6%
where the time goes in v4:
time: 63.5 us; the launch traced here: 63.4 us
  waiting for transfers between devices  29.8 us (47%)
  starting transfers between devices  23.7 us (37%)
  Pallas kernels  8.43 us (13%)
  between operations  1.5 us (2%)
    ppermute x23, waiting for transfers between devices, swap(): return lax.ppermute(x, ('loop', 'rep'), pairs)  29.8 us
    ppermute x23, starting transfers between devices, swap(): return lax.ppermute(x, ('loop', 'rep'), pairs)  23.7 us
    pallas_call x1, Pallas kernels, per_device(): call(functools.partial(pack_kernel, reps, loops, blocks, part), [(size, w...  1.69 us
    pallas_call x1, Pallas kernels, per_device(): call(functools.partial(near_kernel, blocks, part, slots), shapes, [VMEM]...  1.45 us
  transfers between devices with their start and end apart: 23, of which 14 were waited for; matrix products, arithmetic and copies ran while one was open for 0% of the time, Pallas kernels for 6%

profile of v4, /device:TPU:0, one launch (start us, length us, event | category | flops | bytes accessed | tf_op | source)
XLA Modules:
  0.0 63.4 jit_solution(14431680724313261899)
XLA Ops:
  1.4 1.7 %shard_map.111 = (f32[128,128]{1,0:T(8,128)S(1)}, f32[520,128]{1,0:T(8,128)S(1)}, f32[520,128]{1,0:T(8,128)S(1)}, f32[520,128]{1,0:T(8,128)S(1)}, f32[520,128]{1,0:T(8,128)S(1)}) custom-call(s32[1]{0:T(128)} %bitcast.rep_at.here, s32[1]{0:T(128)} %bitcast.1.at_loop, s32[1]{0:T(128)S(6)} %copy.18.count, f32[512,128]{1,0:T(8,128)} %features.1, ...), custom_call_target="tpu_custom_call" | custom-call | bytes 2097152 | tf_op jit(solution)/shard_map/pallas_call | solution.py:298
  3.1 4.1 %collective-permute-start.3 = (f32[128,128]{1,0:T(8,128)S(1)}, f32[128,128]{1,0:T(8,128)S(1)}, u32[]{:S(2)}, u32[]{:S(2)}) collective-permute-start(f32[128,128]{1,0:T(8,128)S(1)} %get-tuple-element.38.refs_0_), channel_id=1, source_target_pairs={{0,16},{1,17},{2,18},{3,19},{4,20},{5,21},{6,22},{7,23},{8,24},{9,... | collective-permute-start | bytes 196616 | tf_op jit(solution)/shard_map/ppermute | solution.py:288
  7.2 0.0 collective-permute-start
  7.2 1.5 %collective-permute-start.1 = (f32[520,128]{1,0:T(8,128)S(1)}, f32[520,128]{1,0:T(8,128)S(1)}, u32[]{:S(2)}, u32[]{:S(2)}) collective-permute-start(f32[520,128]{1,0:T(8,128)S(1)} %get-tuple-element.34), channel_id=1, source_target_pairs={{0,2},{1,3},{2,0},{3,1},{4,6},{5,7},{6,4},{7,5},{8,10},{9,11},{10,... | collective-permute-start | bytes 798728 | tf_op jit(solution)/shard_map/ppermute | solution.py:288
  8.7 0.3 collective-permute-start.2
  9.1 1.8 %collective-permute-done.3.refs_1_ = f32[128,128]{1,0:T(8,128)S(1)} collective-permute-done((f32[128,128]{1,0:T(8,128)S(1)}, f32[128,128]{1,0:T(8,128)S(1)}, u32[]{:S(2)}, u32[]{:S(2)}) %collective-permute-start.3) | collective-permute-done | bytes 65568 | tf_op jit(solution)/shard_map/ppermute | solution.py:288
  10.9 1.8 %collective-permute-start.4 = (f32[256,128]{1,0:T(8,128)S(1)}, f32[256,128]{1,0:T(8,128)S(1)}, u32[]{:S(2)}, u32[]{:S(2)}) collective-permute-start(f32[256,128]{1,0:T(8,128)S(1)} %shard_map.114.refs_0_), channel_id=1, source_target_pairs={{0,4},{1,9},{2,6},{3,11},{4,0},{5,13},{6,2},{7,15},{8,12},{9,1},{1... | collective-permute-start | bytes 393224 | tf_op jit(solution)/shard_map/ppermute | solution.py:288
  12.6 0.4 collective-permute-start.5
  13.0 3.2 %collective-permute-done.4.refs_1_ = f32[256,128]{1,0:T(8,128)S(1)} collective-permute-done((f32[256,128]{1,0:T(8,128)S(1)}, f32[256,128]{1,0:T(8,128)S(1)}, u32[]{:S(2)}, u32[]{:S(2)}) %collective-permute-start.4) | collective-permute-done | bytes 131104 | tf_op jit(solution)/shard_map/ppermute | solution.py:288
  16.2 0.4 collective-permute-start.6
  16.6 0.0 collective-permute-done.refs_1_
  16.6 1.5 %shard_map.112 = (f32[1024,512]{1,0:T(8,128)S(1)}, bf16[1024,512]{1,0:T(8,128)(2,1)S(1)}, bf16[1024,512]{1,0:T(8,128)(2,1)S(1)}) custom-call(f32[520,128]{1,0:T(8,128)S(1)} %get-tuple-element.29.refs_0_, f32[520,128]{1,0:T(8,128)S(1)} %collective-permute-done.refs_1_), custom_call_target="tpu_custom_call" | custom-call | bytes 8388608 | tf_op jit(solution)/shard_map/pallas_call | solution.py:333
  18.0 0.0 collective-permute-done.1.refs_3_
  18.1 3.2 %collective-permute-done.2.refs_4_ = f32[520,128]{1,0:T(8,128)S(1)} collective-permute-done((f32[520,128]{1,0:T(8,128)S(1)}, f32[520,128]{1,0:T(8,128)S(1)}, u32[]{:S(2)}, u32[]{:S(2)}) %collective-permute-start.2) | collective-permute-done | bytes 266272 | tf_op jit(solution)/shard_map/ppermute | solution.py:288
  21.3 0.9 %shard_map.113 = (f32[1024,512]{1,0:T(8,128)S(1)}, bf16[1024,512]{1,0:T(8,128)(2,1)S(1)}, bf16[1024,512]{1,0:T(8,128)(2,1)S(1)}) custom-call(f32[1024,512]{1,0:T(8,128)S(1)} %get-tuple-element.31.refs_0_, bf16[1024,512]{1,0:T(8,128)(2,1)S(1)} %get-tuple-element.32.refs_1_, ...), custom_call_target="tpu_custom_call", output_to_operand_aliasing={{0}: (0, {}), {1}: (1, {}), {2}: (2, {})} | custom-call | bytes 8388608 | tf_op jit(solution)/shard_map/pallas_call | solution.py:341
  22.2 0.0 collective-permute-done.5.refs_2_
  22.2 0.0 collective-permute-done.6.refs_3_
  22.2 0.7 %shard_map.115 = (f32[64,512]{1,0:T(8,128)S(1)}, f32[64,512]{1,0:T(8,128)S(1)}) custom-call(s32[1]{0:T(128)} %bitcast.rep_at.here, bf16[1024,512]{1,0:T(8,128)(2,1)S(1)} %get-tuple-element.36.high, bf16[1024,512]{1,0:T(8,128)(2,1)S(1)} %get-tuple-element.37.low, f32[256,128]{1,0:T(8,128)S(1)} %shard_map.114.refs_0_, ...), custom_call_target="tpu_custom_call" | custom-call | flops 402653184 | bytes 4194304 | tf_op jit(solution)/shard_map/pallas_call | solution.py:351
  22.9 0.3 collective-permute-start.7
  23.3 1.1 %collective-permute-done.7.refs_1_ = f32[64,512]{1,0:T(8,128)S(1)} collective-permute-done((f32[64,512]{1,0:T(8,128)S(1)}, f32[64,512]{1,0:T(8,128)S(1)}, u32[]{:S(2)}, u32[]{:S(2)}) %collective-permute-start.7) | collective-permute-done | bytes 131104 | tf_op jit(solution)/shard_map/ppermute | solution.py:288
  24.4 1.6 %collective-permute-start.8 = (f32[64,512]{1,0:T(8,128)S(1)}, f32[64,512]{1,0:T(8,128)S(1)}, u32[]{:S(2)}, u32[]{:S(2)}) collective-permute-start(f32[64,512]{1,0:T(8,128)S(1)} %shard_map.116.refs_0_), channel_id=1, source_target_pairs={{0,2},{1,3},{2,0},{3,1},{4,6},{5,7},{6,4},{7,5},{8,10},{9,11},{10,... | collective-permute-start | bytes 393224 | tf_op jit(solution)/shard_map/ppermute | solution.py:288
  26.0 4.1 %collective-permute-done.8.refs_1_ = f32[64,512]{1,0:T(8,128)S(1)} collective-permute-done((f32[64,512]{1,0:T(8,128)S(1)}, f32[64,512]{1,0:T(8,128)S(1)}, u32[]{:S(2)}, u32[]{:S(2)}) %collective-permute-start.8) | collective-permute-done | bytes 131104 | tf_op jit(solution)/shard_map/ppermute | solution.py:288
  30.1 0.1 collective-permute-start.9
  30.2 1.3 %collective-permute-done.9.other = f32[64,512]{1,0:T(8,128)S(1)} collective-permute-done((f32[64,512]{1,0:T(8,128)S(1)}, f32[64,512]{1,0:T(8,128)S(1)}, u32[]{:S(2)}, u32[]{:S(2)}) %collective-permute-start.9) | collective-permute-done | bytes 131104 | tf_op jit(solution)/shard_map/ppermute | solution.py:288
  31.5 1.1 %shard_map.118 = (f32[256,128]{1,0:T(8,128)S(1)}, f32[512,256]{1,0:T(8,128)S(1)}, f32[512,256]{1,0:T(8,128)S(1)}, f32[32,512]{1,0:T(8,128)S(1)}, bf16[512,256]{1,0:T(8,128)(2,1)S(1)}) custom-call(s32[1]{0:T(128)} %bitcast.rep_at.here, bf16[1024,512]{1,0:T(8,128)(2,1)S(1)} %get-tuple-element.36.high, bf16[1024,512]{1,0:T(8,128)(2,1)S(1)} %get-tuple-element.37.low, ...), custom_call_target="tpu_custom_call" | custom-call | flops 134217728 | bytes 4194304 | tf_op jit(solution)/shard_map/pallas_call | solution.py:369
  32.7 1.6 %collective-permute-start.11 = (f32[256,128]{1,0:T(8,128)S(1)}, f32[256,128]{1,0:T(8,128)S(1)}, u32[]{:S(2)}, u32[]{:S(2)}) collective-permute-start(f32[256,128]{1,0:T(8,128)S(1)} %get-tuple-element.46), channel_id=1, source_target_pairs={{0,8},{1,5},{2,10},{3,7},{4,12},{5,1},{6,14},{7,3},{8,0},{9,13},{1... | collective-permute-start | bytes 393224 | tf_op jit(solution)/shard_map/ppermute | solution.py:288
  34.3 0.6 shard_map.120
  34.9 0.5 collective-permute-start.10
  35.4 2.3 %collective-permute-done.11.refs_1_ = f32[256,128]{1,0:T(8,128)S(1)} collective-permute-done((f32[256,128]{1,0:T(8,128)S(1)}, f32[256,128]{1,0:T(8,128)S(1)}, u32[]{:S(2)}, u32[]{:S(2)}) %collective-permute-start.11) | collective-permute-done | bytes 131104 | tf_op jit(solution)/shard_map/ppermute | solution.py:288
  37.7 1.6 %collective-permute-start.12 = (f32[256,128]{1,0:T(8,128)S(1)}, f32[256,128]{1,0:T(8,128)S(1)}, u32[]{:S(2)}, u32[]{:S(2)}) collective-permute-start(f32[256,128]{1,0:T(8,128)S(1)} %shard_map.122), channel_id=1, source_target_pairs={{0,4},{1,9},{2,6},{3,11},{4,0},{5,13},{6,2},{7,15},{8,12},{9,1},{1... | collective-permute-start | bytes 393224 | tf_op jit(solution)/shard_map/ppermute | solution.py:288
  39.3 0.8 %collective-permute-done.10.refs_1_ = f32[256,128]{1,0:T(8,128)S(1)} collective-permute-done((f32[256,128]{1,0:T(8,128)S(1)}, f32[256,128]{1,0:T(8,128)S(1)}, u32[]{:S(2)}, u32[]{:S(2)}) %collective-permute-start.10) | collective-permute-done | bytes 131104 | tf_op jit(solution)/shard_map/ppermute | solution.py:288
  40.2 2.6 %collective-permute-done.12.refs_1_ = f32[256,128]{1,0:T(8,128)S(1)} collective-permute-done((f32[256,128]{1,0:T(8,128)S(1)}, f32[256,128]{1,0:T(8,128)S(1)}, u32[]{:S(2)}, u32[]{:S(2)}) %collective-permute-start.12) | collective-permute-done | bytes 131104 | tf_op jit(solution)/shard_map/ppermute | solution.py:288
  42.8 0.7 %collective-permute-start.13 = (f32[128,128]{1,0:T(8,128)S(1)}, f32[128,128]{1,0:T(8,128)S(1)}, u32[]{:S(2)}, u32[]{:S(2)}) collective-permute-start(f32[128,128]{1,0:T(8,128)S(1)} %get-tuple-element.48), channel_id=1, source_target_pairs={{0,16},{1,17},{2,18},{3,19},{4,20},{5,21},{6,22},{7,23},{8,24},{9,... | collective-permute-start | bytes 196616 | tf_op jit(solution)/shard_map/ppermute | solution.py:288
  43.5 0.2 shard_map.125.refs_0_
  43.8 2.3 %collective-permute-start.17 = (f32[72,128]{1,0:T(8,128)S(1)}, f32[72,128]{1,0:T(8,128)S(1)}, u32[]{:S(2)}, u32[]{:S(2)}) collective-permute-start(f32[72,128]{1,0:T(8,128)S(1)} %shard_map.125.refs_0_), channel_id=1, source_target_pairs={{0,16},{1,17},{2,18},{3,19},{4,20},{5,21},{6,22},{7,23},{8,24},{9,... | collective-permute-start | bytes 110600 | tf_op jit(solution)/shard_map/ppermute | solution.py:288
  46.1 3.4 %collective-permute-done.17.refs_1_ = f32[72,128]{1,0:T(8,128)S(1)} collective-permute-done((f32[72,128]{1,0:T(8,128)S(1)}, f32[72,128]{1,0:T(8,128)S(1)}, u32[]{:S(2)}, u32[]{:S(2)}) %collective-permute-start.17) | collective-permute-done | bytes 36896 | tf_op jit(solution)/shard_map/ppermute | solution.py:288
  49.5 1.5 %collective-permute-start.18 = (f32[72,128]{1,0:T(8,128)S(1)}, f32[72,128]{1,0:T(8,128)S(1)}, u32[]{:S(2)}, u32[]{:S(2)}) collective-permute-start(f32[72,128]{1,0:T(8,128)S(1)} %shard_map.126.refs_0_), channel_id=1, source_target_pairs={{0,4},{1,9},{2,6},{3,11},{4,0},{5,13},{6,2},{7,15},{8,12},{9,1},{1... | collective-permute-start | bytes 110600 | tf_op jit(solution)/shard_map/ppermute | solution.py:288
  51.0 1.6 %collective-permute-start.15 = (f32[128,128]{1,0:T(8,128)S(1)}, f32[128,128]{1,0:T(8,128)S(1)}, u32[]{:S(2)}, u32[]{:S(2)}) collective-permute-start(f32[128,128]{1,0:T(8,128)S(1)} %shard_map.124.refs_0_), channel_id=1, source_target_pairs={{0,2},{1,3},{2,0},{3,1},{4,6},{5,7},{6,4},{7,5},{8,10},{9,11},{10,... | collective-permute-start | bytes 196616 | tf_op jit(solution)/shard_map/ppermute | solution.py:288
  52.6 0.8 %collective-permute-done.18.refs_1_ = f32[72,128]{1,0:T(8,128)S(1)} collective-permute-done((f32[72,128]{1,0:T(8,128)S(1)}, f32[72,128]{1,0:T(8,128)S(1)}, u32[]{:S(2)}, u32[]{:S(2)}) %collective-permute-start.18) | collective-permute-done | bytes 36896 | tf_op jit(solution)/shard_map/ppermute | solution.py:288
  53.5 1.2 %collective-permute-start.19 = (f32[72,128]{1,0:T(8,128)S(1)}, f32[72,128]{1,0:T(8,128)S(1)}, u32[]{:S(2)}, u32[]{:S(2)}) collective-permute-start(f32[72,128]{1,0:T(8,128)S(1)} %shard_map.127.refs_0_), channel_id=1, source_target_pairs={{0,8},{1,5},{2,10},{3,7},{4,12},{5,1},{6,14},{7,3},{8,0},{9,13},{1... | collective-permute-start | bytes 110600 | tf_op jit(solution)/shard_map/ppermute | solution.py:288
  54.7 2.7 %collective-permute-done.19.refs_1_ = f32[72,128]{1,0:T(8,128)S(1)} collective-permute-done((f32[72,128]{1,0:T(8,128)S(1)}, f32[72,128]{1,0:T(8,128)S(1)}, u32[]{:S(2)}, u32[]{:S(2)}) %collective-permute-start.19) | collective-permute-done | bytes 36896 | tf_op jit(solution)/shard_map/ppermute | solution.py:288
  57.4 1.6 %collective-permute-start.21 = (f32[72,128]{1,0:T(8,128)S(1)}, f32[72,128]{1,0:T(8,128)S(1)}, u32[]{:S(2)}, u32[]{:S(2)}) collective-permute-start(f32[72,128]{1,0:T(8,128)S(1)} %shard_map.128.refs_4_), channel_id=1, source_target_pairs={{0,2},{1,3},{2,0},{3,1},{4,6},{5,7},{6,4},{7,5},{8,10},{9,11},{10,... | collective-permute-start | bytes 110600 | tf_op jit(solution)/shard_map/ppermute | solution.py:288
  59.0 0.5 collective-permute-start.16
  59.5 0.0 collective-permute-start.20
  59.5 1.9 %collective-permute-done.21.refs_6_ = f32[72,128]{1,0:T(8,128)S(1)} collective-permute-done((f32[72,128]{1,0:T(8,128)S(1)}, f32[72,128]{1,0:T(8,128)S(1)}, u32[]{:S(2)}, u32[]{:S(2)}) %collective-permute-start.21) | collective-permute-done | bytes 36896 | tf_op jit(solution)/shard_map/ppermute | solution.py:288
  61.4 0.8 %shard_map.119 = f32[512,256]{1,0:T(8,128)} custom-call(f32[512,256]{1,0:T(8,128)S(1)} %get-tuple-element.41.refs_0_), custom_call_target="tpu_custom_call" | custom-call | bytes 1048576 | tf_op jit(solution)/shard_map/pallas_call | solution.py:292
  62.2 0.4 collective-permute-done.22.refs_7_
  62.6 0.8 %shard_map.129 = (f32[512,128]{1,0:T(8,128)}, f32[128,256]{1,0:T(8,128)}, f32[1,256]{1,0:T(1,128)}) custom-call(s32[1]{0:T(128)} %bitcast.rep_at.here, f32[128,128]{1,0:T(8,128)S(1)} %shard_map.124.refs_0_, f32[128,128]{1,0:T(8,128)S(1)} %collective-permute-done.14.refs_1_, f32[128,128]{1,0:T(8,128)S(1)} %collective-permute-done.15.refs_2_, ...), custom_call_target="tpu_custom_call" | custom-call | bytes 524288 | tf_op jit(solution)/shard_map/pallas_call | solution.py:423
  (23 shorter events, 0.1 us)
Async XLA Ops:
  0.6 20.6 %copy-start.2 = (f32[256]{0:T(256)S(1)}, f32[256]{0:T(256)}, u32[]{:S(2)}) copy-start(f32[256]{0:T(256)} %param.10) | copy-start | bytes 3076
  0.6 20.6 %copy-start = (f32[512,256]{1,0:T(8,128)S(1)}, f32[512,256]{1,0:T(8,128)}, u32[]{:S(2)}) copy-start(f32[512,256]{1,0:T(8,128)} %cotangent.1) | copy-start | bytes 1572868
  0.7 20.6 %copy-start.1 = (f32[128,256]{1,0:T(8,128)S(1)}, f32[128,256]{1,0:T(8,128)}, u32[]{:S(2)}) copy-start(f32[128,256]{1,0:T(8,128)} %weight.1) | copy-start | bytes 393220
  3.1 7.8 %collective-permute-start.3 = (f32[128,128]{1,0:T(8,128)S(1)}, f32[128,128]{1,0:T(8,128)S(1)}, u32[]{:S(2)}, u32[]{:S(2)}) collective-permute-start(f32[128,128]{1,0:T(8,128)S(1)} %get-tuple-element.38.refs_0_), channel_id=1, source_target_pairs={{0,16},{1,17},{2,18},{3,19},{4,20},{5,21},{6,22},{7,23},{8,24},{9,... | collective-permute-start | bytes 196616 | tf_op jit(solution)/shard_map/ppermute | solution.py:288
  7.2 9.4 %collective-permute-start = (f32[520,128]{1,0:T(8,128)S(1)}, f32[520,128]{1,0:T(8,128)S(1)}, u32[]{:S(2)}, u32[]{:S(2)}) collective-permute-start(f32[520,128]{1,0:T(8,128)S(1)} %get-tuple-element.30), channel_id=1, source_target_pairs={{0,1},{1,0},{2,3},{3,2},{4,5},{5,4},{6,7},{7,6},{8,9},{9,8},{10,11... | collective-permute-start | bytes 798728 | tf_op jit(solution)/shard_map/ppermute | solution.py:288
  7.2 10.8 %collective-permute-start.1 = (f32[520,128]{1,0:T(8,128)S(1)}, f32[520,128]{1,0:T(8,128)S(1)}, u32[]{:S(2)}, u32[]{:S(2)}) collective-permute-start(f32[520,128]{1,0:T(8,128)S(1)} %get-tuple-element.34), channel_id=1, source_target_pairs={{0,2},{1,3},{2,0},{3,1},{4,6},{5,7},{6,4},{7,5},{8,10},{9,11},{10,... | collective-permute-start | bytes 798728 | tf_op jit(solution)/shard_map/ppermute | solution.py:288
  8.7 12.5 %collective-permute-start.2 = (f32[520,128]{1,0:T(8,128)S(1)}, f32[520,128]{1,0:T(8,128)S(1)}, u32[]{:S(2)}, u32[]{:S(2)}) collective-permute-start(f32[520,128]{1,0:T(8,128)S(1)} %get-tuple-element.35), channel_id=1, source_target_pairs={{0,3},{1,2},{2,1},{3,0},{4,7},{5,6},{6,5},{7,4},{8,11},{9,10},{10,... | collective-permute-start | bytes 798728 | tf_op jit(solution)/shard_map/ppermute | solution.py:288
  10.9 5.3 %collective-permute-start.4 = (f32[256,128]{1,0:T(8,128)S(1)}, f32[256,128]{1,0:T(8,128)S(1)}, u32[]{:S(2)}, u32[]{:S(2)}) collective-permute-start(f32[256,128]{1,0:T(8,128)S(1)} %shard_map.114.refs_0_), channel_id=1, source_target_pairs={{0,4},{1,9},{2,6},{3,11},{4,0},{5,13},{6,2},{7,15},{8,12},{9,1},{1... | collective-permute-start | bytes 393224 | tf_op jit(solution)/shard_map/ppermute | solution.py:288
  12.6 9.6 %collective-permute-start.5 = (f32[256,128]{1,0:T(8,128)S(1)}, f32[256,128]{1,0:T(8,128)S(1)}, u32[]{:S(2)}, u32[]{:S(2)}) collective-permute-start(f32[256,128]{1,0:T(8,128)S(1)} %shard_map.114.refs_0_), channel_id=1, source_target_pairs={{0,8},{1,5},{2,10},{3,7},{4,12},{5,1},{6,14},{7,3},{8,0},{9,13},{1... | collective-permute-start | bytes 393224 | tf_op jit(solution)/shard_map/ppermute | solution.py:288
  16.2 6.0 %collective-permute-start.6 = (f32[256,128]{1,0:T(8,128)S(1)}, f32[256,128]{1,0:T(8,128)S(1)}, u32[]{:S(2)}, u32[]{:S(2)}) collective-permute-start(f32[256,128]{1,0:T(8,128)S(1)} %collective-permute-done.4.refs_1_), channel_id=1, source_target_pairs={{0,8},{1,5},{2,10},{3,7},{4,12},{5,1},{6,14},{7,3},{8,0},{9,13},{1... | collective-permute-start | bytes 393224 | tf_op jit(solution)/shard_map/ppermute | solution.py:288
  22.9 1.4 %collective-permute-start.7 = (f32[64,512]{1,0:T(8,128)S(1)}, f32[64,512]{1,0:T(8,128)S(1)}, u32[]{:S(2)}, u32[]{:S(2)}) collective-permute-start(f32[64,512]{1,0:T(8,128)S(1)} %get-tuple-element.40), channel_id=1, source_target_pairs={{0,1},{1,0},{2,3},{3,2},{4,5},{5,4},{6,7},{7,6},{8,9},{9,8},{10,11... | collective-permute-start | bytes 393224 | tf_op jit(solution)/shard_map/ppermute | solution.py:288
  24.4 5.7 %collective-permute-start.8 = (f32[64,512]{1,0:T(8,128)S(1)}, f32[64,512]{1,0:T(8,128)S(1)}, u32[]{:S(2)}, u32[]{:S(2)}) collective-permute-start(f32[64,512]{1,0:T(8,128)S(1)} %shard_map.116.refs_0_), channel_id=1, source_target_pairs={{0,2},{1,3},{2,0},{3,1},{4,6},{5,7},{6,4},{7,5},{8,10},{9,11},{10,... | collective-permute-start | bytes 393224 | tf_op jit(solution)/shard_map/ppermute | solution.py:288
  30.1 1.4 %collective-permute-start.9 = (f32[64,512]{1,0:T(8,128)S(1)}, f32[64,512]{1,0:T(8,128)S(1)}, u32[]{:S(2)}, u32[]{:S(2)}) collective-permute-start(f32[64,512]{1,0:T(8,128)S(1)} %shard_map.117.mine), channel_id=1, source_target_pairs={{0,1},{1,0},{2,3},{3,2},{4,5},{5,4},{6,7},{7,6},{8,9},{9,8},{10,11... | collective-permute-start | bytes 393224 | tf_op jit(solution)/shard_map/ppermute | solution.py:288
  32.7 5.0 %collective-permute-start.11 = (f32[256,128]{1,0:T(8,128)S(1)}, f32[256,128]{1,0:T(8,128)S(1)}, u32[]{:S(2)}, u32[]{:S(2)}) collective-permute-start(f32[256,128]{1,0:T(8,128)S(1)} %get-tuple-element.46), channel_id=1, source_target_pairs={{0,8},{1,5},{2,10},{3,7},{4,12},{5,1},{6,14},{7,3},{8,0},{9,13},{1... | collective-permute-start | bytes 393224 | tf_op jit(solution)/shard_map/ppermute | solution.py:288
  34.9 5.3 %collective-permute-start.10 = (f32[256,128]{1,0:T(8,128)S(1)}, f32[256,128]{1,0:T(8,128)S(1)}, u32[]{:S(2)}, u32[]{:S(2)}) collective-permute-start(f32[256,128]{1,0:T(8,128)S(1)} %get-tuple-element.44), channel_id=1, source_target_pairs={{0,8},{1,5},{2,10},{3,7},{4,12},{5,1},{6,14},{7,3},{8,0},{9,13},{1... | collective-permute-start | bytes 393224 | tf_op jit(solution)/shard_map/ppermute | solution.py:288
  37.7 5.0 %collective-permute-start.12 = (f32[256,128]{1,0:T(8,128)S(1)}, f32[256,128]{1,0:T(8,128)S(1)}, u32[]{:S(2)}, u32[]{:S(2)}) collective-permute-start(f32[256,128]{1,0:T(8,128)S(1)} %shard_map.122), channel_id=1, source_target_pairs={{0,4},{1,9},{2,6},{3,11},{4,0},{5,13},{6,2},{7,15},{8,12},{9,1},{1... | collective-permute-start | bytes 393224 | tf_op jit(solution)/shard_map/ppermute | solution.py:288
  42.8 8.2 %collective-permute-start.13 = (f32[128,128]{1,0:T(8,128)S(1)}, f32[128,128]{1,0:T(8,128)S(1)}, u32[]{:S(2)}, u32[]{:S(2)}) collective-permute-start(f32[128,128]{1,0:T(8,128)S(1)} %get-tuple-element.48), channel_id=1, source_target_pairs={{0,16},{1,17},{2,18},{3,19},{4,20},{5,21},{6,22},{7,23},{8,24},{9,... | collective-permute-start | bytes 196616 | tf_op jit(solution)/shard_map/ppermute | solution.py:288
  43.8 5.7 %collective-permute-start.17 = (f32[72,128]{1,0:T(8,128)S(1)}, f32[72,128]{1,0:T(8,128)S(1)}, u32[]{:S(2)}, u32[]{:S(2)}) collective-permute-start(f32[72,128]{1,0:T(8,128)S(1)} %shard_map.125.refs_0_), channel_id=1, source_target_pairs={{0,16},{1,17},{2,18},{3,19},{4,20},{5,21},{6,22},{7,23},{8,24},{9,... | collective-permute-start | bytes 110600 | tf_op jit(solution)/shard_map/ppermute | solution.py:288
  49.5 4.0 %collective-permute-start.18 = (f32[72,128]{1,0:T(8,128)S(1)}, f32[72,128]{1,0:T(8,128)S(1)}, u32[]{:S(2)}, u32[]{:S(2)}) collective-permute-start(f32[72,128]{1,0:T(8,128)S(1)} %shard_map.126.refs_0_), channel_id=1, source_target_pairs={{0,4},{1,9},{2,6},{3,11},{4,0},{5,13},{6,2},{7,15},{8,12},{9,1},{1... | collective-permute-start | bytes 110600 | tf_op jit(solution)/shard_map/ppermute | solution.py:288
  51.0 8.0 %collective-permute-start.15 = (f32[128,128]{1,0:T(8,128)S(1)}, f32[128,128]{1,0:T(8,128)S(1)}, u32[]{:S(2)}, u32[]{:S(2)}) collective-permute-start(f32[128,128]{1,0:T(8,128)S(1)} %shard_map.124.refs_0_), channel_id=1, source_target_pairs={{0,2},{1,3},{2,0},{3,1},{4,6},{5,7},{6,4},{7,5},{8,10},{9,11},{10,... | collective-permute-start | bytes 196616 | tf_op jit(solution)/shard_map/ppermute | solution.py:288
  53.5 4.0 %collective-permute-start.19 = (f32[72,128]{1,0:T(8,128)S(1)}, f32[72,128]{1,0:T(8,128)S(1)}, u32[]{:S(2)}, u32[]{:S(2)}) collective-permute-start(f32[72,128]{1,0:T(8,128)S(1)} %shard_map.127.refs_0_), channel_id=1, source_target_pairs={{0,8},{1,5},{2,10},{3,7},{4,12},{5,1},{6,14},{7,3},{8,0},{9,13},{1... | collective-permute-start | bytes 110600 | tf_op jit(solution)/shard_map/ppermute | solution.py:288
  57.4 4.0 %collective-permute-start.21 = (f32[72,128]{1,0:T(8,128)S(1)}, f32[72,128]{1,0:T(8,128)S(1)}, u32[]{:S(2)}, u32[]{:S(2)}) collective-permute-start(f32[72,128]{1,0:T(8,128)S(1)} %shard_map.128.refs_4_), channel_id=1, source_target_pairs={{0,2},{1,3},{2,0},{3,1},{4,6},{5,7},{6,4},{7,5},{8,10},{9,11},{10,... | collective-permute-start | bytes 110600 | tf_op jit(solution)/shard_map/ppermute | solution.py:288
  59.0 3.6 %collective-permute-start.14 = (f32[128,128]{1,0:T(8,128)S(1)}, f32[128,128]{1,0:T(8,128)S(1)}, u32[]{:S(2)}, u32[]{:S(2)}) collective-permute-start(f32[128,128]{1,0:T(8,128)S(1)} %shard_map.124.refs_0_), channel_id=1, source_target_pairs={{0,1},{1,0},{2,3},{3,2},{4,5},{5,4},{6,7},{7,6},{8,9},{9,8},{10,11... | collective-permute-start | bytes 196616 | tf_op jit(solution)/shard_map/ppermute | solution.py:288
  59.0 3.6 %collective-permute-start.16 = (f32[128,128]{1,0:T(8,128)S(1)}, f32[128,128]{1,0:T(8,128)S(1)}, u32[]{:S(2)}, u32[]{:S(2)}) collective-permute-start(f32[128,128]{1,0:T(8,128)S(1)} %collective-permute-done.15.refs_2_), channel_id=1, source_target_pairs={{0,1},{1,0},{2,3},{3,2},{4,5},{5,4},{6,7},{7,6},{8,9},{9,8},{10,11... | collective-permute-start | bytes 196616 | tf_op jit(solution)/shard_map/ppermute | solution.py:288
  59.5 2.7 %collective-permute-start.20 = (f32[72,128]{1,0:T(8,128)S(1)}, f32[72,128]{1,0:T(8,128)S(1)}, u32[]{:S(2)}, u32[]{:S(2)}) collective-permute-start(f32[72,128]{1,0:T(8,128)S(1)} %shard_map.128.refs_4_), channel_id=1, source_target_pairs={{0,1},{1,0},{2,3},{3,2},{4,5},{5,4},{6,7},{7,6},{8,9},{9,8},{10,11... | collective-permute-start | bytes 110600 | tf_op jit(solution)/shard_map/ppermute | solution.py:288
  61.4 1.2 %collective-permute-start.22 = (f32[72,128]{1,0:T(8,128)S(1)}, f32[72,128]{1,0:T(8,128)S(1)}, u32[]{:S(2)}, u32[]{:S(2)}) collective-permute-start(f32[72,128]{1,0:T(8,128)S(1)} %collective-permute-done.21.refs_6_), channel_id=1, source_target_pairs={{0,1},{1,0},{2,3},{3,2},{4,5},{5,4},{6,7},{7,6},{8,9},{9,8},{10,11... | collective-permute-start | bytes 110600 | tf_op jit(solution)/shard_map/ppermute | solution.py:288

commit v5 on v4

--- a/solution.py
+++ b/solution.py
@@ -315,9 +315,9 @@
     feats, orders = [own, swap(own, "loop", bit)], [[0], [bit]]
     bit //= 2
     while bit > 1:
-        feats, order = [join(*feats)], sum(orders, [])
-        feats.append(swap(feats[0], "loop", bit))
-        orders = [order, [k | bit for k in order]]
+        order = sum(orders, [])
+        far = [swap(x, "loop", bit) for x in feats]
+        feats, orders = [join(*feats), join(*far)], [order, [k | bit for k in order]]
         bit //= 2
     feats += [swap(x, "loop", 1) for x in feats]
     orders += [[k | 1 for k in order] for order in orders]

time: 63.5 us -> 65.1 us (1.025)
  starting transfers between devices: 23.7 us -> 27.4 us
  waiting for transfers between devices: 29.8 us -> 27.6 us
    ppermute x23 -> x24, starting transfers between devices: 23.7 us -> 27.4 us  [swap(): return lax.ppermute(x, ('loop', 'rep'), pairs)]
    ppermute x23 -> x24, waiting for transfers between devices: 29.8 us -> 27.6 us  [swap(): return lax.ppermute(x, ('loop', 'rep'), pairs)]
  transfers between devices with their start and end apart: 23 -> 24, of which waited for: 14 -> 14; matrix products, arithmetic and copies ran while one was open for 0% -> 0% of each run, Pallas kernels for 6% -> 6%
where the time goes in v5:
time: 65.1 us; the launch traced here: 64.9 us
  waiting for transfers between devices  27.6 us (42%)
  starting transfers between devices  27.4 us (42%)
  Pallas kernels  8.43 us (13%)
  between operations  1.54 us (2%)
    ppermute x24, waiting for transfers between devices, swap(): return lax.ppermute(x, ('loop', 'rep'), pairs)  27.6 us
    ppermute x24, starting transfers between devices, swap(): return lax.ppermute(x, ('loop', 'rep'), pairs)  27.4 us
    pallas_call x1, Pallas kernels, per_device(): call(functools.partial(pack_kernel, reps, loops, blocks, part), [(size, w...  1.69 us
    pallas_call x1, Pallas kernels, per_device(): call(functools.partial(near_kernel, blocks, part, slots), shapes, [VMEM]...  1.45 us
  transfers between devices with their start and end apart: 24, of which 14 were waited for; matrix products, arithmetic and copies ran while one was open for 0% of the time, Pallas kernels for 6%

profile of v5, /device:TPU:0, one launch (start us, length us, event | category | flops | bytes accessed | tf_op | source)
XLA Modules:
  0.0 64.9 jit_solution(13238938326724442712)
XLA Ops:
  1.4 1.7 %shard_map.111 = (f32[128,128]{1,0:T(8,128)S(1)}, f32[520,128]{1,0:T(8,128)S(1)}, f32[520,128]{1,0:T(8,128)S(1)}, f32[520,128]{1,0:T(8,128)S(1)}, f32[520,128]{1,0:T(8,128)S(1)}) custom-call(s32[1]{0:T(128)} %bitcast.rep_at.here, s32[1]{0:T(128)} %bitcast.1.at_loop, s32[1]{0:T(128)S(6)} %copy.18.count, f32[512,128]{1,0:T(8,128)} %features.1, ...), custom_call_target="tpu_custom_call" | custom-call | bytes 2097152 | tf_op jit(solution)/shard_map/pallas_call | solution.py:298
  3.1 0.6 collective-permute-start
  3.6 2.6 %collective-permute-start.1 = (f32[520,128]{1,0:T(8,128)S(1)}, f32[520,128]{1,0:T(8,128)S(1)}, u32[]{:S(2)}, u32[]{:S(2)}) collective-permute-start(f32[520,128]{1,0:T(8,128)S(1)} %get-tuple-element.34), channel_id=1, source_target_pairs={{0,2},{1,3},{2,0},{3,1},{4,6},{5,7},{6,4},{7,5},{8,10},{9,11},{10,... | collective-permute-start | bytes 798728 | tf_op jit(solution)/shard_map/ppermute | solution.py:288
  6.2 0.0 collective-permute-start.2
  6.3 2.8 %collective-permute-start.3 = (f32[128,128]{1,0:T(8,128)S(1)}, f32[128,128]{1,0:T(8,128)S(1)}, u32[]{:S(2)}, u32[]{:S(2)}) collective-permute-start(f32[128,128]{1,0:T(8,128)S(1)} %get-tuple-element.38.refs_0_), channel_id=1, source_target_pairs={{0,16},{1,17},{2,18},{3,19},{4,20},{5,21},{6,22},{7,23},{8,24},{9,... | collective-permute-start | bytes 196616 | tf_op jit(solution)/shard_map/ppermute | solution.py:288
  9.1 1.5 %collective-permute-start.4 = (f32[128,128]{1,0:T(8,128)S(1)}, f32[128,128]{1,0:T(8,128)S(1)}, u32[]{:S(2)}, u32[]{:S(2)}) collective-permute-start(f32[128,128]{1,0:T(8,128)S(1)} %get-tuple-element.38.refs_0_), channel_id=1, source_target_pairs={{0,4},{1,9},{2,6},{3,11},{4,0},{5,13},{6,2},{7,15},{8,12},{9,1},{1... | collective-permute-start | bytes 196616 | tf_op jit(solution)/shard_map/ppermute | solution.py:288
  10.6 2.2 %collective-permute-done.3.refs_1_ = f32[128,128]{1,0:T(8,128)S(1)} collective-permute-done((f32[128,128]{1,0:T(8,128)S(1)}, f32[128,128]{1,0:T(8,128)S(1)}, u32[]{:S(2)}, u32[]{:S(2)}) %collective-permute-start.3) | collective-permute-done | bytes 65568 | tf_op jit(solution)/shard_map/ppermute | solution.py:288
  12.8 1.6 %collective-permute-start.5 = (f32[128,128]{1,0:T(8,128)S(1)}, f32[128,128]{1,0:T(8,128)S(1)}, u32[]{:S(2)}, u32[]{:S(2)}) collective-permute-start(f32[128,128]{1,0:T(8,128)S(1)} %collective-permute-done.3.refs_1_), channel_id=1, source_target_pairs={{0,4},{1,9},{2,6},{3,11},{4,0},{5,13},{6,2},{7,15},{8,12},{9,1},{1... | collective-permute-start | bytes 196616 | tf_op jit(solution)/shard_map/ppermute | solution.py:288
  14.4 1.1 %collective-permute-start.6 = (f32[256,128]{1,0:T(8,128)S(1)}, f32[256,128]{1,0:T(8,128)S(1)}, u32[]{:S(2)}, u32[]{:S(2)}) collective-permute-start(f32[256,128]{1,0:T(8,128)S(1)} %shard_map.114.refs_0_), channel_id=1, source_target_pairs={{0,8},{1,5},{2,10},{3,7},{4,12},{5,1},{6,14},{7,3},{8,0},{9,13},{1... | collective-permute-start | bytes 393224 | tf_op jit(solution)/shard_map/ppermute | solution.py:288
  15.5 2.3 %collective-permute-done.5.refs_1_ = f32[128,128]{1,0:T(8,128)S(1)} collective-permute-done((f32[128,128]{1,0:T(8,128)S(1)}, f32[128,128]{1,0:T(8,128)S(1)}, u32[]{:S(2)}, u32[]{:S(2)}) %collective-permute-start.5) | collective-permute-done | bytes 65568 | tf_op jit(solution)/shard_map/ppermute | solution.py:288
  17.8 1.2 %collective-permute-start.7 = (f32[256,128]{1,0:T(8,128)S(1)}, f32[256,128]{1,0:T(8,128)S(1)}, u32[]{:S(2)}, u32[]{:S(2)}) collective-permute-start(f32[256,128]{1,0:T(8,128)S(1)} %shard_map.115.refs_1_), channel_id=1, source_target_pairs={{0,8},{1,5},{2,10},{3,7},{4,12},{5,1},{6,14},{7,3},{8,0},{9,13},{1... | collective-permute-start | bytes 393224 | tf_op jit(solution)/shard_map/ppermute | solution.py:288
  19.0 1.5 %shard_map.112 = (f32[1024,512]{1,0:T(8,128)S(1)}, bf16[1024,512]{1,0:T(8,128)(2,1)S(1)}, bf16[1024,512]{1,0:T(8,128)(2,1)S(1)}) custom-call(f32[520,128]{1,0:T(8,128)S(1)} %get-tuple-element.29.refs_0_, f32[520,128]{1,0:T(8,128)S(1)} %collective-permute-done.refs_1_), custom_call_target="tpu_custom_call" | custom-call | bytes 8388608 | tf_op jit(solution)/shard_map/pallas_call | solution.py:333
  20.5 0.9 %shard_map.113 = (f32[1024,512]{1,0:T(8,128)S(1)}, bf16[1024,512]{1,0:T(8,128)(2,1)S(1)}, bf16[1024,512]{1,0:T(8,128)(2,1)S(1)}) custom-call(f32[1024,512]{1,0:T(8,128)S(1)} %get-tuple-element.31.refs_0_, bf16[1024,512]{1,0:T(8,128)(2,1)S(1)} %get-tuple-element.32.refs_1_, ...), custom_call_target="tpu_custom_call", output_to_operand_aliasing={{0}: (0, {}), {1}: (1, {}), {2}: (2, {})} | custom-call | bytes 8388608 | tf_op jit(solution)/shard_map/pallas_call | solution.py:341
  21.4 0.0 collective-permute-done.6.refs_2_
  21.4 1.4 %collective-permute-done.7.refs_3_ = f32[256,128]{1,0:T(8,128)S(1)} collective-permute-done((f32[256,128]{1,0:T(8,128)S(1)}, f32[256,128]{1,0:T(8,128)S(1)}, u32[]{:S(2)}, u32[]{:S(2)}) %collective-permute-start.7) | collective-permute-done | bytes 131104 | tf_op jit(solution)/shard_map/ppermute | solution.py:288
  22.8 0.7 %shard_map.116 = (f32[64,512]{1,0:T(8,128)S(1)}, f32[64,512]{1,0:T(8,128)S(1)}) custom-call(s32[1]{0:T(128)} %bitcast.rep_at.here, bf16[1024,512]{1,0:T(8,128)(2,1)S(1)} %get-tuple-element.36.high, bf16[1024,512]{1,0:T(8,128)(2,1)S(1)} %get-tuple-element.37.low, f32[256,128]{1,0:T(8,128)S(1)} %shard_map.114.refs_0_, f32[256,128]{1,0:T(8,128)S(1)} %shard_map.115.refs_1_, ...), custom_call_target="tpu_custom_call" | custom-call | flops 402653184 | bytes 4194304 | tf_op jit(solution)/shard_map/pallas_call | solution.py:351
  23.5 0.1 collective-permute-start.8
  23.6 1.3 %collective-permute-done.8.refs_1_ = f32[64,512]{1,0:T(8,128)S(1)} collective-permute-done((f32[64,512]{1,0:T(8,128)S(1)}, f32[64,512]{1,0:T(8,128)S(1)}, u32[]{:S(2)}, u32[]{:S(2)}) %collective-permute-start.8) | collective-permute-done | bytes 131104 | tf_op jit(solution)/shard_map/ppermute | solution.py:288
  25.0 1.7 %collective-permute-start.9 = (f32[64,512]{1,0:T(8,128)S(1)}, f32[64,512]{1,0:T(8,128)S(1)}, u32[]{:S(2)}, u32[]{:S(2)}) collective-permute-start(f32[64,512]{1,0:T(8,128)S(1)} %shard_map.117.refs_0_), channel_id=1, source_target_pairs={{0,2},{1,3},{2,0},{3,1},{4,6},{5,7},{6,4},{7,5},{8,10},{9,11},{10,... | collective-permute-start | bytes 393224 | tf_op jit(solution)/shard_map/ppermute | solution.py:288
  26.7 3.9 %collective-permute-done.9.refs_1_ = f32[64,512]{1,0:T(8,128)S(1)} collective-permute-done((f32[64,512]{1,0:T(8,128)S(1)}, f32[64,512]{1,0:T(8,128)S(1)}, u32[]{:S(2)}, u32[]{:S(2)}) %collective-permute-start.9) | collective-permute-done | bytes 131104 | tf_op jit(solution)/shard_map/ppermute | solution.py:288
  30.6 0.1 collective-permute-start.10
  30.7 1.3 %collective-permute-done.10.other = f32[64,512]{1,0:T(8,128)S(1)} collective-permute-done((f32[64,512]{1,0:T(8,128)S(1)}, f32[64,512]{1,0:T(8,128)S(1)}, u32[]{:S(2)}, u32[]{:S(2)}) %collective-permute-start.10) | collective-permute-done | bytes 131104 | tf_op jit(solution)/shard_map/ppermute | solution.py:288
  32.0 1.1 %shard_map.119 = (f32[256,128]{1,0:T(8,128)S(1)}, f32[512,256]{1,0:T(8,128)S(1)}, f32[512,256]{1,0:T(8,128)S(1)}, f32[32,512]{1,0:T(8,128)S(1)}, bf16[512,256]{1,0:T(8,128)(2,1)S(1)}) custom-call(s32[1]{0:T(128)} %bitcast.rep_at.here, bf16[1024,512]{1,0:T(8,128)(2,1)S(1)} %get-tuple-element.36.high, bf16[1024,512]{1,0:T(8,128)(2,1)S(1)} %get-tuple-element.37.low, ...), custom_call_target="tpu_custom_call" | custom-call | flops 134217728 | bytes 4194304 | tf_op jit(solution)/shard_map/pallas_call | solution.py:369
  33.2 1.2 %collective-permute-start.12 = (f32[256,128]{1,0:T(8,128)S(1)}, f32[256,128]{1,0:T(8,128)S(1)}, u32[]{:S(2)}, u32[]{:S(2)}) collective-permute-start(f32[256,128]{1,0:T(8,128)S(1)} %get-tuple-element.46), channel_id=1, source_target_pairs={{0,8},{1,5},{2,10},{3,7},{4,12},{5,1},{6,14},{7,3},{8,0},{9,13},{1... | collective-permute-start | bytes 393224 | tf_op jit(solution)/shard_map/ppermute | solution.py:288
  34.3 0.6 shard_map.121
  34.9 1.0 %collective-permute-start.11 = (f32[256,128]{1,0:T(8,128)S(1)}, f32[256,128]{1,0:T(8,128)S(1)}, u32[]{:S(2)}, u32[]{:S(2)}) collective-permute-start(f32[256,128]{1,0:T(8,128)S(1)} %get-tuple-element.44), channel_id=1, source_target_pairs={{0,8},{1,5},{2,10},{3,7},{4,12},{5,1},{6,14},{7,3},{8,0},{9,13},{1... | collective-permute-start | bytes 393224 | tf_op jit(solution)/shard_map/ppermute | solution.py:288
  35.9 2.3 %collective-permute-done.12.refs_1_ = f32[256,128]{1,0:T(8,128)S(1)} collective-permute-done((f32[256,128]{1,0:T(8,128)S(1)}, f32[256,128]{1,0:T(8,128)S(1)}, u32[]{:S(2)}, u32[]{:S(2)}) %collective-permute-start.12) | collective-permute-done | bytes 131104 | tf_op jit(solution)/shard_map/ppermute | solution.py:288
  38.2 1.7 %collective-permute-start.13 = (f32[256,128]{1,0:T(8,128)S(1)}, f32[256,128]{1,0:T(8,128)S(1)}, u32[]{:S(2)}, u32[]{:S(2)}) collective-permute-start(f32[256,128]{1,0:T(8,128)S(1)} %shard_map.123), channel_id=1, source_target_pairs={{0,4},{1,9},{2,6},{3,11},{4,0},{5,13},{6,2},{7,15},{8,12},{9,1},{1... | collective-permute-start | bytes 393224 | tf_op jit(solution)/shard_map/ppermute | solution.py:288
  39.9 0.1 collective-permute-done.11.refs_1_
  40.0 3.3 %collective-permute-done.13.refs_1_ = f32[256,128]{1,0:T(8,128)S(1)} collective-permute-done((f32[256,128]{1,0:T(8,128)S(1)}, f32[256,128]{1,0:T(8,128)S(1)}, u32[]{:S(2)}, u32[]{:S(2)}) %collective-permute-start.13) | collective-permute-done | bytes 131104 | tf_op jit(solution)/shard_map/ppermute | solution.py:288
  43.3 2.3 %collective-permute-start.14 = (f32[128,128]{1,0:T(8,128)S(1)}, f32[128,128]{1,0:T(8,128)S(1)}, u32[]{:S(2)}, u32[]{:S(2)}) collective-permute-start(f32[128,128]{1,0:T(8,128)S(1)} %get-tuple-element.48), channel_id=1, source_target_pairs={{0,16},{1,17},{2,18},{3,19},{4,20},{5,21},{6,22},{7,23},{8,24},{9,... | collective-permute-start | bytes 196616 | tf_op jit(solution)/shard_map/ppermute | solution.py:288
  45.6 0.2 shard_map.126.refs_0_
  45.8 0.7 %collective-permute-start.18 = (f32[72,128]{1,0:T(8,128)S(1)}, f32[72,128]{1,0:T(8,128)S(1)}, u32[]{:S(2)}, u32[]{:S(2)}) collective-permute-start(f32[72,128]{1,0:T(8,128)S(1)} %shard_map.126.refs_0_), channel_id=1, source_target_pairs={{0,16},{1,17},{2,18},{3,19},{4,20},{5,21},{6,22},{7,23},{8,24},{9,... | collective-permute-start | bytes 110600 | tf_op jit(solution)/shard_map/ppermute | solution.py:288
  46.6 4.2 %collective-permute-done.18.refs_1_ = f32[72,128]{1,0:T(8,128)S(1)} collective-permute-done((f32[72,128]{1,0:T(8,128)S(1)}, f32[72,128]{1,0:T(8,128)S(1)}, u32[]{:S(2)}, u32[]{:S(2)}) %collective-permute-start.18) | collective-permute-done | bytes 36896 | tf_op jit(solution)/shard_map/ppermute | solution.py:288
  50.7 1.5 %collective-permute-start.19 = (f32[72,128]{1,0:T(8,128)S(1)}, f32[72,128]{1,0:T(8,128)S(1)}, u32[]{:S(2)}, u32[]{:S(2)}) collective-permute-start(f32[72,128]{1,0:T(8,128)S(1)} %shard_map.127.refs_0_), channel_id=1, source_target_pairs={{0,4},{1,9},{2,6},{3,11},{4,0},{5,13},{6,2},{7,15},{8,12},{9,1},{1... | collective-permute-start | bytes 110600 | tf_op jit(solution)/shard_map/ppermute | solution.py:288
  52.3 1.6 %collective-permute-start.16 = (f32[128,128]{1,0:T(8,128)S(1)}, f32[128,128]{1,0:T(8,128)S(1)}, u32[]{:S(2)}, u32[]{:S(2)}) collective-permute-start(f32[128,128]{1,0:T(8,128)S(1)} %shard_map.125.refs_0_), channel_id=1, source_target_pairs={{0,2},{1,3},{2,0},{3,1},{4,6},{5,7},{6,4},{7,5},{8,10},{9,11},{10,... | collective-permute-start | bytes 196616 | tf_op jit(solution)/shard_map/ppermute | solution.py:288
  53.9 0.8 %collective-permute-done.19.refs_1_ = f32[72,128]{1,0:T(8,128)S(1)} collective-permute-done((f32[72,128]{1,0:T(8,128)S(1)}, f32[72,128]{1,0:T(8,128)S(1)}, u32[]{:S(2)}, u32[]{:S(2)}) %collective-permute-start.19) | collective-permute-done | bytes 36896 | tf_op jit(solution)/shard_map/ppermute | solution.py:288
  54.7 2.3 %collective-permute-start.20 = (f32[72,128]{1,0:T(8,128)S(1)}, f32[72,128]{1,0:T(8,128)S(1)}, u32[]{:S(2)}, u32[]{:S(2)}) collective-permute-start(f32[72,128]{1,0:T(8,128)S(1)} %shard_map.128.refs_0_), channel_id=1, source_target_pairs={{0,8},{1,5},{2,10},{3,7},{4,12},{5,1},{6,14},{7,3},{8,0},{9,13},{1... | collective-permute-start | bytes 110600 | tf_op jit(solution)/shard_map/ppermute | solution.py:288
  57.0 1.9 %collective-permute-done.20.refs_1_ = f32[72,128]{1,0:T(8,128)S(1)} collective-permute-done((f32[72,128]{1,0:T(8,128)S(1)}, f32[72,128]{1,0:T(8,128)S(1)}, u32[]{:S(2)}, u32[]{:S(2)}) %collective-permute-start.20) | collective-permute-done | bytes 36896 | tf_op jit(solution)/shard_map/ppermute | solution.py:288
  59.0 1.4 %collective-permute-start.22 = (f32[72,128]{1,0:T(8,128)S(1)}, f32[72,128]{1,0:T(8,128)S(1)}, u32[]{:S(2)}, u32[]{:S(2)}) collective-permute-start(f32[72,128]{1,0:T(8,128)S(1)} %shard_map.129.refs_4_), channel_id=1, source_target_pairs={{0,2},{1,3},{2,0},{3,1},{4,6},{5,7},{6,4},{7,5},{8,10},{9,11},{10,... | collective-permute-start | bytes 110600 | tf_op jit(solution)/shard_map/ppermute | solution.py:288
  60.4 0.0 collective-permute-start.15
  60.4 0.0 collective-permute-done.16.refs_2_
  60.4 0.5 collective-permute-start.17
  60.9 0.0 collective-permute-start.21
  60.9 2.1 %collective-permute-done.22.refs_6_ = f32[72,128]{1,0:T(8,128)S(1)} collective-permute-done((f32[72,128]{1,0:T(8,128)S(1)}, f32[72,128]{1,0:T(8,128)S(1)}, u32[]{:S(2)}, u32[]{:S(2)}) %collective-permute-start.22) | collective-permute-done | bytes 36896 | tf_op jit(solution)/shard_map/ppermute | solution.py:288
  62.9 0.8 %shard_map.120 = f32[512,256]{1,0:T(8,128)} custom-call(f32[512,256]{1,0:T(8,128)S(1)} %get-tuple-element.41.refs_0_), custom_call_target="tpu_custom_call" | custom-call | bytes 1048576 | tf_op jit(solution)/shard_map/pallas_call | solution.py:292
  63.8 0.4 collective-permute-done.23.refs_7_
  64.2 0.8 %shard_map.130 = (f32[512,128]{1,0:T(8,128)}, f32[128,256]{1,0:T(8,128)}, f32[1,256]{1,0:T(1,128)}) custom-call(s32[1]{0:T(128)} %bitcast.rep_at.here, f32[128,128]{1,0:T(8,128)S(1)} %shard_map.125.refs_0_, f32[128,128]{1,0:T(8,128)S(1)} %collective-permute-done.15.refs_1_, f32[128,128]{1,0:T(8,128)S(1)} %collective-permute-done.16.refs_2_, ...), custom_call_target="tpu_custom_call" | custom-call | bytes 524288 | tf_op jit(solution)/shard_map/pallas_call | solution.py:423
  (26 shorter events, 0.2 us)
Async XLA Ops:
  0.6 19.8 %copy-start.2 = (f32[256]{0:T(256)S(1)}, f32[256]{0:T(256)}, u32[]{:S(2)}) copy-start(f32[256]{0:T(256)} %param.10) | copy-start | bytes 3076
  0.6 19.8 %copy-start = (f32[512,256]{1,0:T(8,128)S(1)}, f32[512,256]{1,0:T(8,128)}, u32[]{:S(2)}) copy-start(f32[512,256]{1,0:T(8,128)} %cotangent.1) | copy-start | bytes 1572868
  0.7 19.8 %copy-start.1 = (f32[128,256]{1,0:T(8,128)S(1)}, f32[128,256]{1,0:T(8,128)}, u32[]{:S(2)}) copy-start(f32[128,256]{1,0:T(8,128)} %weight.1) | copy-start | bytes 393220
  3.1 15.9 %collective-permute-start = (f32[520,128]{1,0:T(8,128)S(1)}, f32[520,128]{1,0:T(8,128)S(1)}, u32[]{:S(2)}, u32[]{:S(2)}) collective-permute-start(f32[520,128]{1,0:T(8,128)S(1)} %get-tuple-element.30), channel_id=1, source_target_pairs={{0,1},{1,0},{2,3},{3,2},{4,5},{5,4},{6,7},{7,6},{8,9},{9,8},{10,11... | collective-permute-start | bytes 798728 | tf_op jit(solution)/shard_map/ppermute | solution.py:288
  3.6 16.8 %collective-permute-start.1 = (f32[520,128]{1,0:T(8,128)S(1)}, f32[520,128]{1,0:T(8,128)S(1)}, u32[]{:S(2)}, u32[]{:S(2)}) collective-permute-start(f32[520,128]{1,0:T(8,128)S(1)} %get-tuple-element.34), channel_id=1, source_target_pairs={{0,2},{1,3},{2,0},{3,1},{4,6},{5,7},{6,4},{7,5},{8,10},{9,11},{10,... | collective-permute-start | bytes 798728 | tf_op jit(solution)/shard_map/ppermute | solution.py:288
  6.2 14.2 %collective-permute-start.2 = (f32[520,128]{1,0:T(8,128)S(1)}, f32[520,128]{1,0:T(8,128)S(1)}, u32[]{:S(2)}, u32[]{:S(2)}) collective-permute-start(f32[520,128]{1,0:T(8,128)S(1)} %get-tuple-element.35), channel_id=1, source_target_pairs={{0,3},{1,2},{2,1},{3,0},{4,7},{5,6},{6,5},{7,4},{8,11},{9,10},{10,... | collective-permute-start | bytes 798728 | tf_op jit(solution)/shard_map/ppermute | solution.py:288
  6.3 6.5 %collective-permute-start.3 = (f32[128,128]{1,0:T(8,128)S(1)}, f32[128,128]{1,0:T(8,128)S(1)}, u32[]{:S(2)}, u32[]{:S(2)}) collective-permute-start(f32[128,128]{1,0:T(8,128)S(1)} %get-tuple-element.38.refs_0_), channel_id=1, source_target_pairs={{0,16},{1,17},{2,18},{3,19},{4,20},{5,21},{6,22},{7,23},{8,24},{9,... | collective-permute-start | bytes 196616 | tf_op jit(solution)/shard_map/ppermute | solution.py:288
  9.1 5.4 %collective-permute-start.4 = (f32[128,128]{1,0:T(8,128)S(1)}, f32[128,128]{1,0:T(8,128)S(1)}, u32[]{:S(2)}, u32[]{:S(2)}) collective-permute-start(f32[128,128]{1,0:T(8,128)S(1)} %get-tuple-element.38.refs_0_), channel_id=1, source_target_pairs={{0,4},{1,9},{2,6},{3,11},{4,0},{5,13},{6,2},{7,15},{8,12},{9,1},{1... | collective-permute-start | bytes 196616 | tf_op jit(solution)/shard_map/ppermute | solution.py:288
  12.8 5.0 %collective-permute-start.5 = (f32[128,128]{1,0:T(8,128)S(1)}, f32[128,128]{1,0:T(8,128)S(1)}, u32[]{:S(2)}, u32[]{:S(2)}) collective-permute-start(f32[128,128]{1,0:T(8,128)S(1)} %collective-permute-done.3.refs_1_), channel_id=1, source_target_pairs={{0,4},{1,9},{2,6},{3,11},{4,0},{5,13},{6,2},{7,15},{8,12},{9,1},{1... | collective-permute-start | bytes 196616 | tf_op jit(solution)/shard_map/ppermute | solution.py:288
  14.4 7.0 %collective-permute-start.6 = (f32[256,128]{1,0:T(8,128)S(1)}, f32[256,128]{1,0:T(8,128)S(1)}, u32[]{:S(2)}, u32[]{:S(2)}) collective-permute-start(f32[256,128]{1,0:T(8,128)S(1)} %shard_map.114.refs_0_), channel_id=1, source_target_pairs={{0,8},{1,5},{2,10},{3,7},{4,12},{5,1},{6,14},{7,3},{8,0},{9,13},{1... | collective-permute-start | bytes 393224 | tf_op jit(solution)/shard_map/ppermute | solution.py:288
  17.8 5.0 %collective-permute-start.7 = (f32[256,128]{1,0:T(8,128)S(1)}, f32[256,128]{1,0:T(8,128)S(1)}, u32[]{:S(2)}, u32[]{:S(2)}) collective-permute-start(f32[256,128]{1,0:T(8,128)S(1)} %shard_map.115.refs_1_), channel_id=1, source_target_pairs={{0,8},{1,5},{2,10},{3,7},{4,12},{5,1},{6,14},{7,3},{8,0},{9,13},{1... | collective-permute-start | bytes 393224 | tf_op jit(solution)/shard_map/ppermute | solution.py:288
  23.5 1.4 %collective-permute-start.8 = (f32[64,512]{1,0:T(8,128)S(1)}, f32[64,512]{1,0:T(8,128)S(1)}, u32[]{:S(2)}, u32[]{:S(2)}) collective-permute-start(f32[64,512]{1,0:T(8,128)S(1)} %get-tuple-element.40), channel_id=1, source_target_pairs={{0,1},{1,0},{2,3},{3,2},{4,5},{5,4},{6,7},{7,6},{8,9},{9,8},{10,11... | collective-permute-start | bytes 393224 | tf_op jit(solution)/shard_map/ppermute | solution.py:288
  25.0 5.6 %collective-permute-start.9 = (f32[64,512]{1,0:T(8,128)S(1)}, f32[64,512]{1,0:T(8,128)S(1)}, u32[]{:S(2)}, u32[]{:S(2)}) collective-permute-start(f32[64,512]{1,0:T(8,128)S(1)} %shard_map.117.refs_0_), channel_id=1, source_target_pairs={{0,2},{1,3},{2,0},{3,1},{4,6},{5,7},{6,4},{7,5},{8,10},{9,11},{10,... | collective-permute-start | bytes 393224 | tf_op jit(solution)/shard_map/ppermute | solution.py:288
  30.6 1.4 %collective-permute-start.10 = (f32[64,512]{1,0:T(8,128)S(1)}, f32[64,512]{1,0:T(8,128)S(1)}, u32[]{:S(2)}, u32[]{:S(2)}) collective-permute-start(f32[64,512]{1,0:T(8,128)S(1)} %shard_map.118.mine), channel_id=1, source_target_pairs={{0,1},{1,0},{2,3},{3,2},{4,5},{5,4},{6,7},{7,6},{8,9},{9,8},{10,11... | collective-permute-start | bytes 393224 | tf_op jit(solution)/shard_map/ppermute | solution.py:288
  33.2 5.0 %collective-permute-start.12 = (f32[256,128]{1,0:T(8,128)S(1)}, f32[256,128]{1,0:T(8,128)S(1)}, u32[]{:S(2)}, u32[]{:S(2)}) collective-permute-start(f32[256,128]{1,0:T(8,128)S(1)} %get-tuple-element.46), channel_id=1, source_target_pairs={{0,8},{1,5},{2,10},{3,7},{4,12},{5,1},{6,14},{7,3},{8,0},{9,13},{1... | collective-permute-start | bytes 393224 | tf_op jit(solution)/shard_map/ppermute | solution.py:288
  34.9 5.0 %collective-permute-start.11 = (f32[256,128]{1,0:T(8,128)S(1)}, f32[256,128]{1,0:T(8,128)S(1)}, u32[]{:S(2)}, u32[]{:S(2)}) collective-permute-start(f32[256,128]{1,0:T(8,128)S(1)} %get-tuple-element.44), channel_id=1, source_target_pairs={{0,8},{1,5},{2,10},{3,7},{4,12},{5,1},{6,14},{7,3},{8,0},{9,13},{1... | collective-permute-start | bytes 393224 | tf_op jit(solution)/shard_map/ppermute | solution.py:288
  38.2 5.0 %collective-permute-start.13 = (f32[256,128]{1,0:T(8,128)S(1)}, f32[256,128]{1,0:T(8,128)S(1)}, u32[]{:S(2)}, u32[]{:S(2)}) collective-permute-start(f32[256,128]{1,0:T(8,128)S(1)} %shard_map.123), channel_id=1, source_target_pairs={{0,4},{1,9},{2,6},{3,11},{4,0},{5,13},{6,2},{7,15},{8,12},{9,1},{1... | collective-permute-start | bytes 393224 | tf_op jit(solution)/shard_map/ppermute | solution.py:288
  43.3 9.0 %collective-permute-start.14 = (f32[128,128]{1,0:T(8,128)S(1)}, f32[128,128]{1,0:T(8,128)S(1)}, u32[]{:S(2)}, u32[]{:S(2)}) collective-permute-start(f32[128,128]{1,0:T(8,128)S(1)} %get-tuple-element.48), channel_id=1, source_target_pairs={{0,16},{1,17},{2,18},{3,19},{4,20},{5,21},{6,22},{7,23},{8,24},{9,... | collective-permute-start | bytes 196616 | tf_op jit(solution)/shard_map/ppermute | solution.py:288
  45.8 4.9 %collective-permute-start.18 = (f32[72,128]{1,0:T(8,128)S(1)}, f32[72,128]{1,0:T(8,128)S(1)}, u32[]{:S(2)}, u32[]{:S(2)}) collective-permute-start(f32[72,128]{1,0:T(8,128)S(1)} %shard_map.126.refs_0_), channel_id=1, source_target_pairs={{0,16},{1,17},{2,18},{3,19},{4,20},{5,21},{6,22},{7,23},{8,24},{9,... | collective-permute-start | bytes 110600 | tf_op jit(solution)/shard_map/ppermute | solution.py:288
  50.7 4.0 %collective-permute-start.19 = (f32[72,128]{1,0:T(8,128)S(1)}, f32[72,128]{1,0:T(8,128)S(1)}, u32[]{:S(2)}, u32[]{:S(2)}) collective-permute-start(f32[72,128]{1,0:T(8,128)S(1)} %shard_map.127.refs_0_), channel_id=1, source_target_pairs={{0,4},{1,9},{2,6},{3,11},{4,0},{5,13},{6,2},{7,15},{8,12},{9,1},{1... | collective-permute-start | bytes 110600 | tf_op jit(solution)/shard_map/ppermute | solution.py:288
  52.3 8.1 %collective-permute-start.16 = (f32[128,128]{1,0:T(8,128)S(1)}, f32[128,128]{1,0:T(8,128)S(1)}, u32[]{:S(2)}, u32[]{:S(2)}) collective-permute-start(f32[128,128]{1,0:T(8,128)S(1)} %shard_map.125.refs_0_), channel_id=1, source_target_pairs={{0,2},{1,3},{2,0},{3,1},{4,6},{5,7},{6,4},{7,5},{8,10},{9,11},{10,... | collective-permute-start | bytes 196616 | tf_op jit(solution)/shard_map/ppermute | solution.py:288
  54.7 4.3 %collective-permute-start.20 = (f32[72,128]{1,0:T(8,128)S(1)}, f32[72,128]{1,0:T(8,128)S(1)}, u32[]{:S(2)}, u32[]{:S(2)}) collective-permute-start(f32[72,128]{1,0:T(8,128)S(1)} %shard_map.128.refs_0_), channel_id=1, source_target_pairs={{0,8},{1,5},{2,10},{3,7},{4,12},{5,1},{6,14},{7,3},{8,0},{9,13},{1... | collective-permute-start | bytes 110600 | tf_op jit(solution)/shard_map/ppermute | solution.py:288
  59.0 4.0 %collective-permute-start.22 = (f32[72,128]{1,0:T(8,128)S(1)}, f32[72,128]{1,0:T(8,128)S(1)}, u32[]{:S(2)}, u32[]{:S(2)}) collective-permute-start(f32[72,128]{1,0:T(8,128)S(1)} %shard_map.129.refs_4_), channel_id=1, source_target_pairs={{0,2},{1,3},{2,0},{3,1},{4,6},{5,7},{6,4},{7,5},{8,10},{9,11},{10,... | collective-permute-start | bytes 110600 | tf_op jit(solution)/shard_map/ppermute | solution.py:288
  60.4 3.8 %collective-permute-start.15 = (f32[128,128]{1,0:T(8,128)S(1)}, f32[128,128]{1,0:T(8,128)S(1)}, u32[]{:S(2)}, u32[]{:S(2)}) collective-permute-start(f32[128,128]{1,0:T(8,128)S(1)} %shard_map.125.refs_0_), channel_id=1, source_target_pairs={{0,1},{1,0},{2,3},{3,2},{4,5},{5,4},{6,7},{7,6},{8,9},{9,8},{10,11... | collective-permute-start | bytes 196616 | tf_op jit(solution)/shard_map/ppermute | solution.py:288
  60.4 3.8 %collective-permute-start.17 = (f32[128,128]{1,0:T(8,128)S(1)}, f32[128,128]{1,0:T(8,128)S(1)}, u32[]{:S(2)}, u32[]{:S(2)}) collective-permute-start(f32[128,128]{1,0:T(8,128)S(1)} %collective-permute-done.16.refs_2_), channel_id=1, source_target_pairs={{0,1},{1,0},{2,3},{3,2},{4,5},{5,4},{6,7},{7,6},{8,9},{9,8},{10,11... | collective-permute-start | bytes 196616 | tf_op jit(solution)/shard_map/ppermute | solution.py:288
  60.9 2.9 %collective-permute-start.21 = (f32[72,128]{1,0:T(8,128)S(1)}, f32[72,128]{1,0:T(8,128)S(1)}, u32[]{:S(2)}, u32[]{:S(2)}) collective-permute-start(f32[72,128]{1,0:T(8,128)S(1)} %shard_map.129.refs_4_), channel_id=1, source_target_pairs={{0,1},{1,0},{2,3},{3,2},{4,5},{5,4},{6,7},{7,6},{8,9},{9,8},{10,11... | collective-permute-start | bytes 110600 | tf_op jit(solution)/shard_map/ppermute | solution.py:288
  62.9 1.2 %collective-permute-start.23 = (f32[72,128]{1,0:T(8,128)S(1)}, f32[72,128]{1,0:T(8,128)S(1)}, u32[]{:S(2)}, u32[]{:S(2)}) collective-permute-start(f32[72,128]{1,0:T(8,128)S(1)} %collective-permute-done.22.refs_6_), channel_id=1, source_target_pairs={{0,1},{1,0},{2,3},{3,2},{4,5},{5,4},{6,7},{7,6},{8,9},{9,8},{10,11... | collective-permute-start | bytes 110600 | tf_op jit(solution)/shard_map/ppermute | solution.py:288

commit v6 on v5

--- a/solution.py
+++ b/solution.py
@@ -246,22 +246,24 @@
     )(*mine, *theirs)
 
 
-def final_kernel(reps, blocks, part, piece, here, *refs):
-    parts, weights = refs[:reps], refs[reps : 2 * reps]
-    grad_features, grad_weight, grad_bias = refs[2 * reps :]
+def features_kernel(reps, blocks, part, here, *refs):
+    grad_features = refs[reps]
     side = grad_features.shape[0] // blocks
+    for d in range(reps):
+        for b in range(blocks):
+            at = pl.ds(pl.multiple_of(b * side + (here[0] ^ d) * part, 8), part)
+            grad_features[at, :] = refs[d][pl.ds(b * part, part), :]
+
+
+def weights_kernel(reps, piece, here, *refs):
+    grad_weight, grad_bias = refs[reps:]
     groups = grad_weight.shape[1] // LANES
-    for d in range(reps):
-        q = here[0] ^ d
-        for b in range(blocks):
-            at = pl.ds(pl.multiple_of(b * side + q * part, 8), part)
-            grad_features[at, :] = parts[d][pl.ds(b * part, part), :]
-        at = pl.ds(pl.multiple_of(q * piece, 8), piece)
-        for g in range(groups):
-            grad_weight[at, pl.ds(g * LANES, LANES)] = weights[d][pl.ds(g * piece, piece), :]
     for g in range(groups):
-        row = weights[0][pl.ds(groups * piece + g, 1), :]
-        grad_bias[:, pl.ds(g * LANES, LANES)] = row
+        lane = pl.ds(g * LANES, LANES)
+        for d in range(reps):
+            at = pl.ds(pl.multiple_of((here[0] ^ d) * piece, 8), piece)
+            grad_weight[at, lane] = refs[d][pl.ds(g * piece, piece), :]
+        grad_bias[:, lane] = refs[0][pl.ds(groups * piece + g, 1), :]
 
 
 def per_device(features, weight, bias, tile_values, tile_rows, tile_cols, tile_count, cotangent):
@@ -293,7 +295,7 @@
             join_kernel, [shape], [VMEM] * len(arrays), [], 0, 8 * shape[0] * shape[1]
         )(*arrays)[0]
 
-    chunks = 4 if slots % 4 == 0 else 1
+    chunks = 8 if slots % 8 == 0 else 1
     sources = (features, tile_values, tile_rows[None], tile_cols[None])
     own, *parcels = call(
         functools.partial(pack_kernel, reps, loops, blocks, part),
@@ -365,6 +367,8 @@
 
     even = range(0, loops, 2)
     on, stay = [k for k in even if k & 2], [k for k in even if not k & 2]
+    on.sort(key=lambda k: (not k & 4, k))
+    stay.sort(key=lambda k: (not k & 4, k))
     groups = [[k | 1 for k in on], [k | 1 for k in stay], on, stay]
     first, output, grads, piece_t, right = call(
         functools.partial(dense_kernel, blocks, groups[0], size),
@@ -391,12 +395,20 @@
     )(piece_t, grads)
 
     grad_term = swap(grad, "loop", loops // 2)
-    (going,) = add([on_own], [on_term])
+    cut = size * sum(1 for k in on if k & 4)
+    cuts = [[(0, 0, 0, cut)], [(0, cut, cut, len(on) * size - cut)]]
+    going, later = add([on_own], [on_term], cuts)
     term = swap(going, "loop", 2)
+    later_term = swap(later, "loop", 2)
     (grad,) = add([grad], [grad_term])
     grad_term = swap(grad, "loop", 2)
-    (held,) = add([stay_own], [stay_term])
-    bit, rest = 2, stay
+    going, held = add([stay_own], [stay_term], cuts)
+    (going,) = add([going], [term])
+    term = swap(going, "loop", 4)
+    (held,) = add([held], [later_term])
+    (grad,) = add([grad], [grad_term])
+    grad_term = swap(grad, "loop", 1)
+    bit, rest = 4, [k for k in stay if not k & 4]
     while bit < loops // 2:
         ahead = [(0, n * size, n * size, size) for n, k in enumerate(rest) if k & (2 * bit)]
         behind = [(0, n * size, n * size, size) for n, k in enumerate(rest) if not k & (2 * bit)]
@@ -404,7 +416,7 @@
         going, held = add([held], [term], [ahead, behind])
         term = swap(going, "loop", 2 * bit)
         (grad,) = add([grad], [grad_term])
-        grad_term = swap(grad, "loop", bit if bit > 2 else 1)
+        grad_term = swap(grad, "loop", bit)
         bit *= 2
     (mine,) = add([held], [term])
     (grad,) = add([grad], [grad_term])
@@ -420,14 +432,22 @@
 
     parts, weights = spread(mine), spread(grad)
     output = join(output)
-    grad_features, grad_weight, grad_bias = call(
-        functools.partial(final_kernel, reps, blocks, part, piece),
-        [(total, width), (width, wide), (1, wide)],
-        [SMEM] + [VMEM] * (2 * reps),
+    (grad_features,) = call(
+        functools.partial(features_kernel, reps, blocks, part),
+        [(total, width)],
+        [SMEM] + [VMEM] * reps,
         [],
         0,
         2 * total * width * 4,
-    )(here, *parts, *weights)
+    )(here, *parts)
+    grad_weight, grad_bias = call(
+        functools.partial(weights_kernel, reps, piece),
+        [(width, wide), (1, wide)],
+        [SMEM] + [VMEM] * reps,
+        [],
+        0,
+        2 * width * wide * 4,
+    )(here, *weights)
     return (output, grad_features, grad_weight, grad_bias.reshape(wide))
 
 

time: 65.1 us -> 65.2 us (level)
  waiting for transfers between devices: 27.6 us -> 26.2 us
  Pallas kernels: 8.43 us -> 9.38 us
    ppermute x24 -> x25, waiting for transfers between devices: 27.6 us -> 26.2 us  [swap(): return lax.ppermute(x, ('loop', 'rep'), pairs)]
    pallas_call x1 -> x2, Pallas kernels: 0.78 us -> 1.4 us  [the longest x1 0.72 us: per_device(): call(functools.partial(features_kernel, reps, blocks, part), [(total, wid...]
    ppermute x24 -> x25, starting transfers between devices: 27.4 us -> 27.8 us  [swap(): return lax.ppermute(x, ('loop', 'rep'), pairs)]
  transfers between devices with their start and end apart: 24 -> 25, of which waited for: 14 -> 13; matrix products, arithmetic and copies ran while one was open for 0% -> 0% of each run, Pallas kernels for 6% -> 7%
where the time goes in v6:
time: 65.2 us; the launch traced here: 65 us
  starting transfers between devices  27.8 us (43%)
  waiting for transfers between devices  26.2 us (40%)
  Pallas kernels  9.38 us (14%)
  between operations  1.56 us (2%)
    ppermute x25, starting transfers between devices, swap(): return lax.ppermute(x, ('loop', 'rep'), pairs)  27.8 us
    ppermute x25, waiting for transfers between devices, swap(): return lax.ppermute(x, ('loop', 'rep'), pairs)  26.2 us
    pallas_call x1, Pallas kernels, per_device(): call(functools.partial(pack_kernel, reps, loops, blocks, part), [(size, w...  2.01 us
    pallas_call x1, Pallas kernels, per_device(): call(functools.partial(near_kernel, blocks, part, slots), shapes, [VMEM]...  1.45 us
  transfers between devices with their start and end apart: 25, of which 13 were waited for; matrix products, arithmetic and copies ran while one was open for 0% of the time, Pallas kernels for 7%

profile of v6, /device:TPU:0, one launch (start us, length us, event | category | flops | bytes accessed | tf_op | source)
XLA Modules:
  0.0 65.0 jit_solution(16235519142124632982)
XLA Ops:
  1.4 2.0 %shard_map.111 = (f32[128,128]{1,0:T(8,128)S(1)}, f32[520,128]{1,0:T(8,128)S(1)}, f32[520,128]{1,0:T(8,128)S(1)}, f32[520,128]{1,0:T(8,128)S(1)}, f32[520,128]{1,0:T(8,128)S(1)}) custom-call(s32[1]{0:T(128)} %bitcast.rep_at.here, s32[1]{0:T(128)} %bitcast.1.at_loop, s32[1]{0:T(128)S(6)} %copy.18.count, f32[512,128]{1,0:T(8,128)} %features.1, ...), custom_call_target="tpu_custom_call" | custom-call | bytes 2097152 | tf_op jit(solution)/shard_map/pallas_call | solution.py:300
  3.4 0.6 collective-permute-start
  4.0 2.6 %collective-permute-start.1 = (f32[520,128]{1,0:T(8,128)S(1)}, f32[520,128]{1,0:T(8,128)S(1)}, u32[]{:S(2)}, u32[]{:S(2)}) collective-permute-start(f32[520,128]{1,0:T(8,128)S(1)} %get-tuple-element.35), channel_id=1, source_target_pairs={{0,2},{1,3},{2,0},{3,1},{4,6},{5,7},{6,4},{7,5},{8,10},{9,11},{10,... | collective-permute-start | bytes 798728 | tf_op jit(solution)/shard_map/ppermute | solution.py:290
  6.6 0.0 collective-permute-start.2
  6.6 2.8 %collective-permute-start.3 = (f32[128,128]{1,0:T(8,128)S(1)}, f32[128,128]{1,0:T(8,128)S(1)}, u32[]{:S(2)}, u32[]{:S(2)}) collective-permute-start(f32[128,128]{1,0:T(8,128)S(1)} %get-tuple-element.39.refs_0_), channel_id=1, source_target_pairs={{0,16},{1,17},{2,18},{3,19},{4,20},{5,21},{6,22},{7,23},{8,24},{9,... | collective-permute-start | bytes 196616 | tf_op jit(solution)/shard_map/ppermute | solution.py:290
  9.4 1.5 %collective-permute-start.4 = (f32[128,128]{1,0:T(8,128)S(1)}, f32[128,128]{1,0:T(8,128)S(1)}, u32[]{:S(2)}, u32[]{:S(2)}) collective-permute-start(f32[128,128]{1,0:T(8,128)S(1)} %get-tuple-element.39.refs_0_), channel_id=1, source_target_pairs={{0,4},{1,9},{2,6},{3,11},{4,0},{5,13},{6,2},{7,15},{8,12},{9,1},{1... | collective-permute-start | bytes 196616 | tf_op jit(solution)/shard_map/ppermute | solution.py:290
  10.9 2.2 %collective-permute-done.3.refs_1_ = f32[128,128]{1,0:T(8,128)S(1)} collective-permute-done((f32[128,128]{1,0:T(8,128)S(1)}, f32[128,128]{1,0:T(8,128)S(1)}, u32[]{:S(2)}, u32[]{:S(2)}) %collective-permute-start.3) | collective-permute-done | bytes 65568 | tf_op jit(solution)/shard_map/ppermute | solution.py:290
  13.1 1.6 %collective-permute-start.5 = (f32[128,128]{1,0:T(8,128)S(1)}, f32[128,128]{1,0:T(8,128)S(1)}, u32[]{:S(2)}, u32[]{:S(2)}) collective-permute-start(f32[128,128]{1,0:T(8,128)S(1)} %collective-permute-done.3.refs_1_), channel_id=1, source_target_pairs={{0,4},{1,9},{2,6},{3,11},{4,0},{5,13},{6,2},{7,15},{8,12},{9,1},{1... | collective-permute-start | bytes 196616 | tf_op jit(solution)/shard_map/ppermute | solution.py:290
  14.7 0.0 collective-permute-done.4.refs_0_
  14.8 1.1 %collective-permute-start.6 = (f32[256,128]{1,0:T(8,128)S(1)}, f32[256,128]{1,0:T(8,128)S(1)}, u32[]{:S(2)}, u32[]{:S(2)}) collective-permute-start(f32[256,128]{1,0:T(8,128)S(1)} %shard_map.114.refs_0_), channel_id=1, source_target_pairs={{0,8},{1,5},{2,10},{3,7},{4,12},{5,1},{6,14},{7,3},{8,0},{9,13},{1... | collective-permute-start | bytes 393224 | tf_op jit(solution)/shard_map/ppermute | solution.py:290
  15.8 2.3 %collective-permute-done.5.refs_1_ = f32[128,128]{1,0:T(8,128)S(1)} collective-permute-done((f32[128,128]{1,0:T(8,128)S(1)}, f32[128,128]{1,0:T(8,128)S(1)}, u32[]{:S(2)}, u32[]{:S(2)}) %collective-permute-start.5) | collective-permute-done | bytes 65568 | tf_op jit(solution)/shard_map/ppermute | solution.py:290
  18.1 1.2 %collective-permute-start.7 = (f32[256,128]{1,0:T(8,128)S(1)}, f32[256,128]{1,0:T(8,128)S(1)}, u32[]{:S(2)}, u32[]{:S(2)}) collective-permute-start(f32[256,128]{1,0:T(8,128)S(1)} %shard_map.115.refs_1_), channel_id=1, source_target_pairs={{0,8},{1,5},{2,10},{3,7},{4,12},{5,1},{6,14},{7,3},{8,0},{9,13},{1... | collective-permute-start | bytes 393224 | tf_op jit(solution)/shard_map/ppermute | solution.py:290
  19.3 0.0 collective-permute-done.refs_1_
  19.3 1.5 %shard_map.112 = (f32[1024,512]{1,0:T(8,128)S(1)}, bf16[1024,512]{1,0:T(8,128)(2,1)S(1)}, bf16[1024,512]{1,0:T(8,128)(2,1)S(1)}) custom-call(f32[520,128]{1,0:T(8,128)S(1)} %get-tuple-element.30.refs_0_, f32[520,128]{1,0:T(8,128)S(1)} %collective-permute-done.refs_1_), custom_call_target="tpu_custom_call" | custom-call | bytes 8388608 | tf_op jit(solution)/shard_map/pallas_call | solution.py:335
  20.8 0.9 %shard_map.113 = (f32[1024,512]{1,0:T(8,128)S(1)}, bf16[1024,512]{1,0:T(8,128)(2,1)S(1)}, bf16[1024,512]{1,0:T(8,128)(2,1)S(1)}) custom-call(f32[1024,512]{1,0:T(8,128)S(1)} %get-tuple-element.32.refs_0_, bf16[1024,512]{1,0:T(8,128)(2,1)S(1)} %get-tuple-element.33.refs_1_, ...), custom_call_target="tpu_custom_call", output_to_operand_aliasing={{0}: (0, {}), {1}: (1, {}), {2}: (2, {})} | custom-call | bytes 8388608 | tf_op jit(solution)/shard_map/pallas_call | solution.py:343
  21.7 1.4 %collective-permute-done.7.refs_3_ = f32[256,128]{1,0:T(8,128)S(1)} collective-permute-done((f32[256,128]{1,0:T(8,128)S(1)}, f32[256,128]{1,0:T(8,128)S(1)}, u32[]{:S(2)}, u32[]{:S(2)}) %collective-permute-start.7) | collective-permute-done | bytes 131104 | tf_op jit(solution)/shard_map/ppermute | solution.py:290
  23.1 0.7 %shard_map.116 = (f32[64,512]{1,0:T(8,128)S(1)}, f32[64,512]{1,0:T(8,128)S(1)}) custom-call(s32[1]{0:T(128)} %bitcast.rep_at.here, bf16[1024,512]{1,0:T(8,128)(2,1)S(1)} %get-tuple-element.37.high, bf16[1024,512]{1,0:T(8,128)(2,1)S(1)} %get-tuple-element.38.low, f32[256,128]{1,0:T(8,128)S(1)} %shard_map.114.refs_0_, f32[256,128]{1,0:T(8,128)S(1)} %shard_map.115.refs_1_, ...), custom_call_target="tpu_custom_call" | custom-call | flops 402653184 | bytes 4194304 | tf_op jit(solution)/shard_map/pallas_call | solution.py:353
  23.9 0.1 collective-permute-start.8
  23.9 1.3 %collective-permute-done.8.refs_1_ = f32[64,512]{1,0:T(8,128)S(1)} collective-permute-done((f32[64,512]{1,0:T(8,128)S(1)}, f32[64,512]{1,0:T(8,128)S(1)}, u32[]{:S(2)}, u32[]{:S(2)}) %collective-permute-start.8) | collective-permute-done | bytes 131104 | tf_op jit(solution)/shard_map/ppermute | solution.py:290
  25.3 1.7 %collective-permute-start.9 = (f32[64,512]{1,0:T(8,128)S(1)}, f32[64,512]{1,0:T(8,128)S(1)}, u32[]{:S(2)}, u32[]{:S(2)}) collective-permute-start(f32[64,512]{1,0:T(8,128)S(1)} %shard_map.117.refs_0_), channel_id=1, source_target_pairs={{0,2},{1,3},{2,0},{3,1},{4,6},{5,7},{6,4},{7,5},{8,10},{9,11},{10,... | collective-permute-start | bytes 393224 | tf_op jit(solution)/shard_map/ppermute | solution.py:290
  27.0 3.9 %collective-permute-done.9.refs_1_ = f32[64,512]{1,0:T(8,128)S(1)} collective-permute-done((f32[64,512]{1,0:T(8,128)S(1)}, f32[64,512]{1,0:T(8,128)S(1)}, u32[]{:S(2)}, u32[]{:S(2)}) %collective-permute-start.9) | collective-permute-done | bytes 131104 | tf_op jit(solution)/shard_map/ppermute | solution.py:290
  30.9 0.1 collective-permute-start.10
  31.0 1.3 %collective-permute-done.10.other = f32[64,512]{1,0:T(8,128)S(1)} collective-permute-done((f32[64,512]{1,0:T(8,128)S(1)}, f32[64,512]{1,0:T(8,128)S(1)}, u32[]{:S(2)}, u32[]{:S(2)}) %collective-permute-start.10) | collective-permute-done | bytes 131104 | tf_op jit(solution)/shard_map/ppermute | solution.py:290
  32.3 1.1 %shard_map.119 = (f32[256,128]{1,0:T(8,128)S(1)}, f32[512,256]{1,0:T(8,128)S(1)}, f32[512,256]{1,0:T(8,128)S(1)}, f32[32,512]{1,0:T(8,128)S(1)}, bf16[512,256]{1,0:T(8,128)(2,1)S(1)}) custom-call(s32[1]{0:T(128)} %bitcast.rep_at.here, bf16[1024,512]{1,0:T(8,128)(2,1)S(1)} %get-tuple-element.37.high, bf16[1024,512]{1,0:T(8,128)(2,1)S(1)} %get-tuple-element.38.low, ...), custom_call_target="tpu_custom_call" | custom-call | flops 134217728 | bytes 4194304 | tf_op jit(solution)/shard_map/pallas_call | solution.py:373
  33.5 1.2 %collective-permute-start.12 = (f32[256,128]{1,0:T(8,128)S(1)}, f32[256,128]{1,0:T(8,128)S(1)}, u32[]{:S(2)}, u32[]{:S(2)}) collective-permute-start(f32[256,128]{1,0:T(8,128)S(1)} %get-tuple-element.48), channel_id=1, source_target_pairs={{0,8},{1,5},{2,10},{3,7},{4,12},{5,1},{6,14},{7,3},{8,0},{9,13},{1... | collective-permute-start | bytes 393224 | tf_op jit(solution)/shard_map/ppermute | solution.py:290
  34.7 0.6 shard_map.121
  35.2 1.0 %collective-permute-start.11 = (f32[256,128]{1,0:T(8,128)S(1)}, f32[256,128]{1,0:T(8,128)S(1)}, u32[]{:S(2)}, u32[]{:S(2)}) collective-permute-start(f32[256,128]{1,0:T(8,128)S(1)} %get-tuple-element.45), channel_id=1, source_target_pairs={{0,8},{1,5},{2,10},{3,7},{4,12},{5,1},{6,14},{7,3},{8,0},{9,13},{1... | collective-permute-start | bytes 393224 | tf_op jit(solution)/shard_map/ppermute | solution.py:290
  36.2 2.3 %collective-permute-done.12.refs_1_ = f32[256,128]{1,0:T(8,128)S(1)} collective-permute-done((f32[256,128]{1,0:T(8,128)S(1)}, f32[256,128]{1,0:T(8,128)S(1)}, u32[]{:S(2)}, u32[]{:S(2)}) %collective-permute-start.12) | collective-permute-done | bytes 131104 | tf_op jit(solution)/shard_map/ppermute | solution.py:290
  38.5 1.7 %collective-permute-start.14 = (f32[128,128]{1,0:T(8,128)S(1)}, f32[128,128]{1,0:T(8,128)S(1)}, u32[]{:S(2)}, u32[]{:S(2)}) collective-permute-start(f32[128,128]{1,0:T(8,128)S(1)} %get-tuple-element.51), channel_id=1, source_target_pairs={{0,4},{1,9},{2,6},{3,11},{4,0},{5,13},{6,2},{7,15},{8,12},{9,1},{1... | collective-permute-start | bytes 196616 | tf_op jit(solution)/shard_map/ppermute | solution.py:290
  40.2 0.4 collective-permute-start.13
  40.7 2.2 %collective-permute-done.14.refs_1_ = f32[128,128]{1,0:T(8,128)S(1)} collective-permute-done((f32[128,128]{1,0:T(8,128)S(1)}, f32[128,128]{1,0:T(8,128)S(1)}, u32[]{:S(2)}, u32[]{:S(2)}) %collective-permute-start.14) | collective-permute-done | bytes 65568 | tf_op jit(solution)/shard_map/ppermute | solution.py:290
  42.9 2.3 %collective-permute-start.15 = (f32[128,128]{1,0:T(8,128)S(1)}, f32[128,128]{1,0:T(8,128)S(1)}, u32[]{:S(2)}, u32[]{:S(2)}) collective-permute-start(f32[128,128]{1,0:T(8,128)S(1)} %shard_map.125), channel_id=1, source_target_pairs={{0,16},{1,17},{2,18},{3,19},{4,20},{5,21},{6,22},{7,23},{8,24},{9,... | collective-permute-start | bytes 196616 | tf_op jit(solution)/shard_map/ppermute | solution.py:290
  45.2 0.2 shard_map.128.refs_0_
  45.4 0.7 %collective-permute-start.19 = (f32[72,128]{1,0:T(8,128)S(1)}, f32[72,128]{1,0:T(8,128)S(1)}, u32[]{:S(2)}, u32[]{:S(2)}) collective-permute-start(f32[72,128]{1,0:T(8,128)S(1)} %shard_map.128.refs_0_), channel_id=1, source_target_pairs={{0,16},{1,17},{2,18},{3,19},{4,20},{5,21},{6,22},{7,23},{8,24},{9,... | collective-permute-start | bytes 110600 | tf_op jit(solution)/shard_map/ppermute | solution.py:290
  46.2 4.2 %collective-permute-done.19.refs_1_ = f32[72,128]{1,0:T(8,128)S(1)} collective-permute-done((f32[72,128]{1,0:T(8,128)S(1)}, f32[72,128]{1,0:T(8,128)S(1)}, u32[]{:S(2)}, u32[]{:S(2)}) %collective-permute-start.19) | collective-permute-done | bytes 36896 | tf_op jit(solution)/shard_map/ppermute | solution.py:290
  50.4 1.5 %collective-permute-start.20 = (f32[72,128]{1,0:T(8,128)S(1)}, f32[72,128]{1,0:T(8,128)S(1)}, u32[]{:S(2)}, u32[]{:S(2)}) collective-permute-start(f32[72,128]{1,0:T(8,128)S(1)} %shard_map.129.refs_0_), channel_id=1, source_target_pairs={{0,4},{1,9},{2,6},{3,11},{4,0},{5,13},{6,2},{7,15},{8,12},{9,1},{1... | collective-permute-start | bytes 110600 | tf_op jit(solution)/shard_map/ppermute | solution.py:290
  51.9 1.6 %collective-permute-start.17 = (f32[128,128]{1,0:T(8,128)S(1)}, f32[128,128]{1,0:T(8,128)S(1)}, u32[]{:S(2)}, u32[]{:S(2)}) collective-permute-start(f32[128,128]{1,0:T(8,128)S(1)} %shard_map.126.refs_0_), channel_id=1, source_target_pairs={{0,2},{1,3},{2,0},{3,1},{4,6},{5,7},{6,4},{7,5},{8,10},{9,11},{10,... | collective-permute-start | bytes 196616 | tf_op jit(solution)/shard_map/ppermute | solution.py:290
  53.5 0.8 %collective-permute-done.20.refs_1_ = f32[72,128]{1,0:T(8,128)S(1)} collective-permute-done((f32[72,128]{1,0:T(8,128)S(1)}, f32[72,128]{1,0:T(8,128)S(1)}, u32[]{:S(2)}, u32[]{:S(2)}) %collective-permute-start.20) | collective-permute-done | bytes 36896 | tf_op jit(solution)/shard_map/ppermute | solution.py:290
  54.3 2.2 %collective-permute-start.21 = (f32[72,128]{1,0:T(8,128)S(1)}, f32[72,128]{1,0:T(8,128)S(1)}, u32[]{:S(2)}, u32[]{:S(2)}) collective-permute-start(f32[72,128]{1,0:T(8,128)S(1)} %shard_map.130.refs_0_), channel_id=1, source_target_pairs={{0,8},{1,5},{2,10},{3,7},{4,12},{5,1},{6,14},{7,3},{8,0},{9,13},{1... | collective-permute-start | bytes 110600 | tf_op jit(solution)/shard_map/ppermute | solution.py:290
  56.5 1.9 %collective-permute-done.21.refs_1_ = f32[72,128]{1,0:T(8,128)S(1)} collective-permute-done((f32[72,128]{1,0:T(8,128)S(1)}, f32[72,128]{1,0:T(8,128)S(1)}, u32[]{:S(2)}, u32[]{:S(2)}) %collective-permute-start.21) | collective-permute-done | bytes 36896 | tf_op jit(solution)/shard_map/ppermute | solution.py:290
  58.4 1.5 %collective-permute-start.23 = (f32[72,128]{1,0:T(8,128)S(1)}, f32[72,128]{1,0:T(8,128)S(1)}, u32[]{:S(2)}, u32[]{:S(2)}) collective-permute-start(f32[72,128]{1,0:T(8,128)S(1)} %shard_map.131.refs_0_), channel_id=1, source_target_pairs={{0,2},{1,3},{2,0},{3,1},{4,6},{5,7},{6,4},{7,5},{8,10},{9,11},{10,... | collective-permute-start | bytes 110600 | tf_op jit(solution)/shard_map/ppermute | solution.py:290
  60.0 0.5 collective-permute-start.18
  60.5 0.0 collective-permute-start.22
  60.5 1.9 %collective-permute-done.23.refs_2_ = f32[72,128]{1,0:T(8,128)S(1)} collective-permute-done((f32[72,128]{1,0:T(8,128)S(1)}, f32[72,128]{1,0:T(8,128)S(1)}, u32[]{:S(2)}, u32[]{:S(2)}) %collective-permute-start.23) | collective-permute-done | bytes 36896 | tf_op jit(solution)/shard_map/ppermute | solution.py:290
  62.4 0.8 %shard_map.120 = f32[512,256]{1,0:T(8,128)} custom-call(f32[512,256]{1,0:T(8,128)S(1)} %get-tuple-element.42.refs_0_), custom_call_target="tpu_custom_call" | custom-call | bytes 1048576 | tf_op jit(solution)/shard_map/pallas_call | solution.py:294
  63.2 0.4 collective-permute-done.24.refs_3_
  63.6 0.7 %shard_map.132 = (f32[128,256]{1,0:T(8,128)}, f32[1,256]{1,0:T(1,128)}) custom-call(s32[1]{0:T(128)} %bitcast.rep_at.here, f32[72,128]{1,0:T(8,128)S(1)} %shard_map.131.refs_0_, f32[72,128]{1,0:T(8,128)S(1)} %collective-permute-done.22.refs_1_, f32[72,128]{1,0:T(8,128)S(1)} %collective-permute-done.23.refs_2_, f32[72,128]{1,0:T(8,128)S(1)} %collective-permute-done.24.refs_3_), custom_call_target="tpu_custom_call" | custom-call | bytes 262144 | tf_op jit(solution)/shard_map/pallas_call | solution.py:443
  64.3 0.7 %shard_map.127 = f32[512,128]{1,0:T(8,128)} custom-call(s32[1]{0:T(128)} %bitcast.rep_at.here, f32[128,128]{1,0:T(8,128)S(1)} %shard_map.126.refs_0_, f32[128,128]{1,0:T(8,128)S(1)} %collective-permute-done.16.refs_1_, f32[128,128]{1,0:T(8,128)S(1)} %collective-permute-done.17.refs_2_, f32[128,128]{1,0:T(8,128)S(1)} %collective-permute-done.18.refs_3_), custom_call_target="tpu_custom_call" | custom-call | bytes 524288 | tf_op jit(solution)/shard_map/pallas_call | solution.py:435
  (30 shorter events, 0.2 us)
Async XLA Ops:
  0.6 20.1 %copy-start.2 = (f32[256]{0:T(256)S(1)}, f32[256]{0:T(256)}, u32[]{:S(2)}) copy-start(f32[256]{0:T(256)} %param.10) | copy-start | bytes 3076
  0.6 20.1 %copy-start = (f32[512,256]{1,0:T(8,128)S(1)}, f32[512,256]{1,0:T(8,128)}, u32[]{:S(2)}) copy-start(f32[512,256]{1,0:T(8,128)} %cotangent.1) | copy-start | bytes 1572868
  0.7 20.1 %copy-start.1 = (f32[128,256]{1,0:T(8,128)S(1)}, f32[128,256]{1,0:T(8,128)}, u32[]{:S(2)}) copy-start(f32[128,256]{1,0:T(8,128)} %weight.1) | copy-start | bytes 393220
  3.4 15.9 %collective-permute-start = (f32[520,128]{1,0:T(8,128)S(1)}, f32[520,128]{1,0:T(8,128)S(1)}, u32[]{:S(2)}, u32[]{:S(2)}) collective-permute-start(f32[520,128]{1,0:T(8,128)S(1)} %get-tuple-element.31), channel_id=1, source_target_pairs={{0,1},{1,0},{2,3},{3,2},{4,5},{5,4},{6,7},{7,6},{8,9},{9,8},{10,11... | collective-permute-start | bytes 798728 | tf_op jit(solution)/shard_map/ppermute | solution.py:290
  4.0 16.8 %collective-permute-start.1 = (f32[520,128]{1,0:T(8,128)S(1)}, f32[520,128]{1,0:T(8,128)S(1)}, u32[]{:S(2)}, u32[]{:S(2)}) collective-permute-start(f32[520,128]{1,0:T(8,128)S(1)} %get-tuple-element.35), channel_id=1, source_target_pairs={{0,2},{1,3},{2,0},{3,1},{4,6},{5,7},{6,4},{7,5},{8,10},{9,11},{10,... | collective-permute-start | bytes 798728 | tf_op jit(solution)/shard_map/ppermute | solution.py:290
  6.6 14.2 %collective-permute-start.2 = (f32[520,128]{1,0:T(8,128)S(1)}, f32[520,128]{1,0:T(8,128)S(1)}, u32[]{:S(2)}, u32[]{:S(2)}) collective-permute-start(f32[520,128]{1,0:T(8,128)S(1)} %get-tuple-element.36), channel_id=1, source_target_pairs={{0,3},{1,2},{2,1},{3,0},{4,7},{5,6},{6,5},{7,4},{8,11},{9,10},{10,... | collective-permute-start | bytes 798728 | tf_op jit(solution)/shard_map/ppermute | solution.py:290
  6.6 6.5 %collective-permute-start.3 = (f32[128,128]{1,0:T(8,128)S(1)}, f32[128,128]{1,0:T(8,128)S(1)}, u32[]{:S(2)}, u32[]{:S(2)}) collective-permute-start(f32[128,128]{1,0:T(8,128)S(1)} %get-tuple-element.39.refs_0_), channel_id=1, source_target_pairs={{0,16},{1,17},{2,18},{3,19},{4,20},{5,21},{6,22},{7,23},{8,24},{9,... | collective-permute-start | bytes 196616 | tf_op jit(solution)/shard_map/ppermute | solution.py:290
  9.4 5.4 %collective-permute-start.4 = (f32[128,128]{1,0:T(8,128)S(1)}, f32[128,128]{1,0:T(8,128)S(1)}, u32[]{:S(2)}, u32[]{:S(2)}) collective-permute-start(f32[128,128]{1,0:T(8,128)S(1)} %get-tuple-element.39.refs_0_), channel_id=1, source_target_pairs={{0,4},{1,9},{2,6},{3,11},{4,0},{5,13},{6,2},{7,15},{8,12},{9,1},{1... | collective-permute-start | bytes 196616 | tf_op jit(solution)/shard_map/ppermute | solution.py:290
  13.1 5.0 %collective-permute-start.5 = (f32[128,128]{1,0:T(8,128)S(1)}, f32[128,128]{1,0:T(8,128)S(1)}, u32[]{:S(2)}, u32[]{:S(2)}) collective-permute-start(f32[128,128]{1,0:T(8,128)S(1)} %collective-permute-done.3.refs_1_), channel_id=1, source_target_pairs={{0,4},{1,9},{2,6},{3,11},{4,0},{5,13},{6,2},{7,15},{8,12},{9,1},{1... | collective-permute-start | bytes 196616 | tf_op jit(solution)/shard_map/ppermute | solution.py:290
  14.8 7.0 %collective-permute-start.6 = (f32[256,128]{1,0:T(8,128)S(1)}, f32[256,128]{1,0:T(8,128)S(1)}, u32[]{:S(2)}, u32[]{:S(2)}) collective-permute-start(f32[256,128]{1,0:T(8,128)S(1)} %shard_map.114.refs_0_), channel_id=1, source_target_pairs={{0,8},{1,5},{2,10},{3,7},{4,12},{5,1},{6,14},{7,3},{8,0},{9,13},{1... | collective-permute-start | bytes 393224 | tf_op jit(solution)/shard_map/ppermute | solution.py:290
  18.1 5.0 %collective-permute-start.7 = (f32[256,128]{1,0:T(8,128)S(1)}, f32[256,128]{1,0:T(8,128)S(1)}, u32[]{:S(2)}, u32[]{:S(2)}) collective-permute-start(f32[256,128]{1,0:T(8,128)S(1)} %shard_map.115.refs_1_), channel_id=1, source_target_pairs={{0,8},{1,5},{2,10},{3,7},{4,12},{5,1},{6,14},{7,3},{8,0},{9,13},{1... | collective-permute-start | bytes 393224 | tf_op jit(solution)/shard_map/ppermute | solution.py:290
  23.9 1.4 %collective-permute-start.8 = (f32[64,512]{1,0:T(8,128)S(1)}, f32[64,512]{1,0:T(8,128)S(1)}, u32[]{:S(2)}, u32[]{:S(2)}) collective-permute-start(f32[64,512]{1,0:T(8,128)S(1)} %get-tuple-element.41), channel_id=1, source_target_pairs={{0,1},{1,0},{2,3},{3,2},{4,5},{5,4},{6,7},{7,6},{8,9},{9,8},{10,11... | collective-permute-start | bytes 393224 | tf_op jit(solution)/shard_map/ppermute | solution.py:290
  25.3 5.6 %collective-permute-start.9 = (f32[64,512]{1,0:T(8,128)S(1)}, f32[64,512]{1,0:T(8,128)S(1)}, u32[]{:S(2)}, u32[]{:S(2)}) collective-permute-start(f32[64,512]{1,0:T(8,128)S(1)} %shard_map.117.refs_0_), channel_id=1, source_target_pairs={{0,2},{1,3},{2,0},{3,1},{4,6},{5,7},{6,4},{7,5},{8,10},{9,11},{10,... | collective-permute-start | bytes 393224 | tf_op jit(solution)/shard_map/ppermute | solution.py:290
  30.9 1.4 %collective-permute-start.10 = (f32[64,512]{1,0:T(8,128)S(1)}, f32[64,512]{1,0:T(8,128)S(1)}, u32[]{:S(2)}, u32[]{:S(2)}) collective-permute-start(f32[64,512]{1,0:T(8,128)S(1)} %shard_map.118.mine), channel_id=1, source_target_pairs={{0,1},{1,0},{2,3},{3,2},{4,5},{5,4},{6,7},{7,6},{8,9},{9,8},{10,11... | collective-permute-start | bytes 393224 | tf_op jit(solution)/shard_map/ppermute | solution.py:290
  33.5 5.0 %collective-permute-start.12 = (f32[256,128]{1,0:T(8,128)S(1)}, f32[256,128]{1,0:T(8,128)S(1)}, u32[]{:S(2)}, u32[]{:S(2)}) collective-permute-start(f32[256,128]{1,0:T(8,128)S(1)} %get-tuple-element.48), channel_id=1, source_target_pairs={{0,8},{1,5},{2,10},{3,7},{4,12},{5,1},{6,14},{7,3},{8,0},{9,13},{1... | collective-permute-start | bytes 393224 | tf_op jit(solution)/shard_map/ppermute | solution.py:290
  35.2 5.4 %collective-permute-start.11 = (f32[256,128]{1,0:T(8,128)S(1)}, f32[256,128]{1,0:T(8,128)S(1)}, u32[]{:S(2)}, u32[]{:S(2)}) collective-permute-start(f32[256,128]{1,0:T(8,128)S(1)} %get-tuple-element.45), channel_id=1, source_target_pairs={{0,8},{1,5},{2,10},{3,7},{4,12},{5,1},{6,14},{7,3},{8,0},{9,13},{1... | collective-permute-start | bytes 393224 | tf_op jit(solution)/shard_map/ppermute | solution.py:290
  38.5 4.3 %collective-permute-start.14 = (f32[128,128]{1,0:T(8,128)S(1)}, f32[128,128]{1,0:T(8,128)S(1)}, u32[]{:S(2)}, u32[]{:S(2)}) collective-permute-start(f32[128,128]{1,0:T(8,128)S(1)} %get-tuple-element.51), channel_id=1, source_target_pairs={{0,4},{1,9},{2,6},{3,11},{4,0},{5,13},{6,2},{7,15},{8,12},{9,1},{1... | collective-permute-start | bytes 196616 | tf_op jit(solution)/shard_map/ppermute | solution.py:290
  40.2 11.7 %collective-permute-start.13 = (f32[128,128]{1,0:T(8,128)S(1)}, f32[128,128]{1,0:T(8,128)S(1)}, u32[]{:S(2)}, u32[]{:S(2)}) collective-permute-start(f32[128,128]{1,0:T(8,128)S(1)} %get-tuple-element.49), channel_id=1, source_target_pairs={{0,4},{1,9},{2,6},{3,11},{4,0},{5,13},{6,2},{7,15},{8,12},{9,1},{1... | collective-permute-start | bytes 196616 | tf_op jit(solution)/shard_map/ppermute | solution.py:290
  42.9 9.0 %collective-permute-start.15 = (f32[128,128]{1,0:T(8,128)S(1)}, f32[128,128]{1,0:T(8,128)S(1)}, u32[]{:S(2)}, u32[]{:S(2)}) collective-permute-start(f32[128,128]{1,0:T(8,128)S(1)} %shard_map.125), channel_id=1, source_target_pairs={{0,16},{1,17},{2,18},{3,19},{4,20},{5,21},{6,22},{7,23},{8,24},{9,... | collective-permute-start | bytes 196616 | tf_op jit(solution)/shard_map/ppermute | solution.py:290
  45.4 4.9 %collective-permute-start.19 = (f32[72,128]{1,0:T(8,128)S(1)}, f32[72,128]{1,0:T(8,128)S(1)}, u32[]{:S(2)}, u32[]{:S(2)}) collective-permute-start(f32[72,128]{1,0:T(8,128)S(1)} %shard_map.128.refs_0_), channel_id=1, source_target_pairs={{0,16},{1,17},{2,18},{3,19},{4,20},{5,21},{6,22},{7,23},{8,24},{9,... | collective-permute-start | bytes 110600 | tf_op jit(solution)/shard_map/ppermute | solution.py:290
  50.4 4.0 %collective-permute-start.20 = (f32[72,128]{1,0:T(8,128)S(1)}, f32[72,128]{1,0:T(8,128)S(1)}, u32[]{:S(2)}, u32[]{:S(2)}) collective-permute-start(f32[72,128]{1,0:T(8,128)S(1)} %shard_map.129.refs_0_), channel_id=1, source_target_pairs={{0,4},{1,9},{2,6},{3,11},{4,0},{5,13},{6,2},{7,15},{8,12},{9,1},{1... | collective-permute-start | bytes 110600 | tf_op jit(solution)/shard_map/ppermute | solution.py:290
  51.9 8.1 %collective-permute-start.17 = (f32[128,128]{1,0:T(8,128)S(1)}, f32[128,128]{1,0:T(8,128)S(1)}, u32[]{:S(2)}, u32[]{:S(2)}) collective-permute-start(f32[128,128]{1,0:T(8,128)S(1)} %shard_map.126.refs_0_), channel_id=1, source_target_pairs={{0,2},{1,3},{2,0},{3,1},{4,6},{5,7},{6,4},{7,5},{8,10},{9,11},{10,... | collective-permute-start | bytes 196616 | tf_op jit(solution)/shard_map/ppermute | solution.py:290
  54.3 4.1 %collective-permute-start.21 = (f32[72,128]{1,0:T(8,128)S(1)}, f32[72,128]{1,0:T(8,128)S(1)}, u32[]{:S(2)}, u32[]{:S(2)}) collective-permute-start(f32[72,128]{1,0:T(8,128)S(1)} %shard_map.130.refs_0_), channel_id=1, source_target_pairs={{0,8},{1,5},{2,10},{3,7},{4,12},{5,1},{6,14},{7,3},{8,0},{9,13},{1... | collective-permute-start | bytes 110600 | tf_op jit(solution)/shard_map/ppermute | solution.py:290
  58.4 4.0 %collective-permute-start.23 = (f32[72,128]{1,0:T(8,128)S(1)}, f32[72,128]{1,0:T(8,128)S(1)}, u32[]{:S(2)}, u32[]{:S(2)}) collective-permute-start(f32[72,128]{1,0:T(8,128)S(1)} %shard_map.131.refs_0_), channel_id=1, source_target_pairs={{0,2},{1,3},{2,0},{3,1},{4,6},{5,7},{6,4},{7,5},{8,10},{9,11},{10,... | collective-permute-start | bytes 110600 | tf_op jit(solution)/shard_map/ppermute | solution.py:290
  60.0 4.3 %collective-permute-start.16 = (f32[128,128]{1,0:T(8,128)S(1)}, f32[128,128]{1,0:T(8,128)S(1)}, u32[]{:S(2)}, u32[]{:S(2)}) collective-permute-start(f32[128,128]{1,0:T(8,128)S(1)} %shard_map.126.refs_0_), channel_id=1, source_target_pairs={{0,1},{1,0},{2,3},{3,2},{4,5},{5,4},{6,7},{7,6},{8,9},{9,8},{10,11... | collective-permute-start | bytes 196616 | tf_op jit(solution)/shard_map/ppermute | solution.py:290
  60.0 4.3 %collective-permute-start.18 = (f32[128,128]{1,0:T(8,128)S(1)}, f32[128,128]{1,0:T(8,128)S(1)}, u32[]{:S(2)}, u32[]{:S(2)}) collective-permute-start(f32[128,128]{1,0:T(8,128)S(1)} %collective-permute-done.17.refs_2_), channel_id=1, source_target_pairs={{0,1},{1,0},{2,3},{3,2},{4,5},{5,4},{6,7},{7,6},{8,9},{9,8},{10,11... | collective-permute-start | bytes 196616 | tf_op jit(solution)/shard_map/ppermute | solution.py:290
  60.5 2.7 %collective-permute-start.22 = (f32[72,128]{1,0:T(8,128)S(1)}, f32[72,128]{1,0:T(8,128)S(1)}, u32[]{:S(2)}, u32[]{:S(2)}) collective-permute-start(f32[72,128]{1,0:T(8,128)S(1)} %shard_map.131.refs_0_), channel_id=1, source_target_pairs={{0,1},{1,0},{2,3},{3,2},{4,5},{5,4},{6,7},{7,6},{8,9},{9,8},{10,11... | collective-permute-start | bytes 110600 | tf_op jit(solution)/shard_map/ppermute | solution.py:290
  62.4 1.2 %collective-permute-start.24 = (f32[72,128]{1,0:T(8,128)S(1)}, f32[72,128]{1,0:T(8,128)S(1)}, u32[]{:S(2)}, u32[]{:S(2)}) collective-permute-start(f32[72,128]{1,0:T(8,128)S(1)} %collective-permute-done.23.refs_2_), channel_id=1, source_target_pairs={{0,1},{1,0},{2,3},{3,2},{4,5},{5,4},{6,7},{7,6},{8,9},{9,8},{10,11... | collective-permute-start | bytes 110600 | tf_op jit(solution)/shard_map/ppermute | solution.py:290
